TPU v7x, 512 devices: a whole 4x4x16 slice. The times are simulated.
512 devices in a mesh: sec: 16 (over y, x_hi, core), op: 32 (over z, x_lo).
Axes of the slice: x: 4 (x_hi: 2, x_lo: 2; x = x_hi * 2 + x_lo), y: 4, z: 16, core: 2. Of those that a mesh axis runs over, the one named last changes fastest.
Arguments:
- wavefunction: bfloat16 [32, 256, 256], P('sec'), may hold values from -6 to 6
- diagonal: bfloat16 [32, 256, 256], P('sec'), may hold values from 1 to 4
- preconditioner: bfloat16 [32, 256, 256], P('sec'), may hold values from 0.25 to 1
- left_operator_blocks: bfloat16 [8192, 256, 256], P(('sec', 'op')), may hold values from -0.1875 to 0.1875
- right_operator_blocks: bfloat16 [8192, 256, 256], P(('sec', 'op')), may hold values from -0.375 to 0.375
- slot_source_sector: int32 [8192], P(('sec', 'op')), may hold values from 0 to 31
- slot_target_sector: int32 [8192], P(('sec', 'op')), may hold values from 0 to 1
- pair_count: int32 [512], P(('sec', 'op')), may hold values from 1 to 16, as said below
- left_dims: int32 [32], replicated, may hold values from 128 to 256, as said below
- right_dims: int32 [32], replicated, may hold values from 128 to 256, as said below
Outputs:
- correction: bfloat16 [32, 256, 256], P('sec')
- product_rows: float32 [32, 256, 256], P('sec', 'op')
- projected: float32 [3], replicated
Inputs may be any that keep to these rules, and one draw needn't show every extreme that they name: `pair_count`: slots below a device's count hold pairs, the rest are ignored; some device has all 16 slots live. `left_dims`: some sector uses all 256 rows. `right_dims`: some sector uses all 256 columns.
All inputs are finite; a program needn't handle non-finite values.
Results may differ from a plain program's by a relative error of at most 0.003.
Values may be sent and summed in bfloat16 or wider, within the bound.
No kernel may reach another device: no remote copies, remote signals or barrier semaphores. Data moves between devices by JAX's collectives and lax.ppermute only.
A program may use at most 64 MiB of HBM per device.

v0:
```python
import jax
import jax.numpy as jnp
from jax import lax
from jax.sharding import PartitionSpec as P


def block_mask(left_dims, right_dims, block_size):
    positions = jnp.arange(block_size, dtype=jnp.int32)
    return (positions[None, :, None] < left_dims[:, None, None]) & (
        positions[None, None, :] < right_dims[:, None, None]
    )


def gather_sources(own_vector):
    return lax.all_gather(own_vector, "sec", axis=0, tiled=True)


def reduce_dots(values):
    return lax.psum(values, "sec")


def pair_partial(
    sources,
    left_operator_blocks,
    right_operator_blocks,
    slot_source_sector,
    slot_target_sector,
    live_count,
    sector_count,
):
    block_size = sources.shape[1]
    zero_sum = jnp.zeros((sector_count, block_size, block_size), jnp.float32)

    def add_pair(slot_index, partial_value):
        source_block = lax.dynamic_index_in_dim(
            sources, slot_source_sector[slot_index], 0, keepdims=False
        )
        middle = jnp.dot(
            left_operator_blocks[slot_index], source_block, preferred_element_type=jnp.float32
        )
        contribution = jnp.dot(
            middle,
            right_operator_blocks[slot_index].astype(jnp.float32),
            precision=lax.Precision.HIGHEST,
            preferred_element_type=jnp.float32,
        )
        contribution = jnp.where(slot_index < live_count, contribution, 0.0)
        return partial_value.at[slot_target_sector[slot_index]].add(contribution)

    return lax.fori_loop(0, left_operator_blocks.shape[0], add_pair, zero_sum)


def sum_pairs(partial_value):
    return lax.psum(partial_value, "op")


def on_device(
    wavefunction,
    diagonal,
    preconditioner,
    left_operator_blocks,
    right_operator_blocks,
    slot_source_sector,
    slot_target_sector,
    pair_count,
    left_dims,
    right_dims,
):
    sector_count = wavefunction.shape[0]
    block_size = wavefunction.shape[1]
    op_devices = lax.axis_size("op")
    share_rows = block_size // op_devices
    first_sector = lax.axis_index("sec") * sector_count
    row_start = lax.axis_index("op") * share_rows
    entries = float(left_dims.shape[0] * block_size * block_size)
    own_mask = block_mask(
        lax.dynamic_slice_in_dim(left_dims, first_sector, sector_count),
        lax.dynamic_slice_in_dim(right_dims, first_sector, sector_count),
        block_size,
    )
    live_count = pair_count[0]
    own_vector = jnp.where(own_mask, wavefunction, jnp.zeros_like(wavefunction))
    diag_view = diagonal.astype(jnp.float32)
    scale_view = preconditioner.astype(jnp.float32)
    vector_view = own_vector.astype(jnp.float32)

    def apply_operator(sources, field_view):
        partial_value = pair_partial(
            sources,
            left_operator_blocks,
            right_operator_blocks,
            slot_source_sector,
            slot_target_sector,
            live_count,
            sector_count,
        )
        return jnp.where(own_mask, diag_view * field_view + sum_pairs(partial_value), 0.0)

    sigma_first = apply_operator(gather_sources(own_vector), vector_view)
    norm_vector, correlation = reduce_dots(
        (jnp.sum(vector_view * vector_view), jnp.sum(vector_view * sigma_first))
    )
    rayleigh = correlation / norm_vector
    residual = sigma_first - rayleigh * vector_view
    scaled = scale_view * residual
    along_vector = reduce_dots((jnp.sum(vector_view * scaled),))[0]
    orthogonal = scaled - along_vector / norm_vector * vector_view
    square_norm = reduce_dots((jnp.sum(orthogonal * orthogonal),))[0]
    corr_view = (orthogonal * lax.rsqrt(square_norm / entries + 1e-06)).astype(jnp.bfloat16)
    next_sources = gather_sources(corr_view)
    corr_float = corr_view.astype(jnp.float32)
    sigma_second = apply_operator(next_sources, corr_float)
    cross_term, self_term = reduce_dots(
        (jnp.sum(vector_view * sigma_second), jnp.sum(corr_float * sigma_second))
    )
    projected = jnp.stack(
        [rayleigh, cross_term * lax.rsqrt(norm_vector * entries), self_term / entries]
    )
    product_rows = lax.dynamic_slice_in_dim(sigma_second, row_start, share_rows, 1)
    return (corr_view, product_rows, projected)


def solution(mesh):
    in_specs = (
        P("sec", None, None),
        P("sec", None, None),
        P("sec", None, None),
        P(("sec", "op"), None, None),
        P(("sec", "op"), None, None),
        P(("sec", "op")),
        P(("sec", "op")),
        P(("sec", "op")),
        P(),
        P(),
    )
    out_specs = (P("sec", None, None), P("sec", "op", None), P())
    return jax.shard_map(
        on_device, mesh=mesh, in_specs=in_specs, out_specs=out_specs, check_vma=False
    )
```

profile of v0, /device:TPU:1, one launch (start us, length us, event | category | flops | bytes accessed | tf_op | source)
XLA Modules:
  0.0 1174.2 jit_solution(14956797437552450582)
XLA Ops:
  8.8 1.8 and_select_fusion.2
  10.6 77.2 %all-gather.3.cloned.1.call-done = bf16[32,256,256]{2,1,0:T(8,128)(2,1)} async-done(((bf16[2,256,256]{2,1,0:T(8,128)(2,1)}), bf16[32,256,256]{2,1,0:T(8,128)(2,1)}) %all-gather.3.cloned.1.call-update) | async-done | bytes 4194320 | tf_op jit(solution)/shard_map/all_gather | solution.py:15
  87.9 182.8 %while.28 = (s32[]{:T(128)}, f32[2,256,256]{2,1,0:T(8,128)S(1)}, s32[16]{0:T(128)}, s32[]{:T(128)}, bf16[16,256,256]{2,1,0:T(8,128)(2,1)}, /*index=5*/s32[16]{0:...) while((s32[]{:T(128)}, f32[2,256,256]{2,1,0:T(8,128)S(1)}, ...), condition=%wide.region_2.3_spmd, body=%wide.region_0.2_spmd.sunk | while | flops 235077664 | bytes 1444100 | solution.py:50
  87.9 1.3 dynamic_slice.122
  92.3 1.2 dynamic_slice.121
  95.5 1.4 and_reduce_fusion.4
  97.5 1.8 fusion.55
  106.9 1.4 and_reduce_fusion.4
  108.9 1.8 fusion.55
  118.3 1.4 and_reduce_fusion.4
  120.3 1.8 fusion.55
  129.7 1.4 and_reduce_fusion.4
  131.8 1.8 fusion.55
  141.2 1.4 and_reduce_fusion.4
  143.2 1.8 fusion.55
  152.6 1.4 and_reduce_fusion.4
  154.6 1.8 fusion.55
  164.0 1.4 and_reduce_fusion.4
  166.0 1.8 fusion.55
  175.4 1.4 and_reduce_fusion.4
  177.4 1.8 fusion.55
  186.8 1.4 and_reduce_fusion.4
  188.9 1.8 fusion.55
  198.3 1.4 and_reduce_fusion.4
  200.3 1.8 fusion.55
  209.7 1.4 and_reduce_fusion.4
  211.7 1.8 fusion.55
  221.1 1.4 and_reduce_fusion.4
  223.1 1.8 fusion.55
  232.5 1.4 and_reduce_fusion.4
  234.5 1.8 fusion.55
  243.9 1.4 and_reduce_fusion.4
  246.0 1.8 fusion.55
  255.3 1.4 and_reduce_fusion.4
  257.4 1.8 fusion.55
  266.8 1.4 and_reduce_fusion.4
  268.8 1.8 fusion.55
  271.5 241.5 %all-reduce.5.cloned.1.call-done = f32[2,256,256]{2,1,0:T(8,128)} async-done(((f32[2,256,256]{2,1,0:T(8,128)}), f32[2,256,256]{2,1,0:T(8,128)}) %all-reduce.5.cloned.1.call-update) | async-done | bytes 524304 | tf_op jit(solution)/shard_map/psum | solution.py:54
  513.0 2.0 fusion.30
  515.1 55.5 %all-reduce.1 = (f32[]{:T(128)}, f32[]{:T(128)}) all-reduce(f32[]{:T(128)} %get-tuple-element.330, f32[]{:T(128)} %get-tuple-element.329), channel_id=1, replica_groups=mesh['sec'=16,'op'=32] {'sec'}, use_global_device_ids=true, to_apply=%region_5.6 | all-reduce | flops 2 | bytes 16 | tf_op jit(solution)/shard_map/psum | solution.py:19
  571.9 2.0 fusion.33
  574.0 33.8 %psum.59 = f32[]{:T(128)} all-reduce(f32[]{:T(128)} %fusion.33), channel_id=1, replica_groups=mesh['sec'=16,'op'=32] {'sec'}, use_global_device_ids=true, to_apply=%region_9.10 | all-reduce | flops 1 | bytes 8 | tf_op jit(solution)/shard_map/psum | solution.py:19
  610.1 33.8 %psum.60 = f32[]{:T(128)} all-reduce(f32[]{:T(128)} %multiply_reduce_fusion), channel_id=1, replica_groups=mesh['sec'=16,'op'=32] {'sec'}, use_global_device_ids=true, to_apply=%region_11.12 | all-reduce | flops 1 | bytes 8 | tf_op jit(solution)/shard_map/psum | solution.py:19
  645.7 64.4 %all-gather.5.cloned.1.call-done = bf16[32,256,256]{2,1,0:T(8,128)(2,1)} async-done(((bf16[2,256,256]{2,1,0:T(8,128)(2,1)}), bf16[32,256,256]{2,1,0:T(8,128)(2,1)}) %all-gather.5.cloned.1.call-update) | async-done | bytes 4194320 | tf_op jit(solution)/shard_map/all_gather | solution.py:15
  710.2 155.1 %while.29 = (s32[]{:T(128)}, f32[2,256,256]{2,1,0:T(8,128)S(1)}, s32[16]{0:T(128)S(1)}, s32[]{:T(128)}, bf16[16,256,256]{2,1,0:T(8,128)(2,1)}, /*index=5*/s32[16...) while((s32[]{:T(128)}, f32[2,256,256]{2,1,0:T(8,128)S(1)}, ...), condition=%wide.region_14.15_spmd, body=%wide.region_12.14_spmd.sunk | while | flops 235077664 | bytes 1444100 | solution.py:50
  718.0 1.9 fusion.61
  727.7 1.9 fusion.61
  737.4 1.9 fusion.61
  747.1 1.9 fusion.61
  756.8 1.9 fusion.61
  766.5 1.9 fusion.61
  776.2 1.9 fusion.61
  785.9 1.9 fusion.61
  795.5 1.9 fusion.61
  805.2 1.9 fusion.61
  814.9 1.9 fusion.61
  824.6 1.9 fusion.61
  834.3 1.9 fusion.61
  844.0 1.9 fusion.61
  853.7 1.9 fusion.61
  863.4 1.9 fusion.61
  866.8 240.9 %all-reduce.7.cloned.1.call-done = f32[2,256,256]{2,1,0:T(8,128)} async-done(((f32[2,256,256]{2,1,0:T(8,128)}), f32[2,256,256]{2,1,0:T(8,128)}) %all-reduce.7.cloned.1.call-update) | async-done | bytes 524304 | tf_op jit(solution)/shard_map/psum | solution.py:54
  1107.7 2.0 fusion.35
  1109.7 55.5 %all-reduce = (f32[]{:T(128)}, f32[]{:T(128)}) all-reduce(f32[]{:T(128)} %get-tuple-element.328, f32[]{:T(128)} %get-tuple-element.327), channel_id=1, replica_groups=mesh['sec'=16,'op'=32] {'sec'}, use_global_device_ids=true, to_apply=%region_19.20 | all-reduce | flops 2 | bytes 16 | tf_op jit(solution)/shard_map/psum | solution.py:19
  (147 shorter events, 114.2 us)
Async XLA Ops:
  7.2 80.6 %all-gather.3.cloned.1.call-start = ((), (), s32[]{:S(2)}) async-start(), calls=%async_computation | async-start | bytes 4456448 | tf_op jit(solution)/shard_map/all_gather | solution.py:15
  10.6 502.5 %all-reduce.5.cloned.1.call-start = ((), (), s32[]{:S(2)}) async-start(), calls=%async_computation.1 | async-start | bytes 1048576 | tf_op jit(solution)/shard_map/psum | solution.py:54
  87.8 425.2 %copy-start.2 = (bf16[2,256,256]{2,1,0:T(8,128)(2,1)S(1)}, bf16[2,256,256]{2,1,0:T(8,128)(2,1)}, u32[]{:S(2)}) copy-start(bf16[2,256,256]{2,1,0:T(8,128)(2,1)} %param.18) | copy-start | bytes 786436
  87.8 425.2 %copy-start.4 = (bf16[2,256,256]{2,1,0:T(8,128)(2,1)S(1)}, bf16[2,256,256]{2,1,0:T(8,128)(2,1)}, u32[]{:S(2)}) copy-start(bf16[2,256,256]{2,1,0:T(8,128)(2,1)} %param.19) | copy-start | bytes 786436
  87.9 484.1 %copy-start.6 = (bf16[2,256,256]{2,1,0:T(8,128)(2,1)S(1)}, bf16[2,256,256]{2,1,0:T(8,128)(2,1)}, u32[]{:S(2)}) copy-start(bf16[2,256,256]{2,1,0:T(8,128)(2,1)} %param.20) | copy-start | bytes 786436
  270.6 0.8 copy-start.1
  271.5 438.6 %all-gather.5.cloned.1.call-start = ((), (), s32[]{:S(2)}) async-start(), calls=%async_computation.2 | async-start | bytes 4456448 | tf_op jit(solution)/shard_map/all_gather | solution.py:15
  513.0 96.0 %copy-start.3 = (f32[2,256,256]{2,1,0:T(8,128)S(1)}, f32[2,256,256]{2,1,0:T(8,128)}, u32[]{:S(2)}) copy-start(f32[2,256,256]{2,1,0:T(8,128)} %all-reduce.5.cloned.1.call-done) | copy-start | bytes 1572868
  574.0 136.2 %copy-start.7 = (s32[3]{0:T(128)S(1)}, s32[3]{0:T(128)}, u32[]{:S(2)}) copy-start(s32[3]{0:T(128)} %get-tuple-element.570) | copy-start | bytes 40
  574.0 136.2 %copy-start.8 = (s32[16]{0:T(128)S(1)}, s32[16]{0:T(128)}, u32[]{:S(2)}) copy-start(s32[16]{0:T(128)} %get-tuple-element.571) | copy-start | bytes 196
  574.0 136.2 %copy-start.9 = (s32[16]{0:T(128)S(1)}, s32[16]{0:T(128)}, u32[]{:S(2)}) copy-start(s32[16]{0:T(128)} %get-tuple-element.572) | copy-start | bytes 196
  645.6 462.1 %all-reduce.7.cloned.1.call-start = ((), (), s32[]{:S(2)}) async-start(), calls=%async_computation.3 | async-start | bytes 1048576 | tf_op jit(solution)/shard_map/psum | solution.py:54
  710.2 397.5 %copy-start.5 = (bf16[2,256,256]{2,1,0:T(8,128)(2,1)S(1)}, bf16[2,256,256]{2,1,0:T(8,128)(2,1)}, u32[]{:S(2)}) copy-start(bf16[2,256,256]{2,1,0:T(8,128)(2,1)} %multiply_convert_fusion) | copy-start | bytes 786436
  865.3 0.8 copy-start
Sparse Core Ops, SparseCore 0:
  11.9 75.8 all-gather.2
  271.6 241.3 all-reduce.4
  645.7 64.3 all-gather.4
  866.2 241.3 all-reduce.6
where the time goes:
time: 1180 us; the launch traced here: 1170 us
  waiting for transfers between devices  624 us (53%)
  blocking collectives  179 us (15%)
  loops' own time  147 us (12%)
  matrix products  96.2 us (8%)
  local copies, waits for them, and re-layouts  64.2 us (5%)
  other arithmetic  45.2 us (4%)
  between operations  19.2 us (2%)
    psum x2, waiting for transfers between devices, sum_pairs(): return lax.psum(partial_value, 'op')  482 us
    psum x4, blocking collectives, reduce_dots(): return lax.psum(values, 'sec')  179 us
    another operation x2, loops' own time, pair_partial(): return lax.fori_loop(0, left_operator_blocks.shape[0], add_pair, zero_sum)  147 us
    all_gather x2, waiting for transfers between devices, gather_sources(): return lax.all_gather(own_vector, 'sec', axis=0, tiled=True)  142 us
    dot_general x32, matrix products, add_pair(): jnp.dot(middle, right_operator_blocks[slot_index].astype(jnp.float32), pr...  59.3 us
    dot_general x32, matrix products, add_pair(): jnp.dot(left_operator_blocks[slot_index], source_block, preferred_element...  36.9 us
    another operation x32, other arithmetic  34.6 us
    dynamic_slice x32, local copies, waits for them, and re-layouts, add_pair(): return partial_value.at[slot_target_sector[slot_index]].add(contribution)  30.6 us
  transfers between devices with their start and end apart: 4, of which 4 were waited for; matrix products, arithmetic and copies ran while one was open for 0% of the time, Pallas kernels for 0%

commit v1 on v0

v1 whole, which is shorter than its diff:
```python
import functools

import jax
import jax.numpy as jnp
from jax import lax
from jax.experimental import pallas as pl
from jax.experimental.pallas import tpu as pltpu
from jax.sharding import PartitionSpec as P


def block_mask(left_dims, right_dims, block_size):
    positions = jnp.arange(block_size, dtype=jnp.int32)
    return (positions[None, :, None] < left_dims[:, None, None]) & (
        positions[None, None, :] < right_dims[:, None, None]
    )


def gather_blocks(value, axis_name, count):
    parts = [value]
    for shift in range(1, count):
        parts.append(
            lax.ppermute(value, axis_name, [(i, (i - shift) % count) for i in range(count)])
        )
    return jnp.stack(parts, 0)


def ordered_gather(value, axis_name, count):
    stacked = gather_blocks(value, axis_name, count)
    index = lax.axis_index(axis_name)
    return jnp.roll(stacked, index, axis=0)


def reduce_vector(values, axis_name, count):
    return jnp.sum(ordered_gather(values, axis_name, count), axis=0)


def reduce_scatter_rows(partial_value, axis_name, count):
    rows = partial_value.shape[1] // count
    index = lax.axis_index(axis_name)
    total = lax.dynamic_slice_in_dim(partial_value, index * rows, rows, 1)
    for shift in range(1, count):
        chunk = lax.dynamic_slice_in_dim(
            partial_value, ((index + shift) % count) * rows, rows, 1
        )
        total = total + lax.ppermute(
            chunk, axis_name, [(i, (i + shift) % count) for i in range(count)]
        )
    return total


def pair_kernel(src_ref, tgt_ref, cnt_ref, s_ref, l_ref, r_ref, o_ref):
    k = pl.program_id(0)

    @pl.when(k == 0)
    def _():
        o_ref[...] = jnp.zeros_like(o_ref)

    @pl.when(k < cnt_ref[0])
    def _():
        middle = jnp.dot(l_ref[0], s_ref[0], preferred_element_type=jnp.float32)
        high = middle.astype(jnp.bfloat16)
        low = (middle - high.astype(jnp.float32)).astype(jnp.bfloat16)
        right = r_ref[0]
        contribution = jnp.dot(high, right, preferred_element_type=jnp.float32) + jnp.dot(
            low, right, preferred_element_type=jnp.float32
        )
        t = tgt_ref[k]
        o_ref[t] = o_ref[t] + contribution


def pair_partial(sources, left_blocks, right_blocks, source_index, target_index, live_count, sector_count):
    slots, block_size, _ = left_blocks.shape
    n_sources = sources.shape[0]

    def live_slot(k, cnt):
        return jnp.minimum(k, jnp.clip(cnt[0] - 1, 0, slots - 1))

    def source_map(k, src, tgt, cnt):
        return (jnp.clip(src[live_slot(k, cnt)], 0, n_sources - 1), 0, 0)

    def operator_map(k, src, tgt, cnt):
        return (live_slot(k, cnt), 0, 0)

    block = (1, block_size, block_size)
    grid_spec = pltpu.PrefetchScalarGridSpec(
        num_scalar_prefetch=3,
        grid=(slots,),
        in_specs=[
            pl.BlockSpec(block, source_map),
            pl.BlockSpec(block, operator_map),
            pl.BlockSpec(block, operator_map),
        ],
        out_specs=pl.BlockSpec(
            (sector_count, block_size, block_size), lambda k, src, tgt, cnt: (0, 0, 0)
        ),
    )
    return pl.pallas_call(
        pair_kernel,
        grid_spec=grid_spec,
        out_shape=jax.ShapeDtypeStruct((sector_count, block_size, block_size), jnp.float32),
        compiler_params=pltpu.CompilerParams(dimension_semantics=("arbitrary",)),
    )(source_index, target_index, live_count, sources, left_blocks, right_blocks)


def on_device(
    wavefunction,
    diagonal,
    preconditioner,
    left_operator_blocks,
    right_operator_blocks,
    slot_source_sector,
    slot_target_sector,
    pair_count,
    left_dims,
    right_dims,
):
    sector_count = wavefunction.shape[0]
    block_size = wavefunction.shape[1]
    n_sec = lax.axis_size("sec")
    n_op = lax.axis_size("op")
    share_rows = block_size // n_op
    sec_index = lax.axis_index("sec")
    op_index = lax.axis_index("op")
    first_sector = sec_index * sector_count
    row_start = op_index * share_rows
    entries = float(left_dims.shape[0] * block_size * block_size)
    own_mask = block_mask(
        lax.dynamic_slice_in_dim(left_dims, first_sector, sector_count),
        lax.dynamic_slice_in_dim(right_dims, first_sector, sector_count),
        block_size,
    )
    own_vector = jnp.where(own_mask, wavefunction, jnp.zeros_like(wavefunction))
    diag_view = diagonal.astype(jnp.float32)
    scale_view = preconditioner.astype(jnp.float32)
    vector_view = own_vector.astype(jnp.float32)

    owner = slot_source_sector // sector_count
    source_index = ((owner - sec_index) % n_sec) * sector_count + slot_source_sector % sector_count
    target_index = jnp.clip(slot_target_sector, 0, sector_count - 1)
    live_count = pair_count

    def apply_partial(field):
        sources = gather_blocks(field, "sec", n_sec).reshape(
            (n_sec * sector_count, block_size, block_size)
        )
        partial_value = pair_partial(
            sources,
            left_operator_blocks,
            right_operator_blocks,
            source_index,
            target_index,
            live_count,
            sector_count,
        )
        return reduce_scatter_rows(partial_value, "op", n_op)

    pair_rows = apply_partial(own_vector)
    pairs_first = (
        ordered_gather(pair_rows, "op", n_op)
        .transpose(1, 0, 2, 3)
        .reshape((sector_count, block_size, block_size))
    )
    sigma_first = jnp.where(own_mask, diag_view * vector_view + pairs_first, 0.0)
    norm_vector, correlation = reduce_vector(
        jnp.stack([jnp.sum(vector_view * vector_view), jnp.sum(vector_view * sigma_first)]),
        "sec",
        n_sec,
    )
    rayleigh = correlation / norm_vector
    residual = sigma_first - rayleigh * vector_view
    scaled = scale_view * residual
    along_vector, scaled_square = reduce_vector(
        jnp.stack([jnp.sum(vector_view * scaled), jnp.sum(scaled * scaled)]), "sec", n_sec
    )
    orthogonal = scaled - along_vector / norm_vector * vector_view
    square_norm = scaled_square - along_vector * along_vector / norm_vector
    corr_view = (orthogonal * lax.rsqrt(square_norm / entries + 1e-06)).astype(jnp.bfloat16)

    pairs_second = apply_partial(corr_view)
    mask_rows = lax.dynamic_slice_in_dim(own_mask, row_start, share_rows, 1)
    diag_rows = lax.dynamic_slice_in_dim(diag_view, row_start, share_rows, 1)
    corr_rows = lax.dynamic_slice_in_dim(corr_view, row_start, share_rows, 1).astype(jnp.float32)
    vector_rows = lax.dynamic_slice_in_dim(vector_view, row_start, share_rows, 1)
    product_rows = jnp.where(mask_rows, diag_rows * corr_rows + pairs_second, 0.0)
    local_terms = jnp.stack(
        [jnp.sum(vector_rows * product_rows), jnp.sum(corr_rows * product_rows)]
    )
    cross_term, self_term = reduce_vector(reduce_vector(local_terms, "op", n_op), "sec", n_sec)
    projected = jnp.stack(
        [rayleigh, cross_term * lax.rsqrt(norm_vector * entries), self_term / entries]
    )
    return (corr_view, product_rows, projected)


def solution(mesh):
    in_specs = (
        P("sec", None, None),
        P("sec", None, None),
        P("sec", None, None),
        P(("sec", "op"), None, None),
        P(("sec", "op"), None, None),
        P(("sec", "op")),
        P(("sec", "op")),
        P(("sec", "op")),
        P(),
        P(),
    )
    out_specs = (P("sec", None, None), P("sec", "op", None), P())
    return jax.shard_map(
        on_device, mesh=mesh, in_specs=in_specs, out_specs=out_specs, check_vma=False
    )
```

time: 1180 us -> 1680 us (1.42)
  starting transfers between devices: 0.16 us -> 1560 us
  waiting for transfers between devices: 624 us -> 26.3 us
  blocking collectives: 179 us -> 0 us
  loops' own time: 147 us -> 0 us
  matrix products: 96.2 us -> 0 us
  other arithmetic: 45.2 us -> 17.2 us
  local copies, waits for them, and re-layouts: 64.2 us -> 37.6 us
  Pallas kernels: 0 us -> 18.5 us
    ppermute x0 -> x199, starting transfers between devices: none -> 1560 us  [the longest x137 949 us: gather_blocks(): lax.ppermute(value, axis_name, [(i, (i - shift) % count) for i in range(c...]
    psum x2 -> x0, waiting for transfers between devices: 482 us -> none  [sum_pairs(): return lax.psum(partial_value, 'op')]
    psum x4 -> x0, blocking collectives: 179 us -> none  [reduce_dots(): return lax.psum(values, 'sec')]
    another operation x2 -> x0, loops' own time: 147 us -> none  [pair_partial(): return lax.fori_loop(0, left_operator_blocks.shape[0], add_pair, zero_sum)]
    all_gather x2 -> x0, waiting for transfers between devices: 142 us -> none  [gather_sources(): return lax.all_gather(own_vector, 'sec', axis=0, tiled=True)]
    dot_general x64 -> x0, matrix products: 96.2 us -> none  [the longest x32 59.3 us: add_pair(): jnp.dot(middle, right_operator_blocks[slot_index].astype(jnp.float32), pr...]
    dynamic_slice x65 -> x4, local copies, waits for them, and re-layouts: 61.1 us -> 3.75 us  [reduce_scatter_rows(): lax.dynamic_slice_in_dim(partial_value, (index + shift) % count * rows, r...]
    another operation x32 -> x6, other arithmetic: 34.6 us -> 7.75 us  [the longest x3 3.88 us: gather_blocks(): return jnp.stack(parts, 0)]
  transfers between devices with their start and end apart: 4 -> 199, of which waited for: 4 -> 11; matrix products, arithmetic and copies ran while one was open for 0% -> 2% of each run, Pallas kernels for 0% -> 0%
where the time goes in v1:
time: 1680 us; the launch traced here: 1670 us
  starting transfers between devices  1560 us (93%)
  local copies, waits for them, and re-layouts  37.6 us (2%)
  waiting for transfers between devices  26.3 us (2%)
  Pallas kernels  18.5 us (1%)
  other arithmetic  17.2 us (1%)
    ppermute x137, starting transfers between devices, gather_blocks(): lax.ppermute(value, axis_name, [(i, (i - shift) % count) for i in range(c...  949 us
    ppermute x62, starting transfers between devices, reduce_scatter_rows(): lax.ppermute(chunk, axis_name, [(i, (i + shift) % count) for i in range(c...  613 us
  transfers between devices with their start and end apart: 199, of which 11 were waited for; matrix products, arithmetic and copies ran while one was open for 2% of the time, Pallas kernels for 0%

profile of v1, /device:TPU:1, one launch (start us, length us, event | category | flops | bytes accessed | tf_op | source)
XLA Modules:
  0.0 1672.2 jit_solution(17112190279191422498)
XLA Ops:
  3.3 8.7 collective-permute-start
  45.4 20.5 %collective-permute-start.9 = (bf16[2,256,256]{2,1,0:T(8,128)(2,1)S(1)}, bf16[2,256,256]{2,1,0:T(8,128)(2,1)S(1)}, u32[]{:S(2)}, u32[]{:S(2)}) collective-permute-start(bf16[2,256,256]{2,1,0:T(8,128)(2,1)S(1)} %get-tuple-element.12), channel_id=1, source_target_pairs={{0,192},{32,224},{64,256},{96,288},{128,320},{160,352},{192,384},{... | collective-permute-start | bytes 786440 | tf_op jit(solution)/shard_map/ppermute | solution.py:22
  95.7 9.3 shard_map.121
  106.0 22.8 %collective-permute-start.45 = (f32[2,8,256]{2,1,0:T(8,128)S(1)}, f32[2,8,256]{2,1,0:T(8,128)S(1)}, u32[]{:S(2)}, u32[]{:S(2)}) collective-permute-start(f32[2,8,256]{2,1,0:T(8,128)S(1)} %get-tuple-element.50), channel_id=1, source_target_pairs={{0,31},{1,0},{2,1},{3,2},{4,3},{5,4},{6,5},{7,6},{8,7},{9,8},{10,9... | collective-permute-start | bytes 49160 | tf_op jit(solution)/shard_map/ppermute | solution.py:45
  128.8 19.0 %collective-permute-start.44 = (f32[2,8,256]{2,1,0:T(8,128)S(1)}, f32[2,8,256]{2,1,0:T(8,128)S(1)}, u32[]{:S(2)}, u32[]{:S(2)}) collective-permute-start(f32[2,8,256]{2,1,0:T(8,128)S(1)} %get-tuple-element.51), channel_id=1, source_target_pairs={{0,30},{1,31},{2,0},{3,1},{4,2},{5,3},{6,4},{7,5},{8,6},{9,7},{10,... | collective-permute-start | bytes 49160 | tf_op jit(solution)/shard_map/ppermute | solution.py:45
  147.8 19.0 %collective-permute-start.43 = (f32[2,8,256]{2,1,0:T(8,128)S(1)}, f32[2,8,256]{2,1,0:T(8,128)S(1)}, u32[]{:S(2)}, u32[]{:S(2)}) collective-permute-start(f32[2,8,256]{2,1,0:T(8,128)S(1)} %get-tuple-element.52), channel_id=1, source_target_pairs={{0,29},{1,30},{2,31},{3,0},{4,1},{5,2},{6,3},{7,4},{8,5},{9,6},{10... | collective-permute-start | bytes 49160 | tf_op jit(solution)/shard_map/ppermute | solution.py:45
  166.8 19.0 %collective-permute-start.42 = (f32[2,8,256]{2,1,0:T(8,128)S(1)}, f32[2,8,256]{2,1,0:T(8,128)S(1)}, u32[]{:S(2)}, u32[]{:S(2)}) collective-permute-start(f32[2,8,256]{2,1,0:T(8,128)S(1)} %get-tuple-element.53), channel_id=1, source_target_pairs={{0,28},{1,29},{2,30},{3,31},{4,0},{5,1},{6,2},{7,3},{8,4},{9,5},{1... | collective-permute-start | bytes 49160 | tf_op jit(solution)/shard_map/ppermute | solution.py:45
  185.8 19.0 %collective-permute-start.41 = (f32[2,8,256]{2,1,0:T(8,128)S(1)}, f32[2,8,256]{2,1,0:T(8,128)S(1)}, u32[]{:S(2)}, u32[]{:S(2)}) collective-permute-start(f32[2,8,256]{2,1,0:T(8,128)S(1)} %get-tuple-element.54), channel_id=1, source_target_pairs={{0,27},{1,28},{2,29},{3,30},{4,31},{5,0},{6,1},{7,2},{8,3},{9,4},{... | collective-permute-start | bytes 49160 | tf_op jit(solution)/shard_map/ppermute | solution.py:45
  204.9 19.0 %collective-permute-start.40 = (f32[2,8,256]{2,1,0:T(8,128)S(1)}, f32[2,8,256]{2,1,0:T(8,128)S(1)}, u32[]{:S(2)}, u32[]{:S(2)}) collective-permute-start(f32[2,8,256]{2,1,0:T(8,128)S(1)} %get-tuple-element.55), channel_id=1, source_target_pairs={{0,26},{1,27},{2,28},{3,29},{4,30},{5,31},{6,0},{7,1},{8,2},{9,3},... | collective-permute-start | bytes 49160 | tf_op jit(solution)/shard_map/ppermute | solution.py:45
  223.9 19.0 %collective-permute-start.39 = (f32[2,8,256]{2,1,0:T(8,128)S(1)}, f32[2,8,256]{2,1,0:T(8,128)S(1)}, u32[]{:S(2)}, u32[]{:S(2)}) collective-permute-start(f32[2,8,256]{2,1,0:T(8,128)S(1)} %get-tuple-element.56), channel_id=1, source_target_pairs={{0,25},{1,26},{2,27},{3,28},{4,29},{5,30},{6,31},{7,0},{8,1},{9,2}... | collective-permute-start | bytes 49160 | tf_op jit(solution)/shard_map/ppermute | solution.py:45
  242.9 19.0 %collective-permute-start.38 = (f32[2,8,256]{2,1,0:T(8,128)S(1)}, f32[2,8,256]{2,1,0:T(8,128)S(1)}, u32[]{:S(2)}, u32[]{:S(2)}) collective-permute-start(f32[2,8,256]{2,1,0:T(8,128)S(1)} %get-tuple-element.57), channel_id=1, source_target_pairs={{0,24},{1,25},{2,26},{3,27},{4,28},{5,29},{6,30},{7,31},{8,0},{9,1... | collective-permute-start | bytes 49160 | tf_op jit(solution)/shard_map/ppermute | solution.py:45
  261.9 19.0 %collective-permute-start.37 = (f32[2,8,256]{2,1,0:T(8,128)S(1)}, f32[2,8,256]{2,1,0:T(8,128)S(1)}, u32[]{:S(2)}, u32[]{:S(2)}) collective-permute-start(f32[2,8,256]{2,1,0:T(8,128)S(1)} %get-tuple-element.58), channel_id=1, source_target_pairs={{0,23},{1,24},{2,25},{3,26},{4,27},{5,28},{6,29},{7,30},{8,31},{9,... | collective-permute-start | bytes 49160 | tf_op jit(solution)/shard_map/ppermute | solution.py:45
  281.0 19.0 %collective-permute-start.36 = (f32[2,8,256]{2,1,0:T(8,128)S(1)}, f32[2,8,256]{2,1,0:T(8,128)S(1)}, u32[]{:S(2)}, u32[]{:S(2)}) collective-permute-start(f32[2,8,256]{2,1,0:T(8,128)S(1)} %get-tuple-element.59), channel_id=1, source_target_pairs={{0,22},{1,23},{2,24},{3,25},{4,26},{5,27},{6,28},{7,29},{8,30},{9,... | collective-permute-start | bytes 49160 | tf_op jit(solution)/shard_map/ppermute | solution.py:45
  300.0 13.6 collective-permute-start.35
  316.2 7.9 collective-permute-start.33
  338.4 7.5 collective-permute-start.30
  357.7 8.6 collective-permute-start.27
  369.2 9.1 collective-permute-start.25
  420.8 20.6 %collective-permute-start.46 = (f32[2,8,256]{2,1,0:T(8,128)S(1)}, f32[2,8,256]{2,1,0:T(8,128)S(1)}, u32[]{:S(2)}, u32[]{:S(2)}) collective-permute-start(f32[2,8,256]{2,1,0:T(8,128)S(1)} %get-tuple-element.17), channel_id=1, source_target_pairs={{0,31},{1,0},{2,1},{3,2},{4,3},{5,4},{6,5},{7,6},{8,7},{9,8},{10,9... | collective-permute-start | bytes 49160 | tf_op jit(solution)/shard_map/ppermute | solution.py:22
  441.4 19.0 %collective-permute-start.47 = (f32[2,8,256]{2,1,0:T(8,128)S(1)}, f32[2,8,256]{2,1,0:T(8,128)S(1)}, u32[]{:S(2)}, u32[]{:S(2)}) collective-permute-start(f32[2,8,256]{2,1,0:T(8,128)S(1)} %get-tuple-element.17), channel_id=1, source_target_pairs={{0,30},{1,31},{2,0},{3,1},{4,2},{5,3},{6,4},{7,5},{8,6},{9,7},{10,... | collective-permute-start | bytes 49160 | tf_op jit(solution)/shard_map/ppermute | solution.py:22
  460.5 19.0 %collective-permute-start.48 = (f32[2,8,256]{2,1,0:T(8,128)S(1)}, f32[2,8,256]{2,1,0:T(8,128)S(1)}, u32[]{:S(2)}, u32[]{:S(2)}) collective-permute-start(f32[2,8,256]{2,1,0:T(8,128)S(1)} %get-tuple-element.17), channel_id=1, source_target_pairs={{0,29},{1,30},{2,31},{3,0},{4,1},{5,2},{6,3},{7,4},{8,5},{9,6},{10... | collective-permute-start | bytes 49160 | tf_op jit(solution)/shard_map/ppermute | solution.py:22
  479.5 19.0 %collective-permute-start.49 = (f32[2,8,256]{2,1,0:T(8,128)S(1)}, f32[2,8,256]{2,1,0:T(8,128)S(1)}, u32[]{:S(2)}, u32[]{:S(2)}) collective-permute-start(f32[2,8,256]{2,1,0:T(8,128)S(1)} %get-tuple-element.17), channel_id=1, source_target_pairs={{0,28},{1,29},{2,30},{3,31},{4,0},{5,1},{6,2},{7,3},{8,4},{9,5},{1... | collective-permute-start | bytes 49160 | tf_op jit(solution)/shard_map/ppermute | solution.py:22
  498.5 19.0 %collective-permute-start.50 = (f32[2,8,256]{2,1,0:T(8,128)S(1)}, f32[2,8,256]{2,1,0:T(8,128)S(1)}, u32[]{:S(2)}, u32[]{:S(2)}) collective-permute-start(f32[2,8,256]{2,1,0:T(8,128)S(1)} %get-tuple-element.17), channel_id=1, source_target_pairs={{0,27},{1,28},{2,29},{3,30},{4,31},{5,0},{6,1},{7,2},{8,3},{9,4},{... | collective-permute-start | bytes 49160 | tf_op jit(solution)/shard_map/ppermute | solution.py:22
  517.5 19.0 %collective-permute-start.51 = (f32[2,8,256]{2,1,0:T(8,128)S(1)}, f32[2,8,256]{2,1,0:T(8,128)S(1)}, u32[]{:S(2)}, u32[]{:S(2)}) collective-permute-start(f32[2,8,256]{2,1,0:T(8,128)S(1)} %get-tuple-element.17), channel_id=1, source_target_pairs={{0,26},{1,27},{2,28},{3,29},{4,30},{5,31},{6,0},{7,1},{8,2},{9,3},... | collective-permute-start | bytes 49160 | tf_op jit(solution)/shard_map/ppermute | solution.py:22
  536.5 19.0 %collective-permute-start.52 = (f32[2,8,256]{2,1,0:T(8,128)S(1)}, f32[2,8,256]{2,1,0:T(8,128)S(1)}, u32[]{:S(2)}, u32[]{:S(2)}) collective-permute-start(f32[2,8,256]{2,1,0:T(8,128)S(1)} %get-tuple-element.17), channel_id=1, source_target_pairs={{0,25},{1,26},{2,27},{3,28},{4,29},{5,30},{6,31},{7,0},{8,1},{9,2}... | collective-permute-start | bytes 49160 | tf_op jit(solution)/shard_map/ppermute | solution.py:22
  555.6 19.0 %collective-permute-start.53 = (f32[2,8,256]{2,1,0:T(8,128)S(1)}, f32[2,8,256]{2,1,0:T(8,128)S(1)}, u32[]{:S(2)}, u32[]{:S(2)}) collective-permute-start(f32[2,8,256]{2,1,0:T(8,128)S(1)} %get-tuple-element.17), channel_id=1, source_target_pairs={{0,24},{1,25},{2,26},{3,27},{4,28},{5,29},{6,30},{7,31},{8,0},{9,1... | collective-permute-start | bytes 49160 | tf_op jit(solution)/shard_map/ppermute | solution.py:22
  574.6 19.0 %collective-permute-start.54 = (f32[2,8,256]{2,1,0:T(8,128)S(1)}, f32[2,8,256]{2,1,0:T(8,128)S(1)}, u32[]{:S(2)}, u32[]{:S(2)}) collective-permute-start(f32[2,8,256]{2,1,0:T(8,128)S(1)} %get-tuple-element.17), channel_id=1, source_target_pairs={{0,23},{1,24},{2,25},{3,26},{4,27},{5,28},{6,29},{7,30},{8,31},{9,... | collective-permute-start | bytes 49160 | tf_op jit(solution)/shard_map/ppermute | solution.py:22
  593.6 19.0 %collective-permute-start.55 = (f32[2,8,256]{2,1,0:T(8,128)S(1)}, f32[2,8,256]{2,1,0:T(8,128)S(1)}, u32[]{:S(2)}, u32[]{:S(2)}) collective-permute-start(f32[2,8,256]{2,1,0:T(8,128)S(1)} %get-tuple-element.17), channel_id=1, source_target_pairs={{0,22},{1,23},{2,24},{3,25},{4,26},{5,27},{6,28},{7,29},{8,30},{9,... | collective-permute-start | bytes 49160 | tf_op jit(solution)/shard_map/ppermute | solution.py:22
  612.7 13.6 collective-permute-start.56
  628.8 7.9 collective-permute-start.58
  669.3 8.6 collective-permute-start.64
  680.9 9.1 collective-permute-start.66
  735.6 8.8 collective-permute-start.77
  915.9 20.9 %collective-permute-start.116 = (bf16[2,256,256]{2,1,0:T(8,128)(2,1)S(1)}, bf16[2,256,256]{2,1,0:T(8,128)(2,1)S(1)}, u32[]{:S(2)}, u32[]{:S(2)}) collective-permute-start(bf16[2,256,256]{2,1,0:T(8,128)(2,1)S(1)} %get-tuple-element.14), channel_id=1, source_target_pairs={{0,192},{32,224},{64,256},{96,288},{128,320},{160,352},{192,384},{... | collective-permute-start | bytes 786440 | tf_op jit(solution)/shard_map/ppermute | solution.py:22
  966.5 9.3 shard_map.122
  976.7 17.4 %collective-permute-start.152 = (f32[2,8,256]{2,1,0:T(8,128)S(1)}, f32[2,8,256]{2,1,0:T(8,128)S(1)}, u32[]{:S(2)}, u32[]{:S(2)}) collective-permute-start(f32[2,8,256]{2,1,0:T(8,128)S(1)} %get-tuple-element.19), channel_id=1, source_target_pairs={{0,31},{1,0},{2,1},{3,2},{4,3},{5,4},{6,5},{7,6},{8,7},{9,8},{10,9... | collective-permute-start | bytes 49160 | tf_op jit(solution)/shard_map/ppermute | solution.py:45
  994.1 19.0 %collective-permute-start.151 = (f32[2,8,256]{2,1,0:T(8,128)S(1)}, f32[2,8,256]{2,1,0:T(8,128)S(1)}, u32[]{:S(2)}, u32[]{:S(2)}) collective-permute-start(f32[2,8,256]{2,1,0:T(8,128)S(1)} %get-tuple-element.20), channel_id=1, source_target_pairs={{0,30},{1,31},{2,0},{3,1},{4,2},{5,3},{6,4},{7,5},{8,6},{9,7},{10,... | collective-permute-start | bytes 49160 | tf_op jit(solution)/shard_map/ppermute | solution.py:45
  1013.1 19.0 %collective-permute-start.150 = (f32[2,8,256]{2,1,0:T(8,128)S(1)}, f32[2,8,256]{2,1,0:T(8,128)S(1)}, u32[]{:S(2)}, u32[]{:S(2)}) collective-permute-start(f32[2,8,256]{2,1,0:T(8,128)S(1)} %get-tuple-element.21), channel_id=1, source_target_pairs={{0,29},{1,30},{2,31},{3,0},{4,1},{5,2},{6,3},{7,4},{8,5},{9,6},{10... | collective-permute-start | bytes 49160 | tf_op jit(solution)/shard_map/ppermute | solution.py:45
  1032.1 19.0 %collective-permute-start.149 = (f32[2,8,256]{2,1,0:T(8,128)S(1)}, f32[2,8,256]{2,1,0:T(8,128)S(1)}, u32[]{:S(2)}, u32[]{:S(2)}) collective-permute-start(f32[2,8,256]{2,1,0:T(8,128)S(1)} %get-tuple-element.22), channel_id=1, source_target_pairs={{0,28},{1,29},{2,30},{3,31},{4,0},{5,1},{6,2},{7,3},{8,4},{9,5},{1... | collective-permute-start | bytes 49160 | tf_op jit(solution)/shard_map/ppermute | solution.py:45
  1051.1 19.0 %collective-permute-start.148 = (f32[2,8,256]{2,1,0:T(8,128)S(1)}, f32[2,8,256]{2,1,0:T(8,128)S(1)}, u32[]{:S(2)}, u32[]{:S(2)}) collective-permute-start(f32[2,8,256]{2,1,0:T(8,128)S(1)} %get-tuple-element.23), channel_id=1, source_target_pairs={{0,27},{1,28},{2,29},{3,30},{4,31},{5,0},{6,1},{7,2},{8,3},{9,4},{... | collective-permute-start | bytes 49160 | tf_op jit(solution)/shard_map/ppermute | solution.py:45
  1070.2 19.0 %collective-permute-start.147 = (f32[2,8,256]{2,1,0:T(8,128)S(1)}, f32[2,8,256]{2,1,0:T(8,128)S(1)}, u32[]{:S(2)}, u32[]{:S(2)}) collective-permute-start(f32[2,8,256]{2,1,0:T(8,128)S(1)} %get-tuple-element.24), channel_id=1, source_target_pairs={{0,26},{1,27},{2,28},{3,29},{4,30},{5,31},{6,0},{7,1},{8,2},{9,3},... | collective-permute-start | bytes 49160 | tf_op jit(solution)/shard_map/ppermute | solution.py:45
  1089.2 19.0 %collective-permute-start.146 = (f32[2,8,256]{2,1,0:T(8,128)S(1)}, f32[2,8,256]{2,1,0:T(8,128)S(1)}, u32[]{:S(2)}, u32[]{:S(2)}) collective-permute-start(f32[2,8,256]{2,1,0:T(8,128)S(1)} %get-tuple-element.25), channel_id=1, source_target_pairs={{0,25},{1,26},{2,27},{3,28},{4,29},{5,30},{6,31},{7,0},{8,1},{9,2}... | collective-permute-start | bytes 49160 | tf_op jit(solution)/shard_map/ppermute | solution.py:45
  1108.2 19.0 %collective-permute-start.145 = (f32[2,8,256]{2,1,0:T(8,128)S(1)}, f32[2,8,256]{2,1,0:T(8,128)S(1)}, u32[]{:S(2)}, u32[]{:S(2)}) collective-permute-start(f32[2,8,256]{2,1,0:T(8,128)S(1)} %get-tuple-element.26), channel_id=1, source_target_pairs={{0,24},{1,25},{2,26},{3,27},{4,28},{5,29},{6,30},{7,31},{8,0},{9,1... | collective-permute-start | bytes 49160 | tf_op jit(solution)/shard_map/ppermute | solution.py:45
  1127.2 19.0 %collective-permute-start.144 = (f32[2,8,256]{2,1,0:T(8,128)S(1)}, f32[2,8,256]{2,1,0:T(8,128)S(1)}, u32[]{:S(2)}, u32[]{:S(2)}) collective-permute-start(f32[2,8,256]{2,1,0:T(8,128)S(1)} %get-tuple-element.27), channel_id=1, source_target_pairs={{0,23},{1,24},{2,25},{3,26},{4,27},{5,28},{6,29},{7,30},{8,31},{9,... | collective-permute-start | bytes 49160 | tf_op jit(solution)/shard_map/ppermute | solution.py:45
  1146.3 19.0 %collective-permute-start.143 = (f32[2,8,256]{2,1,0:T(8,128)S(1)}, f32[2,8,256]{2,1,0:T(8,128)S(1)}, u32[]{:S(2)}, u32[]{:S(2)}) collective-permute-start(f32[2,8,256]{2,1,0:T(8,128)S(1)} %get-tuple-element.28), channel_id=1, source_target_pairs={{0,22},{1,23},{2,24},{3,25},{4,26},{5,27},{6,28},{7,29},{8,30},{9,... | collective-permute-start | bytes 49160 | tf_op jit(solution)/shard_map/ppermute | solution.py:45
  1165.3 13.6 collective-permute-start.142
  1181.3 7.9 collective-permute-start.140
  1222.8 8.6 collective-permute-start.134
  1234.3 9.1 collective-permute-start.132
  1289.7 20.6 %collective-permute-start.153 = (f32[2]{0:T(128)S(1)}, f32[2]{0:T(128)S(1)}, u32[]{:S(2)}, u32[]{:S(2)}) collective-permute-start(f32[2]{0:T(128)S(1)} %pad_maximum_fusion.5), channel_id=1, source_target_pairs={{0,31},{1,0},{2,1},{3,2},{4,3},{5,4},{6,5},{7,6},{8,7},{9,8},{10,9... | collective-permute-start | bytes 32 | tf_op jit(solution)/shard_map/ppermute | solution.py:22
  1310.3 19.0 %collective-permute-start.154 = (f32[2]{0:T(128)S(1)}, f32[2]{0:T(128)S(1)}, u32[]{:S(2)}, u32[]{:S(2)}) collective-permute-start(f32[2]{0:T(128)S(1)} %pad_maximum_fusion.5), channel_id=1, source_target_pairs={{0,30},{1,31},{2,0},{3,1},{4,2},{5,3},{6,4},{7,5},{8,6},{9,7},{10,... | collective-permute-start | bytes 32 | tf_op jit(solution)/shard_map/ppermute | solution.py:22
  1329.3 19.0 %collective-permute-start.155 = (f32[2]{0:T(128)S(1)}, f32[2]{0:T(128)S(1)}, u32[]{:S(2)}, u32[]{:S(2)}) collective-permute-start(f32[2]{0:T(128)S(1)} %pad_maximum_fusion.5), channel_id=1, source_target_pairs={{0,29},{1,30},{2,31},{3,0},{4,1},{5,2},{6,3},{7,4},{8,5},{9,6},{10... | collective-permute-start | bytes 32 | tf_op jit(solution)/shard_map/ppermute | solution.py:22
  1348.3 19.0 %collective-permute-start.156 = (f32[2]{0:T(128)S(1)}, f32[2]{0:T(128)S(1)}, u32[]{:S(2)}, u32[]{:S(2)}) collective-permute-start(f32[2]{0:T(128)S(1)} %pad_maximum_fusion.5), channel_id=1, source_target_pairs={{0,28},{1,29},{2,30},{3,31},{4,0},{5,1},{6,2},{7,3},{8,4},{9,5},{1... | collective-permute-start | bytes 32 | tf_op jit(solution)/shard_map/ppermute | solution.py:22
  1367.3 19.0 %collective-permute-start.157 = (f32[2]{0:T(128)S(1)}, f32[2]{0:T(128)S(1)}, u32[]{:S(2)}, u32[]{:S(2)}) collective-permute-start(f32[2]{0:T(128)S(1)} %pad_maximum_fusion.5), channel_id=1, source_target_pairs={{0,27},{1,28},{2,29},{3,30},{4,31},{5,0},{6,1},{7,2},{8,3},{9,4},{... | collective-permute-start | bytes 32 | tf_op jit(solution)/shard_map/ppermute | solution.py:22
  1386.5 19.0 %collective-permute-start.158 = (f32[2]{0:T(128)S(1)}, f32[2]{0:T(128)S(1)}, u32[]{:S(2)}, u32[]{:S(2)}) collective-permute-start(f32[2]{0:T(128)S(1)} %pad_maximum_fusion.5), channel_id=1, source_target_pairs={{0,26},{1,27},{2,28},{3,29},{4,30},{5,31},{6,0},{7,1},{8,2},{9,3},... | collective-permute-start | bytes 32 | tf_op jit(solution)/shard_map/ppermute | solution.py:22
  1405.6 19.0 %collective-permute-start.159 = (f32[2]{0:T(128)S(1)}, f32[2]{0:T(128)S(1)}, u32[]{:S(2)}, u32[]{:S(2)}) collective-permute-start(f32[2]{0:T(128)S(1)} %pad_maximum_fusion.5), channel_id=1, source_target_pairs={{0,25},{1,26},{2,27},{3,28},{4,29},{5,30},{6,31},{7,0},{8,1},{9,2}... | collective-permute-start | bytes 32 | tf_op jit(solution)/shard_map/ppermute | solution.py:22
  1424.7 19.0 %collective-permute-start.160 = (f32[2]{0:T(128)S(1)}, f32[2]{0:T(128)S(1)}, u32[]{:S(2)}, u32[]{:S(2)}) collective-permute-start(f32[2]{0:T(128)S(1)} %pad_maximum_fusion.5), channel_id=1, source_target_pairs={{0,24},{1,25},{2,26},{3,27},{4,28},{5,29},{6,30},{7,31},{8,0},{9,1... | collective-permute-start | bytes 32 | tf_op jit(solution)/shard_map/ppermute | solution.py:22
  1443.8 19.0 %collective-permute-start.161 = (f32[2]{0:T(128)S(1)}, f32[2]{0:T(128)S(1)}, u32[]{:S(2)}, u32[]{:S(2)}) collective-permute-start(f32[2]{0:T(128)S(1)} %pad_maximum_fusion.5), channel_id=1, source_target_pairs={{0,23},{1,24},{2,25},{3,26},{4,27},{5,28},{6,29},{7,30},{8,31},{9,... | collective-permute-start | bytes 32 | tf_op jit(solution)/shard_map/ppermute | solution.py:22
  1462.9 19.0 %collective-permute-start.162 = (f32[2]{0:T(128)S(1)}, f32[2]{0:T(128)S(1)}, u32[]{:S(2)}, u32[]{:S(2)}) collective-permute-start(f32[2]{0:T(128)S(1)} %pad_maximum_fusion.5), channel_id=1, source_target_pairs={{0,22},{1,23},{2,24},{3,25},{4,26},{5,27},{6,28},{7,29},{8,30},{9,... | collective-permute-start | bytes 32 | tf_op jit(solution)/shard_map/ppermute | solution.py:22
  1482.0 13.6 collective-permute-start.163
  1498.2 7.9 collective-permute-start.165
  1539.1 8.6 collective-permute-start.171
  1550.8 9.1 collective-permute-start.173
  1602.6 8.8 collective-permute-start.184
  (553 shorter events, 644.3 us)
Async XLA Ops:
  25.4 41.2 %collective-permute-start.5 = (bf16[2,256,256]{2,1,0:T(8,128)(2,1)S(1)}, bf16[2,256,256]{2,1,0:T(8,128)(2,1)S(1)}, u32[]{:S(2)}, u32[]{:S(2)}) collective-permute-start(bf16[2,256,256]{2,1,0:T(8,128)(2,1)S(1)} %get-tuple-element.12), channel_id=1, source_target_pairs={{0,320},{32,352},{64,384},{96,416},{128,448},{160,480},{192,0},{22... | collective-permute-start | bytes 786440 | tf_op jit(solution)/shard_map/ppermute | solution.py:22
  31.4 37.9 %collective-permute-start.6 = (bf16[2,256,256]{2,1,0:T(8,128)(2,1)S(1)}, bf16[2,256,256]{2,1,0:T(8,128)(2,1)S(1)}, u32[]{:S(2)}, u32[]{:S(2)}) collective-permute-start(bf16[2,256,256]{2,1,0:T(8,128)(2,1)S(1)} %get-tuple-element.12), channel_id=1, source_target_pairs={{0,288},{32,320},{64,352},{96,384},{128,416},{160,448},{192,480},{... | collective-permute-start | bytes 786440 | tf_op jit(solution)/shard_map/ppermute | solution.py:22
  36.5 35.5 %collective-permute-start.7 = (bf16[2,256,256]{2,1,0:T(8,128)(2,1)S(1)}, bf16[2,256,256]{2,1,0:T(8,128)(2,1)S(1)}, u32[]{:S(2)}, u32[]{:S(2)}) collective-permute-start(bf16[2,256,256]{2,1,0:T(8,128)(2,1)S(1)} %get-tuple-element.12), channel_id=1, source_target_pairs={{0,256},{32,288},{64,320},{96,352},{128,384},{160,416},{192,448},{... | collective-permute-start | bytes 786440 | tf_op jit(solution)/shard_map/ppermute | solution.py:22
  45.4 35.4 %collective-permute-start.9 = (bf16[2,256,256]{2,1,0:T(8,128)(2,1)S(1)}, bf16[2,256,256]{2,1,0:T(8,128)(2,1)S(1)}, u32[]{:S(2)}, u32[]{:S(2)}) collective-permute-start(bf16[2,256,256]{2,1,0:T(8,128)(2,1)S(1)} %get-tuple-element.12), channel_id=1, source_target_pairs={{0,192},{32,224},{64,256},{96,288},{128,320},{160,352},{192,384},{... | collective-permute-start | bytes 786440 | tf_op jit(solution)/shard_map/ppermute | solution.py:22
  106.0 98.9 %collective-permute-start.45 = (f32[2,8,256]{2,1,0:T(8,128)S(1)}, f32[2,8,256]{2,1,0:T(8,128)S(1)}, u32[]{:S(2)}, u32[]{:S(2)}) collective-permute-start(f32[2,8,256]{2,1,0:T(8,128)S(1)} %get-tuple-element.50), channel_id=1, source_target_pairs={{0,31},{1,0},{2,1},{3,2},{4,3},{5,4},{6,5},{7,6},{8,7},{9,8},{10,9... | collective-permute-start | bytes 49160 | tf_op jit(solution)/shard_map/ppermute | solution.py:45
  128.8 95.1 %collective-permute-start.44 = (f32[2,8,256]{2,1,0:T(8,128)S(1)}, f32[2,8,256]{2,1,0:T(8,128)S(1)}, u32[]{:S(2)}, u32[]{:S(2)}) collective-permute-start(f32[2,8,256]{2,1,0:T(8,128)S(1)} %get-tuple-element.51), channel_id=1, source_target_pairs={{0,30},{1,31},{2,0},{3,1},{4,2},{5,3},{6,4},{7,5},{8,6},{9,7},{10,... | collective-permute-start | bytes 49160 | tf_op jit(solution)/shard_map/ppermute | solution.py:45
  147.8 95.1 %collective-permute-start.43 = (f32[2,8,256]{2,1,0:T(8,128)S(1)}, f32[2,8,256]{2,1,0:T(8,128)S(1)}, u32[]{:S(2)}, u32[]{:S(2)}) collective-permute-start(f32[2,8,256]{2,1,0:T(8,128)S(1)} %get-tuple-element.52), channel_id=1, source_target_pairs={{0,29},{1,30},{2,31},{3,0},{4,1},{5,2},{6,3},{7,4},{8,5},{9,6},{10... | collective-permute-start | bytes 49160 | tf_op jit(solution)/shard_map/ppermute | solution.py:45
  166.8 95.1 %collective-permute-start.42 = (f32[2,8,256]{2,1,0:T(8,128)S(1)}, f32[2,8,256]{2,1,0:T(8,128)S(1)}, u32[]{:S(2)}, u32[]{:S(2)}) collective-permute-start(f32[2,8,256]{2,1,0:T(8,128)S(1)} %get-tuple-element.53), channel_id=1, source_target_pairs={{0,28},{1,29},{2,30},{3,31},{4,0},{5,1},{6,2},{7,3},{8,4},{9,5},{1... | collective-permute-start | bytes 49160 | tf_op jit(solution)/shard_map/ppermute | solution.py:45
  185.8 95.1 %collective-permute-start.41 = (f32[2,8,256]{2,1,0:T(8,128)S(1)}, f32[2,8,256]{2,1,0:T(8,128)S(1)}, u32[]{:S(2)}, u32[]{:S(2)}) collective-permute-start(f32[2,8,256]{2,1,0:T(8,128)S(1)} %get-tuple-element.54), channel_id=1, source_target_pairs={{0,27},{1,28},{2,29},{3,30},{4,31},{5,0},{6,1},{7,2},{8,3},{9,4},{... | collective-permute-start | bytes 49160 | tf_op jit(solution)/shard_map/ppermute | solution.py:45
  204.9 95.1 %collective-permute-start.40 = (f32[2,8,256]{2,1,0:T(8,128)S(1)}, f32[2,8,256]{2,1,0:T(8,128)S(1)}, u32[]{:S(2)}, u32[]{:S(2)}) collective-permute-start(f32[2,8,256]{2,1,0:T(8,128)S(1)} %get-tuple-element.55), channel_id=1, source_target_pairs={{0,26},{1,27},{2,28},{3,29},{4,30},{5,31},{6,0},{7,1},{8,2},{9,3},... | collective-permute-start | bytes 49160 | tf_op jit(solution)/shard_map/ppermute | solution.py:45
  223.9 89.9 %collective-permute-start.39 = (f32[2,8,256]{2,1,0:T(8,128)S(1)}, f32[2,8,256]{2,1,0:T(8,128)S(1)}, u32[]{:S(2)}, u32[]{:S(2)}) collective-permute-start(f32[2,8,256]{2,1,0:T(8,128)S(1)} %get-tuple-element.56), channel_id=1, source_target_pairs={{0,25},{1,26},{2,27},{3,28},{4,29},{5,30},{6,31},{7,0},{8,1},{9,2}... | collective-permute-start | bytes 49160 | tf_op jit(solution)/shard_map/ppermute | solution.py:45
  242.9 73.3 %collective-permute-start.38 = (f32[2,8,256]{2,1,0:T(8,128)S(1)}, f32[2,8,256]{2,1,0:T(8,128)S(1)}, u32[]{:S(2)}, u32[]{:S(2)}) collective-permute-start(f32[2,8,256]{2,1,0:T(8,128)S(1)} %get-tuple-element.57), channel_id=1, source_target_pairs={{0,24},{1,25},{2,26},{3,27},{4,28},{5,29},{6,30},{7,31},{8,0},{9,1... | collective-permute-start | bytes 49160 | tf_op jit(solution)/shard_map/ppermute | solution.py:45
  261.9 62.2 %collective-permute-start.37 = (f32[2,8,256]{2,1,0:T(8,128)S(1)}, f32[2,8,256]{2,1,0:T(8,128)S(1)}, u32[]{:S(2)}, u32[]{:S(2)}) collective-permute-start(f32[2,8,256]{2,1,0:T(8,128)S(1)} %get-tuple-element.58), channel_id=1, source_target_pairs={{0,23},{1,24},{2,25},{3,26},{4,27},{5,28},{6,29},{7,30},{8,31},{9,... | collective-permute-start | bytes 49160 | tf_op jit(solution)/shard_map/ppermute | solution.py:45
  281.0 50.1 %collective-permute-start.36 = (f32[2,8,256]{2,1,0:T(8,128)S(1)}, f32[2,8,256]{2,1,0:T(8,128)S(1)}, u32[]{:S(2)}, u32[]{:S(2)}) collective-permute-start(f32[2,8,256]{2,1,0:T(8,128)S(1)} %get-tuple-element.59), channel_id=1, source_target_pairs={{0,22},{1,23},{2,24},{3,25},{4,26},{5,27},{6,28},{7,29},{8,30},{9,... | collective-permute-start | bytes 49160 | tf_op jit(solution)/shard_map/ppermute | solution.py:45
  300.0 38.4 %collective-permute-start.35 = (f32[2,8,256]{2,1,0:T(8,128)S(1)}, f32[2,8,256]{2,1,0:T(8,128)S(1)}, u32[]{:S(2)}, u32[]{:S(2)}) collective-permute-start(f32[2,8,256]{2,1,0:T(8,128)S(1)} %get-tuple-element.60), channel_id=1, source_target_pairs={{0,21},{1,22},{2,23},{3,24},{4,25},{5,26},{6,27},{7,28},{8,29},{9,... | collective-permute-start | bytes 49160 | tf_op jit(solution)/shard_map/ppermute | solution.py:45
  316.2 35.0 %collective-permute-start.33 = (f32[2,8,256]{2,1,0:T(8,128)S(1)}, f32[2,8,256]{2,1,0:T(8,128)S(1)}, u32[]{:S(2)}, u32[]{:S(2)}) collective-permute-start(f32[2,8,256]{2,1,0:T(8,128)S(1)} %get-tuple-element.62), channel_id=1, source_target_pairs={{0,19},{1,20},{2,21},{3,22},{4,23},{5,24},{6,25},{7,26},{8,27},{9,... | collective-permute-start | bytes 49160 | tf_op jit(solution)/shard_map/ppermute | solution.py:45
  324.1 33.5 %collective-permute-start.32 = (f32[2,8,256]{2,1,0:T(8,128)S(1)}, f32[2,8,256]{2,1,0:T(8,128)S(1)}, u32[]{:S(2)}, u32[]{:S(2)}) collective-permute-start(f32[2,8,256]{2,1,0:T(8,128)S(1)} %get-tuple-element.63), channel_id=1, source_target_pairs={{0,18},{1,19},{2,20},{3,21},{4,22},{5,23},{6,24},{7,25},{8,26},{9,... | collective-permute-start | bytes 49160 | tf_op jit(solution)/shard_map/ppermute | solution.py:45
  331.1 35.3 %collective-permute-start.31 = (f32[2,8,256]{2,1,0:T(8,128)S(1)}, f32[2,8,256]{2,1,0:T(8,128)S(1)}, u32[]{:S(2)}, u32[]{:S(2)}) collective-permute-start(f32[2,8,256]{2,1,0:T(8,128)S(1)} %get-tuple-element.64), channel_id=1, source_target_pairs={{0,17},{1,18},{2,19},{3,20},{4,21},{5,22},{6,23},{7,24},{8,25},{9,... | collective-permute-start | bytes 49160 | tf_op jit(solution)/shard_map/ppermute | solution.py:45
  420.8 96.7 %collective-permute-start.46 = (f32[2,8,256]{2,1,0:T(8,128)S(1)}, f32[2,8,256]{2,1,0:T(8,128)S(1)}, u32[]{:S(2)}, u32[]{:S(2)}) collective-permute-start(f32[2,8,256]{2,1,0:T(8,128)S(1)} %get-tuple-element.17), channel_id=1, source_target_pairs={{0,31},{1,0},{2,1},{3,2},{4,3},{5,4},{6,5},{7,6},{8,7},{9,8},{10,9... | collective-permute-start | bytes 49160 | tf_op jit(solution)/shard_map/ppermute | solution.py:22
  441.4 95.1 %collective-permute-start.47 = (f32[2,8,256]{2,1,0:T(8,128)S(1)}, f32[2,8,256]{2,1,0:T(8,128)S(1)}, u32[]{:S(2)}, u32[]{:S(2)}) collective-permute-start(f32[2,8,256]{2,1,0:T(8,128)S(1)} %get-tuple-element.17), channel_id=1, source_target_pairs={{0,30},{1,31},{2,0},{3,1},{4,2},{5,3},{6,4},{7,5},{8,6},{9,7},{10,... | collective-permute-start | bytes 49160 | tf_op jit(solution)/shard_map/ppermute | solution.py:22
  460.5 95.1 %collective-permute-start.48 = (f32[2,8,256]{2,1,0:T(8,128)S(1)}, f32[2,8,256]{2,1,0:T(8,128)S(1)}, u32[]{:S(2)}, u32[]{:S(2)}) collective-permute-start(f32[2,8,256]{2,1,0:T(8,128)S(1)} %get-tuple-element.17), channel_id=1, source_target_pairs={{0,29},{1,30},{2,31},{3,0},{4,1},{5,2},{6,3},{7,4},{8,5},{9,6},{10... | collective-permute-start | bytes 49160 | tf_op jit(solution)/shard_map/ppermute | solution.py:22
  479.5 95.1 %collective-permute-start.49 = (f32[2,8,256]{2,1,0:T(8,128)S(1)}, f32[2,8,256]{2,1,0:T(8,128)S(1)}, u32[]{:S(2)}, u32[]{:S(2)}) collective-permute-start(f32[2,8,256]{2,1,0:T(8,128)S(1)} %get-tuple-element.17), channel_id=1, source_target_pairs={{0,28},{1,29},{2,30},{3,31},{4,0},{5,1},{6,2},{7,3},{8,4},{9,5},{1... | collective-permute-start | bytes 49160 | tf_op jit(solution)/shard_map/ppermute | solution.py:22
  498.5 95.2 %collective-permute-start.50 = (f32[2,8,256]{2,1,0:T(8,128)S(1)}, f32[2,8,256]{2,1,0:T(8,128)S(1)}, u32[]{:S(2)}, u32[]{:S(2)}) collective-permute-start(f32[2,8,256]{2,1,0:T(8,128)S(1)} %get-tuple-element.17), channel_id=1, source_target_pairs={{0,27},{1,28},{2,29},{3,30},{4,31},{5,0},{6,1},{7,2},{8,3},{9,4},{... | collective-permute-start | bytes 49160 | tf_op jit(solution)/shard_map/ppermute | solution.py:22
  517.5 95.2 %collective-permute-start.51 = (f32[2,8,256]{2,1,0:T(8,128)S(1)}, f32[2,8,256]{2,1,0:T(8,128)S(1)}, u32[]{:S(2)}, u32[]{:S(2)}) collective-permute-start(f32[2,8,256]{2,1,0:T(8,128)S(1)} %get-tuple-element.17), channel_id=1, source_target_pairs={{0,26},{1,27},{2,28},{3,29},{4,30},{5,31},{6,0},{7,1},{8,2},{9,3},... | collective-permute-start | bytes 49160 | tf_op jit(solution)/shard_map/ppermute | solution.py:22
  536.5 89.8 %collective-permute-start.52 = (f32[2,8,256]{2,1,0:T(8,128)S(1)}, f32[2,8,256]{2,1,0:T(8,128)S(1)}, u32[]{:S(2)}, u32[]{:S(2)}) collective-permute-start(f32[2,8,256]{2,1,0:T(8,128)S(1)} %get-tuple-element.17), channel_id=1, source_target_pairs={{0,25},{1,26},{2,27},{3,28},{4,29},{5,30},{6,31},{7,0},{8,1},{9,2}... | collective-permute-start | bytes 49160 | tf_op jit(solution)/shard_map/ppermute | solution.py:22
  555.6 73.2 %collective-permute-start.53 = (f32[2,8,256]{2,1,0:T(8,128)S(1)}, f32[2,8,256]{2,1,0:T(8,128)S(1)}, u32[]{:S(2)}, u32[]{:S(2)}) collective-permute-start(f32[2,8,256]{2,1,0:T(8,128)S(1)} %get-tuple-element.17), channel_id=1, source_target_pairs={{0,24},{1,25},{2,26},{3,27},{4,28},{5,29},{6,30},{7,31},{8,0},{9,1... | collective-permute-start | bytes 49160 | tf_op jit(solution)/shard_map/ppermute | solution.py:22
  574.6 62.1 %collective-permute-start.54 = (f32[2,8,256]{2,1,0:T(8,128)S(1)}, f32[2,8,256]{2,1,0:T(8,128)S(1)}, u32[]{:S(2)}, u32[]{:S(2)}) collective-permute-start(f32[2,8,256]{2,1,0:T(8,128)S(1)} %get-tuple-element.17), channel_id=1, source_target_pairs={{0,23},{1,24},{2,25},{3,26},{4,27},{5,28},{6,29},{7,30},{8,31},{9,... | collective-permute-start | bytes 49160 | tf_op jit(solution)/shard_map/ppermute | solution.py:22
  593.6 50.0 %collective-permute-start.55 = (f32[2,8,256]{2,1,0:T(8,128)S(1)}, f32[2,8,256]{2,1,0:T(8,128)S(1)}, u32[]{:S(2)}, u32[]{:S(2)}) collective-permute-start(f32[2,8,256]{2,1,0:T(8,128)S(1)} %get-tuple-element.17), channel_id=1, source_target_pairs={{0,22},{1,23},{2,24},{3,25},{4,26},{5,27},{6,28},{7,29},{8,30},{9,... | collective-permute-start | bytes 49160 | tf_op jit(solution)/shard_map/ppermute | solution.py:22
  612.7 38.3 %collective-permute-start.56 = (f32[2,8,256]{2,1,0:T(8,128)S(1)}, f32[2,8,256]{2,1,0:T(8,128)S(1)}, u32[]{:S(2)}, u32[]{:S(2)}) collective-permute-start(f32[2,8,256]{2,1,0:T(8,128)S(1)} %get-tuple-element.17), channel_id=1, source_target_pairs={{0,21},{1,22},{2,23},{3,24},{4,25},{5,26},{6,27},{7,28},{8,29},{9,... | collective-permute-start | bytes 49160 | tf_op jit(solution)/shard_map/ppermute | solution.py:22
  628.8 34.2 %collective-permute-start.58 = (f32[2,8,256]{2,1,0:T(8,128)S(1)}, f32[2,8,256]{2,1,0:T(8,128)S(1)}, u32[]{:S(2)}, u32[]{:S(2)}) collective-permute-start(f32[2,8,256]{2,1,0:T(8,128)S(1)} %get-tuple-element.17), channel_id=1, source_target_pairs={{0,19},{1,20},{2,21},{3,22},{4,23},{5,24},{6,25},{7,26},{8,27},{9,... | collective-permute-start | bytes 49160 | tf_op jit(solution)/shard_map/ppermute | solution.py:22
  643.6 34.4 %collective-permute-start.60 = (f32[2,8,256]{2,1,0:T(8,128)S(1)}, f32[2,8,256]{2,1,0:T(8,128)S(1)}, u32[]{:S(2)}, u32[]{:S(2)}) collective-permute-start(f32[2,8,256]{2,1,0:T(8,128)S(1)} %get-tuple-element.17), channel_id=1, source_target_pairs={{0,17},{1,18},{2,19},{3,20},{4,21},{5,22},{6,23},{7,24},{8,25},{9,... | collective-permute-start | bytes 49160 | tf_op jit(solution)/shard_map/ppermute | solution.py:22
  893.6 43.9 %collective-permute-start.112 = (bf16[2,256,256]{2,1,0:T(8,128)(2,1)S(1)}, bf16[2,256,256]{2,1,0:T(8,128)(2,1)S(1)}, u32[]{:S(2)}, u32[]{:S(2)}) collective-permute-start(bf16[2,256,256]{2,1,0:T(8,128)(2,1)S(1)} %get-tuple-element.14), channel_id=1, source_target_pairs={{0,320},{32,352},{64,384},{96,416},{128,448},{160,480},{192,0},{22... | collective-permute-start | bytes 786440 | tf_op jit(solution)/shard_map/ppermute | solution.py:22
  898.4 41.9 %collective-permute-start.113 = (bf16[2,256,256]{2,1,0:T(8,128)(2,1)S(1)}, bf16[2,256,256]{2,1,0:T(8,128)(2,1)S(1)}, u32[]{:S(2)}, u32[]{:S(2)}) collective-permute-start(bf16[2,256,256]{2,1,0:T(8,128)(2,1)S(1)} %get-tuple-element.14), channel_id=1, source_target_pairs={{0,288},{32,320},{64,352},{96,384},{128,416},{160,448},{192,480},{... | collective-permute-start | bytes 786440 | tf_op jit(solution)/shard_map/ppermute | solution.py:22
  906.7 36.3 %collective-permute-start.114 = (bf16[2,256,256]{2,1,0:T(8,128)(2,1)S(1)}, bf16[2,256,256]{2,1,0:T(8,128)(2,1)S(1)}, u32[]{:S(2)}, u32[]{:S(2)}) collective-permute-start(bf16[2,256,256]{2,1,0:T(8,128)(2,1)S(1)} %get-tuple-element.14), channel_id=1, source_target_pairs={{0,256},{32,288},{64,320},{96,352},{128,384},{160,416},{192,448},{... | collective-permute-start | bytes 786440 | tf_op jit(solution)/shard_map/ppermute | solution.py:22
  912.2 34.2 %collective-permute-start.115 = (bf16[2,256,256]{2,1,0:T(8,128)(2,1)S(1)}, bf16[2,256,256]{2,1,0:T(8,128)(2,1)S(1)}, u32[]{:S(2)}, u32[]{:S(2)}) collective-permute-start(bf16[2,256,256]{2,1,0:T(8,128)(2,1)S(1)} %get-tuple-element.14), channel_id=1, source_target_pairs={{0,224},{32,256},{64,288},{96,320},{128,352},{160,384},{192,416},{... | collective-permute-start | bytes 786440 | tf_op jit(solution)/shard_map/ppermute | solution.py:22
  915.9 36.0 %collective-permute-start.116 = (bf16[2,256,256]{2,1,0:T(8,128)(2,1)S(1)}, bf16[2,256,256]{2,1,0:T(8,128)(2,1)S(1)}, u32[]{:S(2)}, u32[]{:S(2)}) collective-permute-start(bf16[2,256,256]{2,1,0:T(8,128)(2,1)S(1)} %get-tuple-element.14), channel_id=1, source_target_pairs={{0,192},{32,224},{64,256},{96,288},{128,320},{160,352},{192,384},{... | collective-permute-start | bytes 786440 | tf_op jit(solution)/shard_map/ppermute | solution.py:22
  976.7 93.4 %collective-permute-start.152 = (f32[2,8,256]{2,1,0:T(8,128)S(1)}, f32[2,8,256]{2,1,0:T(8,128)S(1)}, u32[]{:S(2)}, u32[]{:S(2)}) collective-permute-start(f32[2,8,256]{2,1,0:T(8,128)S(1)} %get-tuple-element.19), channel_id=1, source_target_pairs={{0,31},{1,0},{2,1},{3,2},{4,3},{5,4},{6,5},{7,6},{8,7},{9,8},{10,9... | collective-permute-start | bytes 49160 | tf_op jit(solution)/shard_map/ppermute | solution.py:45
  994.1 95.1 %collective-permute-start.151 = (f32[2,8,256]{2,1,0:T(8,128)S(1)}, f32[2,8,256]{2,1,0:T(8,128)S(1)}, u32[]{:S(2)}, u32[]{:S(2)}) collective-permute-start(f32[2,8,256]{2,1,0:T(8,128)S(1)} %get-tuple-element.20), channel_id=1, source_target_pairs={{0,30},{1,31},{2,0},{3,1},{4,2},{5,3},{6,4},{7,5},{8,6},{9,7},{10,... | collective-permute-start | bytes 49160 | tf_op jit(solution)/shard_map/ppermute | solution.py:45
  1013.1 95.1 %collective-permute-start.150 = (f32[2,8,256]{2,1,0:T(8,128)S(1)}, f32[2,8,256]{2,1,0:T(8,128)S(1)}, u32[]{:S(2)}, u32[]{:S(2)}) collective-permute-start(f32[2,8,256]{2,1,0:T(8,128)S(1)} %get-tuple-element.21), channel_id=1, source_target_pairs={{0,29},{1,30},{2,31},{3,0},{4,1},{5,2},{6,3},{7,4},{8,5},{9,6},{10... | collective-permute-start | bytes 49160 | tf_op jit(solution)/shard_map/ppermute | solution.py:45
  1032.1 95.1 %collective-permute-start.149 = (f32[2,8,256]{2,1,0:T(8,128)S(1)}, f32[2,8,256]{2,1,0:T(8,128)S(1)}, u32[]{:S(2)}, u32[]{:S(2)}) collective-permute-start(f32[2,8,256]{2,1,0:T(8,128)S(1)} %get-tuple-element.22), channel_id=1, source_target_pairs={{0,28},{1,29},{2,30},{3,31},{4,0},{5,1},{6,2},{7,3},{8,4},{9,5},{1... | collective-permute-start | bytes 49160 | tf_op jit(solution)/shard_map/ppermute | solution.py:45
  1051.1 95.1 %collective-permute-start.148 = (f32[2,8,256]{2,1,0:T(8,128)S(1)}, f32[2,8,256]{2,1,0:T(8,128)S(1)}, u32[]{:S(2)}, u32[]{:S(2)}) collective-permute-start(f32[2,8,256]{2,1,0:T(8,128)S(1)} %get-tuple-element.23), channel_id=1, source_target_pairs={{0,27},{1,28},{2,29},{3,30},{4,31},{5,0},{6,1},{7,2},{8,3},{9,4},{... | collective-permute-start | bytes 49160 | tf_op jit(solution)/shard_map/ppermute | solution.py:45
  1070.2 95.1 %collective-permute-start.147 = (f32[2,8,256]{2,1,0:T(8,128)S(1)}, f32[2,8,256]{2,1,0:T(8,128)S(1)}, u32[]{:S(2)}, u32[]{:S(2)}) collective-permute-start(f32[2,8,256]{2,1,0:T(8,128)S(1)} %get-tuple-element.24), channel_id=1, source_target_pairs={{0,26},{1,27},{2,28},{3,29},{4,30},{5,31},{6,0},{7,1},{8,2},{9,3},... | collective-permute-start | bytes 49160 | tf_op jit(solution)/shard_map/ppermute | solution.py:45
  1089.2 89.8 %collective-permute-start.146 = (f32[2,8,256]{2,1,0:T(8,128)S(1)}, f32[2,8,256]{2,1,0:T(8,128)S(1)}, u32[]{:S(2)}, u32[]{:S(2)}) collective-permute-start(f32[2,8,256]{2,1,0:T(8,128)S(1)} %get-tuple-element.25), channel_id=1, source_target_pairs={{0,25},{1,26},{2,27},{3,28},{4,29},{5,30},{6,31},{7,0},{8,1},{9,2}... | collective-permute-start | bytes 49160 | tf_op jit(solution)/shard_map/ppermute | solution.py:45
  1108.2 73.1 %collective-permute-start.145 = (f32[2,8,256]{2,1,0:T(8,128)S(1)}, f32[2,8,256]{2,1,0:T(8,128)S(1)}, u32[]{:S(2)}, u32[]{:S(2)}) collective-permute-start(f32[2,8,256]{2,1,0:T(8,128)S(1)} %get-tuple-element.26), channel_id=1, source_target_pairs={{0,24},{1,25},{2,26},{3,27},{4,28},{5,29},{6,30},{7,31},{8,0},{9,1... | collective-permute-start | bytes 49160 | tf_op jit(solution)/shard_map/ppermute | solution.py:45
  1127.2 62.0 %collective-permute-start.144 = (f32[2,8,256]{2,1,0:T(8,128)S(1)}, f32[2,8,256]{2,1,0:T(8,128)S(1)}, u32[]{:S(2)}, u32[]{:S(2)}) collective-permute-start(f32[2,8,256]{2,1,0:T(8,128)S(1)} %get-tuple-element.27), channel_id=1, source_target_pairs={{0,23},{1,24},{2,25},{3,26},{4,27},{5,28},{6,29},{7,30},{8,31},{9,... | collective-permute-start | bytes 49160 | tf_op jit(solution)/shard_map/ppermute | solution.py:45
  1146.3 49.9 %collective-permute-start.143 = (f32[2,8,256]{2,1,0:T(8,128)S(1)}, f32[2,8,256]{2,1,0:T(8,128)S(1)}, u32[]{:S(2)}, u32[]{:S(2)}) collective-permute-start(f32[2,8,256]{2,1,0:T(8,128)S(1)} %get-tuple-element.28), channel_id=1, source_target_pairs={{0,22},{1,23},{2,24},{3,25},{4,26},{5,27},{6,28},{7,29},{8,30},{9,... | collective-permute-start | bytes 49160 | tf_op jit(solution)/shard_map/ppermute | solution.py:45
  1165.3 38.3 %collective-permute-start.142 = (f32[2,8,256]{2,1,0:T(8,128)S(1)}, f32[2,8,256]{2,1,0:T(8,128)S(1)}, u32[]{:S(2)}, u32[]{:S(2)}) collective-permute-start(f32[2,8,256]{2,1,0:T(8,128)S(1)} %get-tuple-element.29), channel_id=1, source_target_pairs={{0,21},{1,22},{2,23},{3,24},{4,25},{5,26},{6,27},{7,28},{8,29},{9,... | collective-permute-start | bytes 49160 | tf_op jit(solution)/shard_map/ppermute | solution.py:45
  1178.9 33.1 %collective-permute-start.141 = (f32[2,8,256]{2,1,0:T(8,128)S(1)}, f32[2,8,256]{2,1,0:T(8,128)S(1)}, u32[]{:S(2)}, u32[]{:S(2)}) collective-permute-start(f32[2,8,256]{2,1,0:T(8,128)S(1)} %get-tuple-element.30), channel_id=1, source_target_pairs={{0,20},{1,21},{2,22},{3,23},{4,24},{5,25},{6,26},{7,27},{8,28},{9,... | collective-permute-start | bytes 49160 | tf_op jit(solution)/shard_map/ppermute | solution.py:45
  1181.3 35.0 %collective-permute-start.140 = (f32[2,8,256]{2,1,0:T(8,128)S(1)}, f32[2,8,256]{2,1,0:T(8,128)S(1)}, u32[]{:S(2)}, u32[]{:S(2)}) collective-permute-start(f32[2,8,256]{2,1,0:T(8,128)S(1)} %get-tuple-element.31), channel_id=1, source_target_pairs={{0,19},{1,20},{2,21},{3,22},{4,23},{5,24},{6,25},{7,26},{8,27},{9,... | collective-permute-start | bytes 49160 | tf_op jit(solution)/shard_map/ppermute | solution.py:45
  1189.2 33.5 %collective-permute-start.139 = (f32[2,8,256]{2,1,0:T(8,128)S(1)}, f32[2,8,256]{2,1,0:T(8,128)S(1)}, u32[]{:S(2)}, u32[]{:S(2)}) collective-permute-start(f32[2,8,256]{2,1,0:T(8,128)S(1)} %get-tuple-element.32), channel_id=1, source_target_pairs={{0,18},{1,19},{2,20},{3,21},{4,22},{5,23},{6,24},{7,25},{8,26},{9,... | collective-permute-start | bytes 49160 | tf_op jit(solution)/shard_map/ppermute | solution.py:45
  1196.2 35.3 %collective-permute-start.138 = (f32[2,8,256]{2,1,0:T(8,128)S(1)}, f32[2,8,256]{2,1,0:T(8,128)S(1)}, u32[]{:S(2)}, u32[]{:S(2)}) collective-permute-start(f32[2,8,256]{2,1,0:T(8,128)S(1)} %get-tuple-element.33), channel_id=1, source_target_pairs={{0,17},{1,18},{2,19},{3,20},{4,21},{5,22},{6,23},{7,24},{8,25},{9,... | collective-permute-start | bytes 49160 | tf_op jit(solution)/shard_map/ppermute | solution.py:45
  1289.7 96.8 %collective-permute-start.153 = (f32[2]{0:T(128)S(1)}, f32[2]{0:T(128)S(1)}, u32[]{:S(2)}, u32[]{:S(2)}) collective-permute-start(f32[2]{0:T(128)S(1)} %pad_maximum_fusion.5), channel_id=1, source_target_pairs={{0,31},{1,0},{2,1},{3,2},{4,3},{5,4},{6,5},{7,6},{8,7},{9,8},{10,9... | collective-permute-start | bytes 32 | tf_op jit(solution)/shard_map/ppermute | solution.py:22
  1310.3 95.3 %collective-permute-start.154 = (f32[2]{0:T(128)S(1)}, f32[2]{0:T(128)S(1)}, u32[]{:S(2)}, u32[]{:S(2)}) collective-permute-start(f32[2]{0:T(128)S(1)} %pad_maximum_fusion.5), channel_id=1, source_target_pairs={{0,30},{1,31},{2,0},{3,1},{4,2},{5,3},{6,4},{7,5},{8,6},{9,7},{10,... | collective-permute-start | bytes 32 | tf_op jit(solution)/shard_map/ppermute | solution.py:22
  1329.3 95.3 %collective-permute-start.155 = (f32[2]{0:T(128)S(1)}, f32[2]{0:T(128)S(1)}, u32[]{:S(2)}, u32[]{:S(2)}) collective-permute-start(f32[2]{0:T(128)S(1)} %pad_maximum_fusion.5), channel_id=1, source_target_pairs={{0,29},{1,30},{2,31},{3,0},{4,1},{5,2},{6,3},{7,4},{8,5},{9,6},{10... | collective-permute-start | bytes 32 | tf_op jit(solution)/shard_map/ppermute | solution.py:22
  1348.3 95.4 %collective-permute-start.156 = (f32[2]{0:T(128)S(1)}, f32[2]{0:T(128)S(1)}, u32[]{:S(2)}, u32[]{:S(2)}) collective-permute-start(f32[2]{0:T(128)S(1)} %pad_maximum_fusion.5), channel_id=1, source_target_pairs={{0,28},{1,29},{2,30},{3,31},{4,0},{5,1},{6,2},{7,3},{8,4},{9,5},{1... | collective-permute-start | bytes 32 | tf_op jit(solution)/shard_map/ppermute | solution.py:22
  1367.3 95.5 %collective-permute-start.157 = (f32[2]{0:T(128)S(1)}, f32[2]{0:T(128)S(1)}, u32[]{:S(2)}, u32[]{:S(2)}) collective-permute-start(f32[2]{0:T(128)S(1)} %pad_maximum_fusion.5), channel_id=1, source_target_pairs={{0,27},{1,28},{2,29},{3,30},{4,31},{5,0},{6,1},{7,2},{8,3},{9,4},{... | collective-permute-start | bytes 32 | tf_op jit(solution)/shard_map/ppermute | solution.py:22
  1386.5 95.5 %collective-permute-start.158 = (f32[2]{0:T(128)S(1)}, f32[2]{0:T(128)S(1)}, u32[]{:S(2)}, u32[]{:S(2)}) collective-permute-start(f32[2]{0:T(128)S(1)} %pad_maximum_fusion.5), channel_id=1, source_target_pairs={{0,26},{1,27},{2,28},{3,29},{4,30},{5,31},{6,0},{7,1},{8,2},{9,3},... | collective-permute-start | bytes 32 | tf_op jit(solution)/shard_map/ppermute | solution.py:22
  1405.6 90.1 %collective-permute-start.159 = (f32[2]{0:T(128)S(1)}, f32[2]{0:T(128)S(1)}, u32[]{:S(2)}, u32[]{:S(2)}) collective-permute-start(f32[2]{0:T(128)S(1)} %pad_maximum_fusion.5), channel_id=1, source_target_pairs={{0,25},{1,26},{2,27},{3,28},{4,29},{5,30},{6,31},{7,0},{8,1},{9,2}... | collective-permute-start | bytes 32 | tf_op jit(solution)/shard_map/ppermute | solution.py:22
  1424.7 73.5 %collective-permute-start.160 = (f32[2]{0:T(128)S(1)}, f32[2]{0:T(128)S(1)}, u32[]{:S(2)}, u32[]{:S(2)}) collective-permute-start(f32[2]{0:T(128)S(1)} %pad_maximum_fusion.5), channel_id=1, source_target_pairs={{0,24},{1,25},{2,26},{3,27},{4,28},{5,29},{6,30},{7,31},{8,0},{9,1... | collective-permute-start | bytes 32 | tf_op jit(solution)/shard_map/ppermute | solution.py:22
  1443.8 62.4 %collective-permute-start.161 = (f32[2]{0:T(128)S(1)}, f32[2]{0:T(128)S(1)}, u32[]{:S(2)}, u32[]{:S(2)}) collective-permute-start(f32[2]{0:T(128)S(1)} %pad_maximum_fusion.5), channel_id=1, source_target_pairs={{0,23},{1,24},{2,25},{3,26},{4,27},{5,28},{6,29},{7,30},{8,31},{9,... | collective-permute-start | bytes 32 | tf_op jit(solution)/shard_map/ppermute | solution.py:22
  1462.9 50.3 %collective-permute-start.162 = (f32[2]{0:T(128)S(1)}, f32[2]{0:T(128)S(1)}, u32[]{:S(2)}, u32[]{:S(2)}) collective-permute-start(f32[2]{0:T(128)S(1)} %pad_maximum_fusion.5), channel_id=1, source_target_pairs={{0,22},{1,23},{2,24},{3,25},{4,26},{5,27},{6,28},{7,29},{8,30},{9,... | collective-permute-start | bytes 32 | tf_op jit(solution)/shard_map/ppermute | solution.py:22
  1482.0 38.7 %collective-permute-start.163 = (f32[2]{0:T(128)S(1)}, f32[2]{0:T(128)S(1)}, u32[]{:S(2)}, u32[]{:S(2)}) collective-permute-start(f32[2]{0:T(128)S(1)} %pad_maximum_fusion.5), channel_id=1, source_target_pairs={{0,21},{1,22},{2,23},{3,24},{4,25},{5,26},{6,27},{7,28},{8,29},{9,... | collective-permute-start | bytes 32 | tf_op jit(solution)/shard_map/ppermute | solution.py:22
  1498.2 34.5 %collective-permute-start.165 = (f32[2]{0:T(128)S(1)}, f32[2]{0:T(128)S(1)}, u32[]{:S(2)}, u32[]{:S(2)}) collective-permute-start(f32[2]{0:T(128)S(1)} %pad_maximum_fusion.5), channel_id=1, source_target_pairs={{0,19},{1,20},{2,21},{3,22},{4,23},{5,24},{6,25},{7,26},{8,27},{9,... | collective-permute-start | bytes 32 | tf_op jit(solution)/shard_map/ppermute | solution.py:22
  1513.1 34.7 %collective-permute-start.167 = (f32[2]{0:T(128)S(1)}, f32[2]{0:T(128)S(1)}, u32[]{:S(2)}, u32[]{:S(2)}) collective-permute-start(f32[2]{0:T(128)S(1)} %pad_maximum_fusion.5), channel_id=1, source_target_pairs={{0,17},{1,18},{2,19},{3,20},{4,21},{5,22},{6,23},{7,24},{8,25},{9,... | collective-permute-start | bytes 32 | tf_op jit(solution)/shard_map/ppermute | solution.py:22
  (138 other events, 4443.7 us)

commit v2 on v1

--- a/solution.py
+++ b/solution.py
@@ -25,9 +25,8 @@
 
 
 def ordered_gather(value, axis_name, count):
-    stacked = gather_blocks(value, axis_name, count)
-    index = lax.axis_index(axis_name)
-    return jnp.roll(stacked, index, axis=0)
+    spread = jnp.broadcast_to(value[None], (count,) + value.shape)
+    return lax.all_to_all(spread, axis_name, 0, 0, tiled=True)
 
 
 def reduce_vector(values, axis_name, count):
@@ -35,17 +34,10 @@
 
 
 def reduce_scatter_rows(partial_value, axis_name, count):
-    rows = partial_value.shape[1] // count
-    index = lax.axis_index(axis_name)
-    total = lax.dynamic_slice_in_dim(partial_value, index * rows, rows, 1)
-    for shift in range(1, count):
-        chunk = lax.dynamic_slice_in_dim(
-            partial_value, ((index + shift) % count) * rows, rows, 1
-        )
-        total = total + lax.ppermute(
-            chunk, axis_name, [(i, (i + shift) % count) for i in range(count)]
-        )
-    return total
+    sectors, rows, cols = partial_value.shape
+    chunks = partial_value.reshape((sectors, count, rows // count, cols)).transpose(1, 0, 2, 3)
+    received = lax.all_to_all(chunks, axis_name, 0, 0, tiled=True)
+    return jnp.sum(received, axis=0)
 
 
 def pair_kernel(src_ref, tgt_ref, cnt_ref, s_ref, l_ref, r_ref, o_ref):

time: 1680 us -> 395 us (0.24)
  starting transfers between devices: 1560 us -> 151 us
  blocking collectives: 0 us -> 129 us
  waiting for transfers between devices: 26.3 us -> 49.6 us
    ppermute x137 -> x30, starting transfers between devices: 949 us -> 134 us  [gather_blocks(): lax.ppermute(value, axis_name, [(i, (i - shift) % count) for i in range(c...]
    ppermute x62 -> x0, starting transfers between devices: 613 us -> none  [reduce_scatter_rows(): lax.ppermute(chunk, axis_name, [(i, (i + shift) % count) for i in range(c...]
    all_to_all x0 -> x5, blocking collectives: none -> 129 us  [the longest x4 74.3 us: ordered_gather(): return lax.all_to_all(spread, axis_name, 0, 0, tiled=True)]
    all_to_all x0 -> x2, waiting for transfers between devices: none -> 35.3 us  [the longest x1 28.9 us: reduce_scatter_rows(): received = lax.all_to_all(chunks, axis_name, 0, 0, tiled=True)]
    all_to_all x0 -> x2, starting transfers between devices: none -> 16.9 us  [the longest x1 10.1 us: reduce_scatter_rows(): received = lax.all_to_all(chunks, axis_name, 0, 0, tiled=True)]
  transfers between devices with their start and end apart: 199 -> 32, of which waited for: 11 -> 4; matrix products, arithmetic and copies ran while one was open for 2% -> 6% of each run, Pallas kernels for 0% -> 0%
where the time goes in v2:
time: 395 us; the launch traced here: 393 us
  starting transfers between devices  151 us (38%)
  blocking collectives  129 us (33%)
  waiting for transfers between devices  49.6 us (13%)
  local copies, waits for them, and re-layouts  29.5 us (7%)
  Pallas kernels  13.1 us (3%)
  other arithmetic  11.4 us (3%)
  between operations  9.11 us (2%)
    ppermute x30, starting transfers between devices, gather_blocks(): lax.ppermute(value, axis_name, [(i, (i - shift) % count) for i in range(c...  134 us
    all_to_all x4, blocking collectives, ordered_gather(): return lax.all_to_all(spread, axis_name, 0, 0, tiled=True)  74.3 us
    all_to_all x1, blocking collectives, reduce_scatter_rows(): received = lax.all_to_all(chunks, axis_name, 0, 0, tiled=True)  55 us
    all_to_all x1, waiting for transfers between devices, reduce_scatter_rows(): received = lax.all_to_all(chunks, axis_name, 0, 0, tiled=True)  28.9 us
    unnamed x35, local copies, waits for them, and re-layouts  21 us
    ppermute x30, waiting for transfers between devices, gather_blocks(): lax.ppermute(value, axis_name, [(i, (i - shift) % count) for i in range(c...  14.3 us
    pallas_call x2, Pallas kernels, pair_partial(): pl.pallas_call(pair_kernel, grid_spec=grid_spec, out_shape=jax.ShapeDtype...  13.1 us
    all_to_all x1, starting transfers between devices, reduce_scatter_rows(): received = lax.all_to_all(chunks, axis_name, 0, 0, tiled=True)  10.1 us
  transfers between devices with their start and end apart: 32, of which 4 were waited for; matrix products, arithmetic and copies ran while one was open for 6% of the time, Pallas kernels for 0%

profile of v2, /device:TPU:1, one launch (start us, length us, event | category | flops | bytes accessed | tf_op | source)
XLA Modules:
  0.0 393.0 jit_solution(212110431228071568)
XLA Ops:
  0.6 0.7 dynamic_slice.19
  1.4 0.7 dynamic_slice.18
  2.2 1.1 fusion.17
  3.3 8.7 %collective-permute-start = (bf16[2,256,256]{2,1,0:T(8,128)(2,1)S(1)}, bf16[2,256,256]{2,1,0:T(8,128)(2,1)S(1)}, u32[]{:S(2)}, u32[]{:S(2)}) collective-permute-start(bf16[2,256,256]{2,1,0:T(8,128)(2,1)S(1)} %get-tuple-element.11), channel_id=1, source_target_pairs={{0,480},{32,0},{64,32},{96,64},{128,96},{160,128},{192,160},{224,1... | collective-permute-start | bytes 786440 | tf_op jit(solution)/shard_map/ppermute | solution.py:22
  12.0 1.9 collective-permute-start.1
  14.0 4.8 %collective-permute-start.2 = (bf16[2,256,256]{2,1,0:T(8,128)(2,1)S(1)}, bf16[2,256,256]{2,1,0:T(8,128)(2,1)S(1)}, u32[]{:S(2)}, u32[]{:S(2)}) collective-permute-start(bf16[2,256,256]{2,1,0:T(8,128)(2,1)S(1)} %get-tuple-element.11), channel_id=1, source_target_pairs={{0,416},{32,448},{64,480},{96,0},{128,32},{160,64},{192,96},{224,1... | collective-permute-start | bytes 786440 | tf_op jit(solution)/shard_map/ppermute | solution.py:22
  18.7 2.1 collective-permute-start.3
  20.8 1.9 collective-permute-start.4
  23.5 1.2 fusion.13
  25.3 5.3 %collective-permute-start.5 = (bf16[2,256,256]{2,1,0:T(8,128)(2,1)S(1)}, bf16[2,256,256]{2,1,0:T(8,128)(2,1)S(1)}, u32[]{:S(2)}, u32[]{:S(2)}) collective-permute-start(bf16[2,256,256]{2,1,0:T(8,128)(2,1)S(1)} %get-tuple-element.11), channel_id=1, source_target_pairs={{0,320},{32,352},{64,384},{96,416},{128,448},{160,480},{192,0},{22... | collective-permute-start | bytes 786440 | tf_op jit(solution)/shard_map/ppermute | solution.py:22
  31.3 4.3 %collective-permute-start.6 = (bf16[2,256,256]{2,1,0:T(8,128)(2,1)S(1)}, bf16[2,256,256]{2,1,0:T(8,128)(2,1)S(1)}, u32[]{:S(2)}, u32[]{:S(2)}) collective-permute-start(bf16[2,256,256]{2,1,0:T(8,128)(2,1)S(1)} %get-tuple-element.11), channel_id=1, source_target_pairs={{0,288},{32,320},{64,352},{96,384},{128,416},{160,448},{192,480},{... | collective-permute-start | bytes 786440 | tf_op jit(solution)/shard_map/ppermute | solution.py:22
  36.4 5.6 %collective-permute-start.7 = (bf16[2,256,256]{2,1,0:T(8,128)(2,1)S(1)}, bf16[2,256,256]{2,1,0:T(8,128)(2,1)S(1)}, u32[]{:S(2)}, u32[]{:S(2)}) collective-permute-start(bf16[2,256,256]{2,1,0:T(8,128)(2,1)S(1)} %get-tuple-element.11), channel_id=1, source_target_pairs={{0,256},{32,288},{64,320},{96,352},{128,384},{160,416},{192,448},{... | collective-permute-start | bytes 786440 | tf_op jit(solution)/shard_map/ppermute | solution.py:22
  42.7 1.9 collective-permute-start.8
  45.3 20.6 %collective-permute-start.9 = (bf16[2,256,256]{2,1,0:T(8,128)(2,1)S(1)}, bf16[2,256,256]{2,1,0:T(8,128)(2,1)S(1)}, u32[]{:S(2)}, u32[]{:S(2)}) collective-permute-start(bf16[2,256,256]{2,1,0:T(8,128)(2,1)S(1)} %get-tuple-element.11), channel_id=1, source_target_pairs={{0,192},{32,224},{64,256},{96,288},{128,320},{160,352},{192,384},{... | collective-permute-start | bytes 786440 | tf_op jit(solution)/shard_map/ppermute | solution.py:22
  66.7 1.9 collective-permute-start.10
  69.3 1.9 collective-permute-start.11
  71.2 0.7 bitcast_dynamic-update-slice_fusion.24
  72.0 2.7 collective-permute-start.12
  75.4 4.6 %collective-permute-start.13 = (bf16[2,256,256]{2,1,0:T(8,128)(2,1)S(1)}, bf16[2,256,256]{2,1,0:T(8,128)(2,1)S(1)}, u32[]{:S(2)}, u32[]{:S(2)}) collective-permute-start(bf16[2,256,256]{2,1,0:T(8,128)(2,1)S(1)} %get-tuple-element.11), channel_id=1, source_target_pairs={{0,64},{32,96},{64,128},{96,160},{128,192},{160,224},{192,256},{22... | collective-permute-start | bytes 786440 | tf_op jit(solution)/shard_map/ppermute | solution.py:22
  80.8 3.8 collective-permute-start.14
  85.3 0.7 bitcast_dynamic-update-slice_fusion.20
  86.1 0.7 bitcast_dynamic-update-slice_fusion.19
  86.8 6.8 %collective-permute-done.12 = bf16[2,256,256]{2,1,0:T(8,128)(2,1)S(1)} collective-permute-done((bf16[2,256,256]{2,1,0:T(8,128)(2,1)S(1)}, bf16[2,256,256]{2,1,0:T(8,128)(2,1)S(1)}, u32[]{:S(2)}, u32[]{:S(2)}) %collective-permute-start.12) | collective-permute-done | bytes 262176 | tf_op jit(solution)/shard_map/ppermute | solution.py:22
  93.6 0.7 bitcast_dynamic-update-slice_fusion.18
  95.7 6.6 %shard_map.121 = f32[2,256,256]{2,1,0:T(8,128)} custom-call(s32[16]{0:T(128)} %get-tuple-element.21.src_ref, s32[16]{0:T(128)} %get-tuple-element.22.tgt_ref, s32[1]{0:T(128)S(6)} %copy.76.cnt_ref, bf16[32,256,256]{2,1,0:T(8,128)(2,1)} %bitcast.16.s_ref, bf16[16,256,256]{2,1,0:T(8,128)(2,1)} %l_ref.3, bf16[16,256,256]{2,1,0:T(8,128)(2,1)} %r_ref.3), custom_call_target="tpu_custom_call" | custom-call | tf_op jit(solution)/shard_map/pallas_call | solution.py:89
  102.3 1.1 copy_bitcast_fusion.1
  103.5 55.0 %all_to_all.39 = f32[32,2,8,256]{3,2,1,0:T(8,128)S(1)} all-to-all(f32[32,2,8,256]{3,2,1,0:T(8,128)S(1)} %copy_bitcast_fusion.1), channel_id=1, replica_groups=mesh['sec'=16,'op'=32] {'op'}, dimensions={0} | all-to-all | bytes 1048576 | tf_op jit(solution)/shard_map/all_to_all | solution.py:39
  158.5 34.5 %all_to_all.40 = f32[32,2,8,256]{3,2,1,0:T(8,128)S(1)} all-to-all(f32[32,2,8,256]{3,2,1,0:T(8,128)S(1)} %broadcast_in_dim.21), channel_id=1, replica_groups=mesh['sec'=16,'op'=32] {'op'}, dimensions={0} | all-to-all | bytes 1048576 | tf_op jit(solution)/shard_map/all_to_all | solution.py:29
  193.1 0.9 fusion.2
  194.0 1.3 pad_maximum_fusion
  195.4 11.9 %all_to_all.41 = f32[16,1,2]{2,1,0:T(1,128)S(1)} all-to-all(f32[16,1,2]{2,1,0:T(1,128)S(1)} %broadcast_in_dim.23), channel_id=1, replica_groups=mesh['sec'=16,'op'=32] {'sec'}, dimensions={0} | all-to-all | bytes 256 | tf_op jit(solution)/shard_map/all_to_all | solution.py:29
  209.3 1.0 fusion.6
  210.3 1.3 pad_maximum_fusion.1
  211.7 10.1 %all_to_all.42 = f32[16,1,2]{2,1,0:T(1,128)S(1)} all-to-all(f32[16,1,2]{2,1,0:T(1,128)S(1)} %broadcast_in_dim.24), channel_id=1, replica_groups=mesh['sec'=16,'op'=32] {'sec'}, dimensions={0} | all-to-all | bytes 256 | tf_op jit(solution)/shard_map/all_to_all | solution.py:29
  226.5 0.8 bitcast_dynamic-update-slice_fusion.15
  227.3 2.6 collective-permute-start.15
  229.9 2.8 collective-permute-start.16
  232.7 4.8 %collective-permute-start.17 = (bf16[2,256,256]{2,1,0:T(8,128)(2,1)S(1)}, bf16[2,256,256]{2,1,0:T(8,128)(2,1)S(1)}, u32[]{:S(2)}, u32[]{:S(2)}) collective-permute-start(bf16[2,256,256]{2,1,0:T(8,128)(2,1)S(1)} %get-tuple-element.13), channel_id=1, source_target_pairs={{0,416},{32,448},{64,480},{96,0},{128,32},{160,64},{192,96},{224,1... | collective-permute-start | bytes 786440 | tf_op jit(solution)/shard_map/ppermute | solution.py:22
  237.5 3.1 collective-permute-start.18
  240.6 2.2 collective-permute-start.19
  242.8 5.2 %collective-permute-start.20 = (bf16[2,256,256]{2,1,0:T(8,128)(2,1)S(1)}, bf16[2,256,256]{2,1,0:T(8,128)(2,1)S(1)}, u32[]{:S(2)}, u32[]{:S(2)}) collective-permute-start(bf16[2,256,256]{2,1,0:T(8,128)(2,1)S(1)} %get-tuple-element.13), channel_id=1, source_target_pairs={{0,320},{32,352},{64,384},{96,416},{128,448},{160,480},{192,0},{22... | collective-permute-start | bytes 786440 | tf_op jit(solution)/shard_map/ppermute | solution.py:22
  248.7 6.3 %collective-permute-start.21 = (bf16[2,256,256]{2,1,0:T(8,128)(2,1)S(1)}, bf16[2,256,256]{2,1,0:T(8,128)(2,1)S(1)}, u32[]{:S(2)}, u32[]{:S(2)}) collective-permute-start(bf16[2,256,256]{2,1,0:T(8,128)(2,1)S(1)} %get-tuple-element.13), channel_id=1, source_target_pairs={{0,288},{32,320},{64,352},{96,384},{128,416},{160,448},{192,480},{... | collective-permute-start | bytes 786440 | tf_op jit(solution)/shard_map/ppermute | solution.py:22
  255.8 4.8 %collective-permute-start.22 = (bf16[2,256,256]{2,1,0:T(8,128)(2,1)S(1)}, bf16[2,256,256]{2,1,0:T(8,128)(2,1)S(1)}, u32[]{:S(2)}, u32[]{:S(2)}) collective-permute-start(bf16[2,256,256]{2,1,0:T(8,128)(2,1)S(1)} %get-tuple-element.13), channel_id=1, source_target_pairs={{0,256},{32,288},{64,320},{96,352},{128,384},{160,416},{192,448},{... | collective-permute-start | bytes 786440 | tf_op jit(solution)/shard_map/ppermute | solution.py:22
  261.4 1.9 collective-permute-start.23
  264.0 11.9 %collective-permute-start.24 = (bf16[2,256,256]{2,1,0:T(8,128)(2,1)S(1)}, bf16[2,256,256]{2,1,0:T(8,128)(2,1)S(1)}, u32[]{:S(2)}, u32[]{:S(2)}) collective-permute-start(bf16[2,256,256]{2,1,0:T(8,128)(2,1)S(1)} %get-tuple-element.13), channel_id=1, source_target_pairs={{0,192},{32,224},{64,256},{96,288},{128,320},{160,352},{192,384},{... | collective-permute-start | bytes 786440 | tf_op jit(solution)/shard_map/ppermute | solution.py:22
  276.7 2.2 collective-permute-start.25
  279.6 3.6 collective-permute-start.26
  283.3 0.7 bitcast_dynamic-update-slice_fusion.8
  284.0 2.2 collective-permute-start.27
  286.9 3.1 collective-permute-start.28
  290.8 5.1 %collective-permute-start.29 = (bf16[2,256,256]{2,1,0:T(8,128)(2,1)S(1)}, bf16[2,256,256]{2,1,0:T(8,128)(2,1)S(1)}, u32[]{:S(2)}, u32[]{:S(2)}) collective-permute-start(bf16[2,256,256]{2,1,0:T(8,128)(2,1)S(1)} %get-tuple-element.13), channel_id=1, source_target_pairs={{0,32},{32,64},{64,96},{96,128},{128,160},{160,192},{192,224},{224... | collective-permute-start | bytes 786440 | tf_op jit(solution)/shard_map/ppermute | solution.py:22
  296.7 0.7 bitcast_dynamic-update-slice_fusion.4
  297.4 0.7 bitcast_dynamic-update-slice_fusion.3
  298.1 7.5 %collective-permute-done.27 = bf16[2,256,256]{2,1,0:T(8,128)(2,1)S(1)} collective-permute-done((bf16[2,256,256]{2,1,0:T(8,128)(2,1)S(1)}, bf16[2,256,256]{2,1,0:T(8,128)(2,1)S(1)}, u32[]{:S(2)}, u32[]{:S(2)}) %collective-permute-start.27) | collective-permute-done | bytes 262176 | tf_op jit(solution)/shard_map/ppermute | solution.py:22
  305.6 0.7 bitcast_dynamic-update-slice_fusion.2
  307.8 6.6 %shard_map.122 = f32[2,256,256]{2,1,0:T(8,128)} custom-call(s32[16]{0:T(128)} %get-tuple-element.21.src_ref, s32[16]{0:T(128)} %get-tuple-element.22.tgt_ref, s32[1]{0:T(128)S(6)} %copy.76.cnt_ref, bf16[32,256,256]{2,1,0:T(8,128)(2,1)} %bitcast.45.s_ref, bf16[16,256,256]{2,1,0:T(8,128)(2,1)} %l_ref.3, bf16[16,256,256]{2,1,0:T(8,128)(2,1)} %r_ref.3), custom_call_target="tpu_custom_call" | custom-call | tf_op jit(solution)/shard_map/pallas_call | solution.py:89
  314.4 1.9 copy_bitcast_fusion
  316.3 10.1 %all-to-all-start.4 = ((f32[32,2,8,256]{3,2,1,0:T(8,128)}), f32[32,2,8,256]{3,2,1,0:T(8,128)S(1)}, u32[]{:S(2)}, u32[]{:S(2)}) async-start(f32[32,2,8,256]{3,2,1,0:T(8,128)} %copy_bitcast_fusion), calls=%async_computation.4 | async-start | bytes 1048576 | tf_op jit(solution)/shard_map/all_to_all | solution.py:39
  326.5 28.9 %all-to-all-done.4 = f32[32,2,8,256]{3,2,1,0:T(8,128)S(1)} async-done(((f32[32,2,8,256]{3,2,1,0:T(8,128)}), f32[32,2,8,256]{3,2,1,0:T(8,128)S(1)}, u32[]{:S(2)}, u32[]{:S(2)}) %all-to-all-start.4) | async-done | bytes 524320 | tf_op jit(solution)/shard_map/all_to_all | solution.py:39
  355.5 1.3 multiply_reduce_fusion.1
  356.8 1.3 pad_maximum_fusion.2
  358.2 17.7 %all_to_all.43 = f32[32,1,2]{2,1,0:T(1,128)S(1)} all-to-all(f32[32,1,2]{2,1,0:T(1,128)S(1)} %broadcast_in_dim.26), channel_id=1, replica_groups=mesh['sec'=16,'op'=32] {'op'}, dimensions={0} | all-to-all | bytes 512 | tf_op jit(solution)/shard_map/all_to_all | solution.py:29
  376.5 6.8 %all-to-all-start.6 = ((f32[16,1,2]{2,1,0:T(1,128)}), f32[16,1,2]{2,1,0:T(1,128)S(1)}, u32[]{:S(2)}, u32[]{:S(2)}) async-start(f32[16,1,2]{2,1,0:T(1,128)} %broadcast_in_dim.27), calls=%async_computation.6 | async-start | bytes 16384 | tf_op jit(solution)/shard_map/all_to_all | solution.py:29
  384.1 6.3 %all-to-all-done.6 = f32[16,1,2]{2,1,0:T(1,128)S(1)} async-done(((f32[16,1,2]{2,1,0:T(1,128)}), f32[16,1,2]{2,1,0:T(1,128)S(1)}, u32[]{:S(2)}, u32[]{:S(2)}) %all-to-all-start.6) | async-done | bytes 160 | tf_op jit(solution)/shard_map/all_to_all | solution.py:29
  (75 shorter events, 20.3 us)
Async XLA Ops:
  3.3 22.1 %collective-permute-start = (bf16[2,256,256]{2,1,0:T(8,128)(2,1)S(1)}, bf16[2,256,256]{2,1,0:T(8,128)(2,1)S(1)}, u32[]{:S(2)}, u32[]{:S(2)}) collective-permute-start(bf16[2,256,256]{2,1,0:T(8,128)(2,1)S(1)} %get-tuple-element.11), channel_id=1, source_target_pairs={{0,480},{32,0},{64,32},{96,64},{128,96},{160,128},{192,160},{224,1... | collective-permute-start | bytes 786440 | tf_op jit(solution)/shard_map/ppermute | solution.py:22
  12.0 19.3 %collective-permute-start.1 = (bf16[2,256,256]{2,1,0:T(8,128)(2,1)S(1)}, bf16[2,256,256]{2,1,0:T(8,128)(2,1)S(1)}, u32[]{:S(2)}, u32[]{:S(2)}) collective-permute-start(bf16[2,256,256]{2,1,0:T(8,128)(2,1)S(1)} %get-tuple-element.11), channel_id=1, source_target_pairs={{0,448},{32,480},{64,0},{96,32},{128,64},{160,96},{192,128},{224,1... | collective-permute-start | bytes 786440 | tf_op jit(solution)/shard_map/ppermute | solution.py:22
  14.0 22.4 %collective-permute-start.2 = (bf16[2,256,256]{2,1,0:T(8,128)(2,1)S(1)}, bf16[2,256,256]{2,1,0:T(8,128)(2,1)S(1)}, u32[]{:S(2)}, u32[]{:S(2)}) collective-permute-start(bf16[2,256,256]{2,1,0:T(8,128)(2,1)S(1)} %get-tuple-element.11), channel_id=1, source_target_pairs={{0,416},{32,448},{64,480},{96,0},{128,32},{160,64},{192,96},{224,1... | collective-permute-start | bytes 786440 | tf_op jit(solution)/shard_map/ppermute | solution.py:22
  18.7 23.9 %collective-permute-start.3 = (bf16[2,256,256]{2,1,0:T(8,128)(2,1)S(1)}, bf16[2,256,256]{2,1,0:T(8,128)(2,1)S(1)}, u32[]{:S(2)}, u32[]{:S(2)}) collective-permute-start(bf16[2,256,256]{2,1,0:T(8,128)(2,1)S(1)} %get-tuple-element.11), channel_id=1, source_target_pairs={{0,384},{32,416},{64,448},{96,480},{128,0},{160,32},{192,64},{224,... | collective-permute-start | bytes 786440 | tf_op jit(solution)/shard_map/ppermute | solution.py:22
  20.8 24.5 %collective-permute-start.4 = (bf16[2,256,256]{2,1,0:T(8,128)(2,1)S(1)}, bf16[2,256,256]{2,1,0:T(8,128)(2,1)S(1)}, u32[]{:S(2)}, u32[]{:S(2)}) collective-permute-start(bf16[2,256,256]{2,1,0:T(8,128)(2,1)S(1)} %get-tuple-element.11), channel_id=1, source_target_pairs={{0,352},{32,384},{64,416},{96,448},{128,480},{160,0},{192,32},{224... | collective-permute-start | bytes 786440 | tf_op jit(solution)/shard_map/ppermute | solution.py:22
  25.3 41.3 %collective-permute-start.5 = (bf16[2,256,256]{2,1,0:T(8,128)(2,1)S(1)}, bf16[2,256,256]{2,1,0:T(8,128)(2,1)S(1)}, u32[]{:S(2)}, u32[]{:S(2)}) collective-permute-start(bf16[2,256,256]{2,1,0:T(8,128)(2,1)S(1)} %get-tuple-element.11), channel_id=1, source_target_pairs={{0,320},{32,352},{64,384},{96,416},{128,448},{160,480},{192,0},{22... | collective-permute-start | bytes 786440 | tf_op jit(solution)/shard_map/ppermute | solution.py:22
  31.3 38.0 %collective-permute-start.6 = (bf16[2,256,256]{2,1,0:T(8,128)(2,1)S(1)}, bf16[2,256,256]{2,1,0:T(8,128)(2,1)S(1)}, u32[]{:S(2)}, u32[]{:S(2)}) collective-permute-start(bf16[2,256,256]{2,1,0:T(8,128)(2,1)S(1)} %get-tuple-element.11), channel_id=1, source_target_pairs={{0,288},{32,320},{64,352},{96,384},{128,416},{160,448},{192,480},{... | collective-permute-start | bytes 786440 | tf_op jit(solution)/shard_map/ppermute | solution.py:22
  36.4 35.6 %collective-permute-start.7 = (bf16[2,256,256]{2,1,0:T(8,128)(2,1)S(1)}, bf16[2,256,256]{2,1,0:T(8,128)(2,1)S(1)}, u32[]{:S(2)}, u32[]{:S(2)}) collective-permute-start(bf16[2,256,256]{2,1,0:T(8,128)(2,1)S(1)} %get-tuple-element.11), channel_id=1, source_target_pairs={{0,256},{32,288},{64,320},{96,352},{128,384},{160,416},{192,448},{... | collective-permute-start | bytes 786440 | tf_op jit(solution)/shard_map/ppermute | solution.py:22
  42.7 32.8 %collective-permute-start.8 = (bf16[2,256,256]{2,1,0:T(8,128)(2,1)S(1)}, bf16[2,256,256]{2,1,0:T(8,128)(2,1)S(1)}, u32[]{:S(2)}, u32[]{:S(2)}) collective-permute-start(bf16[2,256,256]{2,1,0:T(8,128)(2,1)S(1)} %get-tuple-element.11), channel_id=1, source_target_pairs={{0,224},{32,256},{64,288},{96,320},{128,352},{160,384},{192,416},{... | collective-permute-start | bytes 786440 | tf_op jit(solution)/shard_map/ppermute | solution.py:22
  45.3 35.5 %collective-permute-start.9 = (bf16[2,256,256]{2,1,0:T(8,128)(2,1)S(1)}, bf16[2,256,256]{2,1,0:T(8,128)(2,1)S(1)}, u32[]{:S(2)}, u32[]{:S(2)}) collective-permute-start(bf16[2,256,256]{2,1,0:T(8,128)(2,1)S(1)} %get-tuple-element.11), channel_id=1, source_target_pairs={{0,192},{32,224},{64,256},{96,288},{128,320},{160,352},{192,384},{... | collective-permute-start | bytes 786440 | tf_op jit(solution)/shard_map/ppermute | solution.py:22
  66.7 18.7 %collective-permute-start.10 = (bf16[2,256,256]{2,1,0:T(8,128)(2,1)S(1)}, bf16[2,256,256]{2,1,0:T(8,128)(2,1)S(1)}, u32[]{:S(2)}, u32[]{:S(2)}) collective-permute-start(bf16[2,256,256]{2,1,0:T(8,128)(2,1)S(1)} %get-tuple-element.11), channel_id=1, source_target_pairs={{0,160},{32,192},{64,224},{96,256},{128,288},{160,320},{192,352},{... | collective-permute-start | bytes 786440 | tf_op jit(solution)/shard_map/ppermute | solution.py:22
  69.3 16.8 %collective-permute-start.11 = (bf16[2,256,256]{2,1,0:T(8,128)(2,1)S(1)}, bf16[2,256,256]{2,1,0:T(8,128)(2,1)S(1)}, u32[]{:S(2)}, u32[]{:S(2)}) collective-permute-start(bf16[2,256,256]{2,1,0:T(8,128)(2,1)S(1)} %get-tuple-element.11), channel_id=1, source_target_pairs={{0,128},{32,160},{64,192},{96,224},{128,256},{160,288},{192,320},{... | collective-permute-start | bytes 786440 | tf_op jit(solution)/shard_map/ppermute | solution.py:22
  72.0 21.6 %collective-permute-start.12 = (bf16[2,256,256]{2,1,0:T(8,128)(2,1)S(1)}, bf16[2,256,256]{2,1,0:T(8,128)(2,1)S(1)}, u32[]{:S(2)}, u32[]{:S(2)}) collective-permute-start(bf16[2,256,256]{2,1,0:T(8,128)(2,1)S(1)} %get-tuple-element.11), channel_id=1, source_target_pairs={{0,96},{32,128},{64,160},{96,192},{128,224},{160,256},{192,288},{2... | collective-permute-start | bytes 786440 | tf_op jit(solution)/shard_map/ppermute | solution.py:22
  75.4 18.9 %collective-permute-start.13 = (bf16[2,256,256]{2,1,0:T(8,128)(2,1)S(1)}, bf16[2,256,256]{2,1,0:T(8,128)(2,1)S(1)}, u32[]{:S(2)}, u32[]{:S(2)}) collective-permute-start(bf16[2,256,256]{2,1,0:T(8,128)(2,1)S(1)} %get-tuple-element.11), channel_id=1, source_target_pairs={{0,64},{32,96},{64,128},{96,160},{128,192},{160,224},{192,256},{22... | collective-permute-start | bytes 786440 | tf_op jit(solution)/shard_map/ppermute | solution.py:22
  80.8 14.3 %collective-permute-start.14 = (bf16[2,256,256]{2,1,0:T(8,128)(2,1)S(1)}, bf16[2,256,256]{2,1,0:T(8,128)(2,1)S(1)}, u32[]{:S(2)}, u32[]{:S(2)}) collective-permute-start(bf16[2,256,256]{2,1,0:T(8,128)(2,1)S(1)} %get-tuple-element.11), channel_id=1, source_target_pairs={{0,32},{32,64},{64,96},{96,128},{128,160},{160,192},{192,224},{224... | collective-permute-start | bytes 786440 | tf_op jit(solution)/shard_map/ppermute | solution.py:22
  102.3 90.7 %copy-start = (bf16[2,256,256]{2,1,0:T(8,128)(2,1)S(1)}, bf16[2,256,256]{2,1,0:T(8,128)(2,1)}, u32[]{:S(2)}) copy-start(bf16[2,256,256]{2,1,0:T(8,128)(2,1)} %param.11) | copy-start | bytes 786436
  102.3 107.0 %copy-start.2 = (bf16[2,256,256]{2,1,0:T(8,128)(2,1)S(1)}, bf16[2,256,256]{2,1,0:T(8,128)(2,1)}, u32[]{:S(2)}) copy-start(bf16[2,256,256]{2,1,0:T(8,128)(2,1)} %param.12) | copy-start | bytes 786436
  227.3 128.2 %copy-start.1 = (bf16[2,256,256]{2,1,0:T(8,128)(2,1)}, bf16[2,256,256]{2,1,0:T(8,128)(2,1)S(1)}, u32[]{:S(2)}) copy-start(bf16[2,256,256]{2,1,0:T(8,128)(2,1)S(1)} %get-tuple-element.13) | copy-start | bytes 786436
  227.3 15.5 %collective-permute-start.15 = (bf16[2,256,256]{2,1,0:T(8,128)(2,1)S(1)}, bf16[2,256,256]{2,1,0:T(8,128)(2,1)S(1)}, u32[]{:S(2)}, u32[]{:S(2)}) collective-permute-start(bf16[2,256,256]{2,1,0:T(8,128)(2,1)S(1)} %get-tuple-element.13), channel_id=1, source_target_pairs={{0,480},{32,0},{64,32},{96,64},{128,96},{160,128},{192,160},{224,1... | collective-permute-start | bytes 786440 | tf_op jit(solution)/shard_map/ppermute | solution.py:22
  229.9 18.8 %collective-permute-start.16 = (bf16[2,256,256]{2,1,0:T(8,128)(2,1)S(1)}, bf16[2,256,256]{2,1,0:T(8,128)(2,1)S(1)}, u32[]{:S(2)}, u32[]{:S(2)}) collective-permute-start(bf16[2,256,256]{2,1,0:T(8,128)(2,1)S(1)} %get-tuple-element.13), channel_id=1, source_target_pairs={{0,448},{32,480},{64,0},{96,32},{128,64},{160,96},{192,128},{224,1... | collective-permute-start | bytes 786440 | tf_op jit(solution)/shard_map/ppermute | solution.py:22
  232.7 23.1 %collective-permute-start.17 = (bf16[2,256,256]{2,1,0:T(8,128)(2,1)S(1)}, bf16[2,256,256]{2,1,0:T(8,128)(2,1)S(1)}, u32[]{:S(2)}, u32[]{:S(2)}) collective-permute-start(bf16[2,256,256]{2,1,0:T(8,128)(2,1)S(1)} %get-tuple-element.13), channel_id=1, source_target_pairs={{0,416},{32,448},{64,480},{96,0},{128,32},{160,64},{192,96},{224,1... | collective-permute-start | bytes 786440 | tf_op jit(solution)/shard_map/ppermute | solution.py:22
  237.5 23.9 %collective-permute-start.18 = (bf16[2,256,256]{2,1,0:T(8,128)(2,1)S(1)}, bf16[2,256,256]{2,1,0:T(8,128)(2,1)S(1)}, u32[]{:S(2)}, u32[]{:S(2)}) collective-permute-start(bf16[2,256,256]{2,1,0:T(8,128)(2,1)S(1)} %get-tuple-element.13), channel_id=1, source_target_pairs={{0,384},{32,416},{64,448},{96,480},{128,0},{160,32},{192,64},{224,... | collective-permute-start | bytes 786440 | tf_op jit(solution)/shard_map/ppermute | solution.py:22
  240.6 23.4 %collective-permute-start.19 = (bf16[2,256,256]{2,1,0:T(8,128)(2,1)S(1)}, bf16[2,256,256]{2,1,0:T(8,128)(2,1)S(1)}, u32[]{:S(2)}, u32[]{:S(2)}) collective-permute-start(bf16[2,256,256]{2,1,0:T(8,128)(2,1)S(1)} %get-tuple-element.13), channel_id=1, source_target_pairs={{0,352},{32,384},{64,416},{96,448},{128,480},{160,0},{192,32},{224... | collective-permute-start | bytes 786440 | tf_op jit(solution)/shard_map/ppermute | solution.py:22
  242.8 33.9 %collective-permute-start.20 = (bf16[2,256,256]{2,1,0:T(8,128)(2,1)S(1)}, bf16[2,256,256]{2,1,0:T(8,128)(2,1)S(1)}, u32[]{:S(2)}, u32[]{:S(2)}) collective-permute-start(bf16[2,256,256]{2,1,0:T(8,128)(2,1)S(1)} %get-tuple-element.13), channel_id=1, source_target_pairs={{0,320},{32,352},{64,384},{96,416},{128,448},{160,480},{192,0},{22... | collective-permute-start | bytes 786440 | tf_op jit(solution)/shard_map/ppermute | solution.py:22
  248.7 30.9 %collective-permute-start.21 = (bf16[2,256,256]{2,1,0:T(8,128)(2,1)S(1)}, bf16[2,256,256]{2,1,0:T(8,128)(2,1)S(1)}, u32[]{:S(2)}, u32[]{:S(2)}) collective-permute-start(bf16[2,256,256]{2,1,0:T(8,128)(2,1)S(1)} %get-tuple-element.13), channel_id=1, source_target_pairs={{0,288},{32,320},{64,352},{96,384},{128,416},{160,448},{192,480},{... | collective-permute-start | bytes 786440 | tf_op jit(solution)/shard_map/ppermute | solution.py:22
  255.8 28.2 %collective-permute-start.22 = (bf16[2,256,256]{2,1,0:T(8,128)(2,1)S(1)}, bf16[2,256,256]{2,1,0:T(8,128)(2,1)S(1)}, u32[]{:S(2)}, u32[]{:S(2)}) collective-permute-start(bf16[2,256,256]{2,1,0:T(8,128)(2,1)S(1)} %get-tuple-element.13), channel_id=1, source_target_pairs={{0,256},{32,288},{64,320},{96,352},{128,384},{160,416},{192,448},{... | collective-permute-start | bytes 786440 | tf_op jit(solution)/shard_map/ppermute | solution.py:22
  261.4 25.6 %collective-permute-start.23 = (bf16[2,256,256]{2,1,0:T(8,128)(2,1)S(1)}, bf16[2,256,256]{2,1,0:T(8,128)(2,1)S(1)}, u32[]{:S(2)}, u32[]{:S(2)}) collective-permute-start(bf16[2,256,256]{2,1,0:T(8,128)(2,1)S(1)} %get-tuple-element.13), channel_id=1, source_target_pairs={{0,224},{32,256},{64,288},{96,320},{128,352},{160,384},{192,416},{... | collective-permute-start | bytes 786440 | tf_op jit(solution)/shard_map/ppermute | solution.py:22
  264.0 26.8 %collective-permute-start.24 = (bf16[2,256,256]{2,1,0:T(8,128)(2,1)S(1)}, bf16[2,256,256]{2,1,0:T(8,128)(2,1)S(1)}, u32[]{:S(2)}, u32[]{:S(2)}) collective-permute-start(bf16[2,256,256]{2,1,0:T(8,128)(2,1)S(1)} %get-tuple-element.13), channel_id=1, source_target_pairs={{0,192},{32,224},{64,256},{96,288},{128,320},{160,352},{192,384},{... | collective-permute-start | bytes 786440 | tf_op jit(solution)/shard_map/ppermute | solution.py:22
  276.7 20.0 %collective-permute-start.25 = (bf16[2,256,256]{2,1,0:T(8,128)(2,1)S(1)}, bf16[2,256,256]{2,1,0:T(8,128)(2,1)S(1)}, u32[]{:S(2)}, u32[]{:S(2)}) collective-permute-start(bf16[2,256,256]{2,1,0:T(8,128)(2,1)S(1)} %get-tuple-element.13), channel_id=1, source_target_pairs={{0,160},{32,192},{64,224},{96,256},{128,288},{160,320},{192,352},{... | collective-permute-start | bytes 786440 | tf_op jit(solution)/shard_map/ppermute | solution.py:22
  279.6 17.8 %collective-permute-start.26 = (bf16[2,256,256]{2,1,0:T(8,128)(2,1)S(1)}, bf16[2,256,256]{2,1,0:T(8,128)(2,1)S(1)}, u32[]{:S(2)}, u32[]{:S(2)}) collective-permute-start(bf16[2,256,256]{2,1,0:T(8,128)(2,1)S(1)} %get-tuple-element.13), channel_id=1, source_target_pairs={{0,128},{32,160},{64,192},{96,224},{128,256},{160,288},{192,320},{... | collective-permute-start | bytes 786440 | tf_op jit(solution)/shard_map/ppermute | solution.py:22
  284.0 21.6 %collective-permute-start.27 = (bf16[2,256,256]{2,1,0:T(8,128)(2,1)S(1)}, bf16[2,256,256]{2,1,0:T(8,128)(2,1)S(1)}, u32[]{:S(2)}, u32[]{:S(2)}) collective-permute-start(bf16[2,256,256]{2,1,0:T(8,128)(2,1)S(1)} %get-tuple-element.13), channel_id=1, source_target_pairs={{0,96},{32,128},{64,160},{96,192},{128,224},{160,256},{192,288},{2... | collective-permute-start | bytes 786440 | tf_op jit(solution)/shard_map/ppermute | solution.py:22
  286.9 19.4 %collective-permute-start.28 = (bf16[2,256,256]{2,1,0:T(8,128)(2,1)S(1)}, bf16[2,256,256]{2,1,0:T(8,128)(2,1)S(1)}, u32[]{:S(2)}, u32[]{:S(2)}) collective-permute-start(bf16[2,256,256]{2,1,0:T(8,128)(2,1)S(1)} %get-tuple-element.13), channel_id=1, source_target_pairs={{0,64},{32,96},{64,128},{96,160},{128,192},{160,224},{192,256},{22... | collective-permute-start | bytes 786440 | tf_op jit(solution)/shard_map/ppermute | solution.py:22
  290.8 16.3 %collective-permute-start.29 = (bf16[2,256,256]{2,1,0:T(8,128)(2,1)S(1)}, bf16[2,256,256]{2,1,0:T(8,128)(2,1)S(1)}, u32[]{:S(2)}, u32[]{:S(2)}) collective-permute-start(bf16[2,256,256]{2,1,0:T(8,128)(2,1)S(1)} %get-tuple-element.13), channel_id=1, source_target_pairs={{0,32},{32,64},{64,96},{96,128},{128,160},{160,192},{192,224},{224... | collective-permute-start | bytes 786440 | tf_op jit(solution)/shard_map/ppermute | solution.py:22
  316.3 39.2 %all-to-all-start.4 = ((f32[32,2,8,256]{3,2,1,0:T(8,128)}), f32[32,2,8,256]{3,2,1,0:T(8,128)S(1)}, u32[]{:S(2)}, u32[]{:S(2)}) async-start(f32[32,2,8,256]{3,2,1,0:T(8,128)} %copy_bitcast_fusion), calls=%async_computation.4 | async-start | bytes 1048576 | tf_op jit(solution)/shard_map/all_to_all | solution.py:39
  376.5 13.9 %all-to-all-start.6 = ((f32[16,1,2]{2,1,0:T(1,128)}), f32[16,1,2]{2,1,0:T(1,128)S(1)}, u32[]{:S(2)}, u32[]{:S(2)}) async-start(f32[16,1,2]{2,1,0:T(1,128)} %broadcast_in_dim.27), calls=%async_computation.6 | async-start | bytes 16384 | tf_op jit(solution)/shard_map/all_to_all | solution.py:29

commit v3 on v2

--- a/solution.py
+++ b/solution.py
@@ -5,7 +5,7 @@
 from jax import lax
 from jax.experimental import pallas as pl
 from jax.experimental.pallas import tpu as pltpu
-from jax.sharding import PartitionSpec as P
+from jax.sharding import Mesh, PartitionSpec as P
 
 
 def block_mask(left_dims, right_dims, block_size):
@@ -15,13 +15,14 @@
     )
 
 
-def gather_blocks(value, axis_name, count):
-    parts = [value]
-    for shift in range(1, count):
-        parts.append(
-            lax.ppermute(value, axis_name, [(i, (i - shift) % count) for i in range(count)])
-        )
-    return jnp.stack(parts, 0)
+SEC = ("chip", "core")
+
+
+def gather_sec(value, chips):
+    spread = jnp.broadcast_to(value[None], (chips,) + value.shape)
+    same_core = lax.all_to_all(spread, "chip", 0, 0, tiled=True)
+    other_core = lax.ppermute(same_core, "core", [(0, 1), (1, 0)])
+    return jnp.concatenate([same_core, other_core], 0)
 
 
 def ordered_gather(value, axis_name, count):
@@ -108,10 +109,12 @@
 ):
     sector_count = wavefunction.shape[0]
     block_size = wavefunction.shape[1]
-    n_sec = lax.axis_size("sec")
+    n_chip = lax.axis_size("chip")
+    n_sec = n_chip * lax.axis_size("core")
     n_op = lax.axis_size("op")
     share_rows = block_size // n_op
-    sec_index = lax.axis_index("sec")
+    sec_index = lax.axis_index(SEC)
+    core_index = lax.axis_index("core")
     op_index = lax.axis_index("op")
     first_sector = sec_index * sector_count
     row_start = op_index * share_rows
@@ -127,12 +130,14 @@
     vector_view = own_vector.astype(jnp.float32)
 
     owner = slot_source_sector // sector_count
-    source_index = ((owner - sec_index) % n_sec) * sector_count + slot_source_sector % sector_count
+    owner_core = owner % 2
+    position = (owner_core != core_index).astype(jnp.int32) * n_chip + owner // 2
+    source_index = position * sector_count + slot_source_sector % sector_count
     target_index = jnp.clip(slot_target_sector, 0, sector_count - 1)
     live_count = pair_count
 
     def apply_partial(field):
-        sources = gather_blocks(field, "sec", n_sec).reshape(
+        sources = gather_sec(field, n_chip).reshape(
             (n_sec * sector_count, block_size, block_size)
         )
         partial_value = pair_partial(
@@ -155,14 +160,14 @@
     sigma_first = jnp.where(own_mask, diag_view * vector_view + pairs_first, 0.0)
     norm_vector, correlation = reduce_vector(
         jnp.stack([jnp.sum(vector_view * vector_view), jnp.sum(vector_view * sigma_first)]),
-        "sec",
+        SEC,
         n_sec,
     )
     rayleigh = correlation / norm_vector
     residual = sigma_first - rayleigh * vector_view
     scaled = scale_view * residual
     along_vector, scaled_square = reduce_vector(
-        jnp.stack([jnp.sum(vector_view * scaled), jnp.sum(scaled * scaled)]), "sec", n_sec
+        jnp.stack([jnp.sum(vector_view * scaled), jnp.sum(scaled * scaled)]), SEC, n_sec
     )
     orthogonal = scaled - along_vector / norm_vector * vector_view
     square_norm = scaled_square - along_vector * along_vector / norm_vector
@@ -177,7 +182,7 @@
     local_terms = jnp.stack(
         [jnp.sum(vector_rows * product_rows), jnp.sum(corr_rows * product_rows)]
     )
-    cross_term, self_term = reduce_vector(reduce_vector(local_terms, "op", n_op), "sec", n_sec)
+    cross_term, self_term = reduce_vector(reduce_vector(local_terms, "op", n_op), SEC, n_sec)
     projected = jnp.stack(
         [rayleigh, cross_term * lax.rsqrt(norm_vector * entries), self_term / entries]
     )
@@ -185,19 +190,21 @@
 
 
 def solution(mesh):
+    n_sec, n_op = mesh.devices.shape
+    mesh = Mesh(mesh.devices.reshape((n_sec // 2, 2, n_op)), ("chip", "core", "op"))
     in_specs = (
-        P("sec", None, None),
-        P("sec", None, None),
-        P("sec", None, None),
-        P(("sec", "op"), None, None),
-        P(("sec", "op"), None, None),
-        P(("sec", "op")),
-        P(("sec", "op")),
-        P(("sec", "op")),
+        P(SEC, None, None),
+        P(SEC, None, None),
+        P(SEC, None, None),
+        P(("chip", "core", "op"), None, None),
+        P(("chip", "core", "op"), None, None),
+        P(("chip", "core", "op")),
+        P(("chip", "core", "op")),
+        P(("chip", "core", "op")),
         P(),
         P(),
     )
-    out_specs = (P("sec", None, None), P("sec", "op", None), P())
+    out_specs = (P(SEC, None, None), P(SEC, "op", None), P())
     return jax.shard_map(
         on_device, mesh=mesh, in_specs=in_specs, out_specs=out_specs, check_vma=False
     )

time: 395 us -> 304 us (0.77)
  starting transfers between devices: 151 us -> 25.2 us
  blocking collectives: 129 us -> 190 us
  local copies, waits for them, and re-layouts: 29.5 us -> 7.51 us
  waiting for transfers between devices: 49.6 us -> 45 us
    ppermute x30 -> x2, starting transfers between devices: 134 us -> 8.78 us  [gather_sec(): other_core = lax.ppermute(same_core, 'core', [(0, 1), (1, 0)])]
    all_to_all x0 -> x2, blocking collectives: none -> 63.5 us  [gather_sec(): same_core = lax.all_to_all(spread, 'chip', 0, 0, tiled=True)]
    unnamed x35 -> x10, local copies, waits for them, and re-layouts: 21 us -> 0.03 us
    ppermute x30 -> x2, waiting for transfers between devices: 14.3 us -> 6.33 us  [gather_sec(): other_core = lax.ppermute(same_core, 'core', [(0, 1), (1, 0)])]
    concatenate x0 -> x2, other arithmetic: none -> 4.57 us  [gather_sec(): return jnp.concatenate([same_core, other_core], 0)]
  transfers between devices with their start and end apart: 32 -> 4, of which waited for: 4 -> 4; matrix products, arithmetic and copies ran while one was open for 6% -> 0% of each run, Pallas kernels for 0% -> 0%
where the time goes in v3:
time: 304 us; the launch traced here: 303 us
  blocking collectives  190 us (62%)
  waiting for transfers between devices  45 us (15%)
  starting transfers between devices  25.2 us (8%)
  other arithmetic  14.9 us (5%)
  Pallas kernels  11.3 us (4%)
  between operations  8.83 us (3%)
  local copies, waits for them, and re-layouts  7.51 us (2%)
    all_to_all x4, blocking collectives, ordered_gather(): return lax.all_to_all(spread, axis_name, 0, 0, tiled=True)  74.7 us
    all_to_all x2, blocking collectives, gather_sec(): same_core = lax.all_to_all(spread, 'chip', 0, 0, tiled=True)  63.5 us
    all_to_all x1, blocking collectives, reduce_scatter_rows(): received = lax.all_to_all(chunks, axis_name, 0, 0, tiled=True)  51.9 us
    all_to_all x1, waiting for transfers between devices, reduce_scatter_rows(): received = lax.all_to_all(chunks, axis_name, 0, 0, tiled=True)  32.3 us
    pallas_call x2, Pallas kernels, pair_partial(): pl.pallas_call(pair_kernel, grid_spec=grid_spec, out_shape=jax.ShapeDtype...  11.3 us
    all_to_all x1, starting transfers between devices, reduce_scatter_rows(): received = lax.all_to_all(chunks, axis_name, 0, 0, tiled=True)  10.5 us
    ppermute x2, starting transfers between devices, gather_sec(): other_core = lax.ppermute(same_core, 'core', [(0, 1), (1, 0)])  8.78 us
    all_to_all x1, waiting for transfers between devices, ordered_gather(): return lax.all_to_all(spread, axis_name, 0, 0, tiled=True)  6.33 us
  transfers between devices with their start and end apart: 4, of which 4 were waited for; matrix products, arithmetic and copies ran while one was open for 0% of the time, Pallas kernels for 0%

profile of v3, /device:TPU:1, one launch (start us, length us, event | category | flops | bytes accessed | tf_op | source)
XLA Modules:
  0.0 302.7 jit_solution(5829723782014204858)
XLA Ops:
  0.6 0.7 dynamic_slice.19
  1.4 0.7 dynamic_slice.18
  2.1 0.1 iota_compare_fusion
  2.2 1.1 fusion.16
  3.3 0.2 broadcast_in_dim.24
  3.5 0.0 copy-start.3
  3.5 0.0 copy-start.4
  3.5 33.5 %all_to_all.49 = bf16[8,2,256,256]{3,2,1,0:T(8,128)(2,1)S(1)} all-to-all(bf16[8,2,256,256]{3,2,1,0:T(8,128)(2,1)S(1)} %broadcast_in_dim.24), channel_id=1, replica_groups=mesh['chip'=8,'core'=2,'op'=32] {'chip'}, dimensions={0} | all-to-all | bytes 4194304 | tf_op jit(solution)/shard_map/all_to_all | solution.py:23
  37.0 5.1 %collective-permute-start = (bf16[8,2,256,256]{3,2,1,0:T(8,128)(2,1)S(1)}, bf16[8,2,256,256]{3,2,1,0:T(8,128)(2,1)S(1)}, u32[]{:S(2)}, u32[]{:S(2)}) collective-permute-start(bf16[8,2,256,256]{3,2,1,0:T(8,128)(2,1)S(1)} %all_to_all.49), channel_id=1, source_target_pairs={{0,32},{32,0},{1,33},{33,1},{2,34},{34,2},{3,35},{35,3},{4,36},{36... | collective-permute-start | bytes 6291464 | tf_op jit(solution)/shard_map/ppermute | solution.py:24
  42.7 0.0 copy-done.3
  42.7 0.0 copy-done.4
  42.7 0.5 fusion.13
  43.3 2.6 collective-permute-done
  45.8 2.3 pad_maximum_fusion
  48.1 5.6 %shard_map.121 = f32[2,256,256]{2,1,0:T(8,128)} custom-call(s32[16]{0:T(128)} %get-tuple-element.19.src_ref, s32[16]{0:T(128)} %get-tuple-element.20.tgt_ref, s32[1]{0:T(128)S(6)} %copy.46.cnt_ref, bf16[32,256,256]{2,1,0:T(8,128)(2,1)} %bitcast.35, bf16[16,256,256]{2,1,0:T(8,128)(2,1)} %l_ref.3, bf16[16,256,256]{2,1,0:T(8,128)(2,1)} %r_ref.3), custom_call_target="tpu_custom_call" | custom-call | tf_op jit(solution)/shard_map/pallas_call | solution.py:90
  53.8 0.0 copy-start
  53.8 1.1 copy_bitcast_fusion.1
  54.9 0.0 copy-start.2
  54.9 51.9 %all_to_all.50 = f32[32,2,8,256]{3,2,1,0:T(8,128)S(1)} all-to-all(f32[32,2,8,256]{3,2,1,0:T(8,128)S(1)} %copy_bitcast_fusion.1), channel_id=1, replica_groups=mesh['chip'=8,'core'=2,'op'=32] {'op'}, dimensions={0} | all-to-all | bytes 1048576 | tf_op jit(solution)/shard_map/all_to_all | solution.py:40
  106.8 0.1 broadcast_in_dim.25
  106.9 35.6 %all_to_all.51 = f32[32,2,8,256]{3,2,1,0:T(8,128)S(1)} all-to-all(f32[32,2,8,256]{3,2,1,0:T(8,128)S(1)} %broadcast_in_dim.25), channel_id=1, replica_groups=mesh['chip'=8,'core'=2,'op'=32] {'op'}, dimensions={0} | all-to-all | bytes 1048576 | tf_op jit(solution)/shard_map/all_to_all | solution.py:30
  142.5 0.0 copy-done
  142.5 1.0 fusion.2
  143.4 1.4 pad_maximum_fusion.2
  144.9 13.8 %all_to_all.52 = f32[16,1,2]{2,1,0:T(1,128)S(1)} all-to-all(f32[16,1,2]{2,1,0:T(1,128)S(1)} %broadcast_in_dim.27), channel_id=1, replica_groups=mesh['chip'=8,'core'=2,'op'=32] {'chip','core'}, dimensions={0} | all-to-all | bytes 256 | tf_op jit(solution)/shard_map/all_to_all | solution.py:30
  158.7 0.6 fusion.20
  160.6 0.0 copy-done.2
  160.6 1.0 fusion.6
  161.7 1.4 pad_maximum_fusion.3
  163.1 10.1 %all_to_all.53 = f32[16,1,2]{2,1,0:T(1,128)S(1)} all-to-all(f32[16,1,2]{2,1,0:T(1,128)S(1)} %broadcast_in_dim.29), channel_id=1, replica_groups=mesh['chip'=8,'core'=2,'op'=32] {'chip','core'}, dimensions={0} | all-to-all | bytes 256 | tf_op jit(solution)/shard_map/all_to_all | solution.py:30
  173.2 0.7 fusion.19
  177.9 0.1 fusion.9
  178.0 0.0 copy-start.1
  178.0 0.2 broadcast_in_dim.30
  178.2 30.0 %all_to_all.54 = bf16[8,2,256,256]{3,2,1,0:T(8,128)(2,1)S(1)} all-to-all(bf16[8,2,256,256]{3,2,1,0:T(8,128)(2,1)S(1)} %broadcast_in_dim.30), channel_id=1, replica_groups=mesh['chip'=8,'core'=2,'op'=32] {'chip'}, dimensions={0} | all-to-all | bytes 4194304 | tf_op jit(solution)/shard_map/all_to_all | solution.py:23
  208.2 3.7 %collective-permute-start.1 = (bf16[8,2,256,256]{3,2,1,0:T(8,128)(2,1)S(1)}, bf16[8,2,256,256]{3,2,1,0:T(8,128)(2,1)S(1)}, u32[]{:S(2)}, u32[]{:S(2)}) collective-permute-start(bf16[8,2,256,256]{3,2,1,0:T(8,128)(2,1)S(1)} %all_to_all.54), channel_id=1, source_target_pairs={{0,32},{32,0},{1,33},{33,1},{2,34},{34,2},{3,35},{35,3},{4,36},{36... | collective-permute-start | bytes 6291464 | tf_op jit(solution)/shard_map/ppermute | solution.py:24
  212.0 3.8 %collective-permute-done.1 = bf16[8,2,256,256]{3,2,1,0:T(8,128)(2,1)S(1)} collective-permute-done((bf16[8,2,256,256]{3,2,1,0:T(8,128)(2,1)S(1)}, bf16[8,2,256,256]{3,2,1,0:T(8,128)(2,1)S(1)}, u32[]{:S(2)}, u32[]{:S(2)}) %collective-permute-start.1) | collective-permute-done | bytes 2097184 | tf_op jit(solution)/shard_map/ppermute | solution.py:24
  215.7 2.3 pad_maximum_fusion.1
  218.0 5.6 %shard_map.122 = f32[2,256,256]{2,1,0:T(8,128)} custom-call(s32[16]{0:T(128)} %get-tuple-element.19.src_ref, s32[16]{0:T(128)} %get-tuple-element.20.tgt_ref, s32[1]{0:T(128)S(6)} %copy.46.cnt_ref, bf16[32,256,256]{2,1,0:T(8,128)(2,1)} %bitcast.34, bf16[16,256,256]{2,1,0:T(8,128)(2,1)} %l_ref.3, bf16[16,256,256]{2,1,0:T(8,128)(2,1)} %r_ref.3), custom_call_target="tpu_custom_call" | custom-call | tf_op jit(solution)/shard_map/pallas_call | solution.py:90
  223.7 1.9 copy_bitcast_fusion
  225.6 10.5 %all-to-all-start.6 = ((f32[32,2,8,256]{3,2,1,0:T(8,128)}), f32[32,2,8,256]{3,2,1,0:T(8,128)S(1)}, u32[]{:S(2)}, u32[]{:S(2)}) async-start(f32[32,2,8,256]{3,2,1,0:T(8,128)} %copy_bitcast_fusion), calls=%async_computation.6 | async-start | bytes 1048576 | tf_op jit(solution)/shard_map/all_to_all | solution.py:40
  236.2 0.1 broadcast_and_fusion
  236.3 32.3 %all-to-all-done.6 = f32[32,2,8,256]{3,2,1,0:T(8,128)S(1)} async-done(((f32[32,2,8,256]{3,2,1,0:T(8,128)}), f32[32,2,8,256]{3,2,1,0:T(8,128)S(1)}, u32[]{:S(2)}, u32[]{:S(2)}) %all-to-all-start.6) | async-done | bytes 524320 | tf_op jit(solution)/shard_map/all_to_all | solution.py:40
  268.7 0.0 copy-done.1
  268.7 1.3 multiply_reduce_fusion.1
  270.0 1.4 pad_maximum_fusion.4
  271.4 15.1 %all_to_all.55 = f32[32,1,2]{2,1,0:T(1,128)S(1)} all-to-all(f32[32,1,2]{2,1,0:T(1,128)S(1)} %broadcast_in_dim.32), channel_id=1, replica_groups=mesh['chip'=8,'core'=2,'op'=32] {'op'}, dimensions={0} | all-to-all | bytes 512 | tf_op jit(solution)/shard_map/all_to_all | solution.py:30
  286.5 0.1 reduce_sum.118
  286.6 0.6 broadcast_in_dim.33
  287.2 5.8 %all-to-all-start.8 = ((f32[16,1,2]{2,1,0:T(1,128)}), f32[16,1,2]{2,1,0:T(1,128)S(1)}, u32[]{:S(2)}, u32[]{:S(2)}) async-start(f32[16,1,2]{2,1,0:T(1,128)} %broadcast_in_dim.33), calls=%async_computation.8 | async-start | bytes 16384 | tf_op jit(solution)/shard_map/all_to_all | solution.py:30
  293.7 6.3 %all-to-all-done.8 = f32[16,1,2]{2,1,0:T(1,128)S(1)} async-done(((f32[16,1,2]{2,1,0:T(1,128)}), f32[16,1,2]{2,1,0:T(1,128)S(1)}, u32[]{:S(2)}, u32[]{:S(2)}) %all-to-all-start.8) | async-done | bytes 160 | tf_op jit(solution)/shard_map/all_to_all | solution.py:30
  300.1 0.7 fusion.18
  302.1 0.6 pad_maximum_fusion.5
  (9 shorter events, 0.3 us)
Async XLA Ops:
  3.5 39.2 %copy-start.3 = (s32[16]{0:T(128)S(1)}, s32[16]{0:T(128)}, u32[]{:S(2)}) copy-start(s32[16]{0:T(128)} %param.15) | copy-start | bytes 196
  3.5 39.2 %copy-start.4 = (s32[16]{0:T(128)S(1)}, s32[16]{0:T(128)}, u32[]{:S(2)}) copy-start(s32[16]{0:T(128)} %param.16) | copy-start | bytes 196
  37.0 8.8 %collective-permute-start = (bf16[8,2,256,256]{3,2,1,0:T(8,128)(2,1)S(1)}, bf16[8,2,256,256]{3,2,1,0:T(8,128)(2,1)S(1)}, u32[]{:S(2)}, u32[]{:S(2)}) collective-permute-start(bf16[8,2,256,256]{3,2,1,0:T(8,128)(2,1)S(1)} %all_to_all.49), channel_id=1, source_target_pairs={{0,32},{32,0},{1,33},{33,1},{2,34},{34,2},{3,35},{35,3},{4,36},{36... | collective-permute-start | bytes 6291464 | tf_op jit(solution)/shard_map/ppermute | solution.py:24
  53.8 88.7 %copy-start = (bf16[2,256,256]{2,1,0:T(8,128)(2,1)S(1)}, bf16[2,256,256]{2,1,0:T(8,128)(2,1)}, u32[]{:S(2)}) copy-start(bf16[2,256,256]{2,1,0:T(8,128)(2,1)} %param.11) | copy-start | bytes 786436
  54.9 105.7 %copy-start.2 = (bf16[2,256,256]{2,1,0:T(8,128)(2,1)S(1)}, bf16[2,256,256]{2,1,0:T(8,128)(2,1)}, u32[]{:S(2)}) copy-start(bf16[2,256,256]{2,1,0:T(8,128)(2,1)} %param.12) | copy-start | bytes 786436
  178.0 90.7 %copy-start.1 = (bf16[2,256,256]{2,1,0:T(8,128)(2,1)}, bf16[2,256,256]{2,1,0:T(8,128)(2,1)S(1)}, u32[]{:S(2)}) copy-start(bf16[2,256,256]{2,1,0:T(8,128)(2,1)S(1)} %fusion.9) | copy-start | bytes 786436
  208.2 7.5 %collective-permute-start.1 = (bf16[8,2,256,256]{3,2,1,0:T(8,128)(2,1)S(1)}, bf16[8,2,256,256]{3,2,1,0:T(8,128)(2,1)S(1)}, u32[]{:S(2)}, u32[]{:S(2)}) collective-permute-start(bf16[8,2,256,256]{3,2,1,0:T(8,128)(2,1)S(1)} %all_to_all.54), channel_id=1, source_target_pairs={{0,32},{32,0},{1,33},{33,1},{2,34},{34,2},{3,35},{35,3},{4,36},{36... | collective-permute-start | bytes 6291464 | tf_op jit(solution)/shard_map/ppermute | solution.py:24
  225.6 43.1 %all-to-all-start.6 = ((f32[32,2,8,256]{3,2,1,0:T(8,128)}), f32[32,2,8,256]{3,2,1,0:T(8,128)S(1)}, u32[]{:S(2)}, u32[]{:S(2)}) async-start(f32[32,2,8,256]{3,2,1,0:T(8,128)} %copy_bitcast_fusion), calls=%async_computation.6 | async-start | bytes 1048576 | tf_op jit(solution)/shard_map/all_to_all | solution.py:40
  287.2 12.9 %all-to-all-start.8 = ((f32[16,1,2]{2,1,0:T(1,128)}), f32[16,1,2]{2,1,0:T(1,128)S(1)}, u32[]{:S(2)}, u32[]{:S(2)}) async-start(f32[16,1,2]{2,1,0:T(1,128)} %broadcast_in_dim.33), calls=%async_computation.8 | async-start | bytes 16384 | tf_op jit(solution)/shard_map/all_to_all | solution.py:30

commit v4 on v3

--- a/solution.py
+++ b/solution.py
@@ -16,6 +16,7 @@
 
 
 SEC = ("chip", "core")
+OP = ("z", "xl")
 
 
 def gather_sec(value, chips):
@@ -34,11 +35,32 @@
     return jnp.sum(ordered_gather(values, axis_name, count), axis=0)
 
 
-def reduce_scatter_rows(partial_value, axis_name, count):
+def reduce_scatter_rows(partial_value, extra, zs):
     sectors, rows, cols = partial_value.shape
-    chunks = partial_value.reshape((sectors, count, rows // count, cols)).transpose(1, 0, 2, 3)
-    received = lax.all_to_all(chunks, axis_name, 0, 0, tiled=True)
-    return jnp.sum(received, axis=0)
+    share = rows // (2 * zs)
+    chunks = partial_value.reshape((sectors, zs, 2, share, cols)).transpose(2, 1, 0, 3, 4)
+    chunks = chunks.reshape((2, zs, sectors * share * cols))
+    tail = jnp.zeros((2, zs, 128), jnp.float32).at[:, :, : extra.shape[0]].set(extra)
+    chunks = jnp.concatenate([chunks, tail], axis=2)
+    xl = lax.axis_index("xl")
+    mine = lax.dynamic_index_in_dim(chunks, xl, 0, keepdims=False)
+    other = lax.dynamic_index_in_dim(chunks, 1 - xl, 0, keepdims=False)
+    pair_sum = mine + lax.ppermute(other, "xl", [(0, 1), (1, 0)])
+    total = jnp.sum(lax.all_to_all(pair_sum, "z", 0, 0, tiled=True), axis=0)
+    body = total[: sectors * share * cols].reshape((sectors, share, cols))
+    return body, total[sectors * share * cols : sectors * share * cols + extra.shape[0]]
+
+
+def gather_rows(rows_value, zs):
+    sectors, share, cols = rows_value.shape
+    spread = jnp.broadcast_to(rows_value[None], (zs,) + rows_value.shape)
+    same = lax.all_to_all(spread, "z", 0, 0, tiled=True)
+    other = lax.ppermute(same, "xl", [(0, 1), (1, 0)])
+    xl = lax.axis_index("xl")
+    pair = jnp.where(xl == 0, jnp.stack([same, other], 1), jnp.stack([other, same], 1))
+    return pair.reshape((2 * zs, sectors, share, cols)).transpose(1, 0, 2, 3).reshape(
+        (sectors, 2 * zs * share, cols)
+    )
 
 
 def pair_kernel(src_ref, tgt_ref, cnt_ref, s_ref, l_ref, r_ref, o_ref):
@@ -111,11 +133,12 @@
     block_size = wavefunction.shape[1]
     n_chip = lax.axis_size("chip")
     n_sec = n_chip * lax.axis_size("core")
-    n_op = lax.axis_size("op")
+    n_z = lax.axis_size("z")
+    n_op = n_z * lax.axis_size("xl")
     share_rows = block_size // n_op
     sec_index = lax.axis_index(SEC)
     core_index = lax.axis_index("core")
-    op_index = lax.axis_index("op")
+    op_index = lax.axis_index(OP)
     first_sector = sec_index * sector_count
     row_start = op_index * share_rows
     entries = float(left_dims.shape[0] * block_size * block_size)
@@ -136,7 +159,7 @@
     target_index = jnp.clip(slot_target_sector, 0, sector_count - 1)
     live_count = pair_count
 
-    def apply_partial(field):
+    def apply_partial(field, weights):
         sources = gather_sec(field, n_chip).reshape(
             (n_sec * sector_count, block_size, block_size)
         )
@@ -149,14 +172,11 @@
             live_count,
             sector_count,
         )
-        return reduce_scatter_rows(partial_value, "op", n_op)
-
-    pair_rows = apply_partial(own_vector)
-    pairs_first = (
-        ordered_gather(pair_rows, "op", n_op)
-        .transpose(1, 0, 2, 3)
-        .reshape((sector_count, block_size, block_size))
-    )
+        extra = jnp.stack([jnp.sum(w * partial_value) for w in weights] or [jnp.float32(0)])
+        return reduce_scatter_rows(partial_value, extra, n_z)
+
+    pair_rows, _ = apply_partial(own_vector, ())
+    pairs_first = gather_rows(pair_rows, n_z)
     sigma_first = jnp.where(own_mask, diag_view * vector_view + pairs_first, 0.0)
     norm_vector, correlation = reduce_vector(
         jnp.stack([jnp.sum(vector_view * vector_view), jnp.sum(vector_view * sigma_first)]),
@@ -173,16 +193,16 @@
     square_norm = scaled_square - along_vector * along_vector / norm_vector
     corr_view = (orthogonal * lax.rsqrt(square_norm / entries + 1e-06)).astype(jnp.bfloat16)
 
-    pairs_second = apply_partial(corr_view)
+    corr_full = corr_view.astype(jnp.float32)
+    pairs_second, pair_terms = apply_partial(corr_view, (vector_view, corr_full))
     mask_rows = lax.dynamic_slice_in_dim(own_mask, row_start, share_rows, 1)
     diag_rows = lax.dynamic_slice_in_dim(diag_view, row_start, share_rows, 1)
     corr_rows = lax.dynamic_slice_in_dim(corr_view, row_start, share_rows, 1).astype(jnp.float32)
-    vector_rows = lax.dynamic_slice_in_dim(vector_view, row_start, share_rows, 1)
     product_rows = jnp.where(mask_rows, diag_rows * corr_rows + pairs_second, 0.0)
     local_terms = jnp.stack(
-        [jnp.sum(vector_rows * product_rows), jnp.sum(corr_rows * product_rows)]
-    )
-    cross_term, self_term = reduce_vector(reduce_vector(local_terms, "op", n_op), SEC, n_sec)
+        [jnp.sum(vector_view * diag_view * corr_full), jnp.sum(corr_full * diag_view * corr_full)]
+    )
+    cross_term, self_term = reduce_vector(local_terms + pair_terms, SEC, n_sec)
     projected = jnp.stack(
         [rayleigh, cross_term * lax.rsqrt(norm_vector * entries), self_term / entries]
     )
@@ -191,20 +211,20 @@
 
 def solution(mesh):
     n_sec, n_op = mesh.devices.shape
-    mesh = Mesh(mesh.devices.reshape((n_sec // 2, 2, n_op)), ("chip", "core", "op"))
+    mesh = Mesh(mesh.devices.reshape((n_sec // 2, 2, n_op // 2, 2)), ("chip", "core", "z", "xl"))
     in_specs = (
         P(SEC, None, None),
         P(SEC, None, None),
         P(SEC, None, None),
-        P(("chip", "core", "op"), None, None),
-        P(("chip", "core", "op"), None, None),
-        P(("chip", "core", "op")),
-        P(("chip", "core", "op")),
-        P(("chip", "core", "op")),
+        P(("chip", "core", "z", "xl"), None, None),
+        P(("chip", "core", "z", "xl"), None, None),
+        P(("chip", "core", "z", "xl")),
+        P(("chip", "core", "z", "xl")),
+        P(("chip", "core", "z", "xl")),
         P(),
         P(),
     )
-    out_specs = (P(SEC, None, None), P(SEC, "op", None), P())
+    out_specs = (P(SEC, None, None), P(SEC, OP, None), P())
     return jax.shard_map(
         on_device, mesh=mesh, in_specs=in_specs, out_specs=out_specs, check_vma=False
     )

time: 304 us -> 280 us (0.921)
  blocking collectives: 190 us -> 147 us
  starting transfers between devices: 25.2 us -> 37 us
  Pallas kernels: 11.3 us -> 16.7 us
  other arithmetic: 14.9 us -> 19.6 us
  waiting for transfers between devices: 45 us -> 41.7 us
    all_to_all x4 -> x2, blocking collectives: 74.7 us -> 26.6 us  [ordered_gather(): return lax.all_to_all(spread, axis_name, 0, 0, tiled=True)]
    all_to_all x1, waiting for transfers between devices: 32.3 us -> 13.3 us  [reduce_scatter_rows(): total = jnp.sum(lax.all_to_all(pair_sum, 'z', 0, 0, tiled=True), axis=0)]
    ppermute x0 -> x3, waiting for transfers between devices: none -> 15.5 us  [the longest x2 11.8 us: reduce_scatter_rows(): pair_sum = mine + lax.ppermute(other, 'xl', [(0, 1), (1, 0)])]
    ppermute x0 -> x3, starting transfers between devices: none -> 7.54 us  [the longest x2 3.84 us: reduce_scatter_rows(): pair_sum = mine + lax.ppermute(other, 'xl', [(0, 1), (1, 0)])]
    pallas_call x2, Pallas kernels: 11.3 us -> 16.7 us  [pair_partial(): pl.pallas_call(pair_kernel, grid_spec=grid_spec, out_shape=jax.ShapeDtype...]
    all_to_all x1 -> x2, blocking collectives: 51.9 us -> 57.1 us  [the longest x1 33.1 us: reduce_scatter_rows(): total = jnp.sum(lax.all_to_all(pair_sum, 'z', 0, 0, tiled=True), axis=0)]
    all_to_all x1, starting transfers between devices: 5.85 us -> 9.07 us  [ordered_gather(): return lax.all_to_all(spread, axis_name, 0, 0, tiled=True)]
  transfers between devices with their start and end apart: 4 -> 7, of which waited for: 4 -> 7; matrix products, arithmetic and copies ran while one was open for 0% -> 0% of each run, Pallas kernels for 0% -> 0%
where the time goes in v4:
time: 280 us; the launch traced here: 279 us
  blocking collectives  147 us (52%)
  waiting for transfers between devices  41.7 us (15%)
  starting transfers between devices  37 us (13%)
  other arithmetic  19.6 us (7%)
  Pallas kernels  16.7 us (6%)
  between operations  8.86 us (3%)
  local copies, waits for them, and re-layouts  7.89 us (3%)
    all_to_all x2, blocking collectives, gather_sec(): same_core = lax.all_to_all(spread, 'chip', 0, 0, tiled=True)  63.5 us
    all_to_all x1, blocking collectives, reduce_scatter_rows(): total = jnp.sum(lax.all_to_all(pair_sum, 'z', 0, 0, tiled=True), axis=0)  33.1 us
    all_to_all x2, blocking collectives, ordered_gather(): return lax.all_to_all(spread, axis_name, 0, 0, tiled=True)  26.6 us
    all_to_all x1, blocking collectives, gather_rows(): same = lax.all_to_all(spread, 'z', 0, 0, tiled=True)  24 us
    pallas_call x2, Pallas kernels, pair_partial(): pl.pallas_call(pair_kernel, grid_spec=grid_spec, out_shape=jax.ShapeDtype...  16.7 us
    all_to_all x1, waiting for transfers between devices, reduce_scatter_rows(): total = jnp.sum(lax.all_to_all(pair_sum, 'z', 0, 0, tiled=True), axis=0)  13.3 us
    ppermute x2, waiting for transfers between devices, reduce_scatter_rows(): pair_sum = mine + lax.ppermute(other, 'xl', [(0, 1), (1, 0)])  11.8 us
    all_to_all x1, starting transfers between devices, reduce_scatter_rows(): total = jnp.sum(lax.all_to_all(pair_sum, 'z', 0, 0, tiled=True), axis=0)  11.6 us
  transfers between devices with their start and end apart: 7, of which 7 were waited for; matrix products, arithmetic and copies ran while one was open for 0% of the time, Pallas kernels for 0%

profile of v4, /device:TPU:1, one launch (start us, length us, event | category | flops | bytes accessed | tf_op | source)
XLA Modules:
  0.0 279.0 jit_solution(13736403415635592984)
XLA Ops:
  0.6 0.7 dynamic_slice.28
  1.4 0.7 dynamic_slice.29
  2.1 0.1 iota_compare_fusion
  2.2 1.1 and_select_fusion
  3.3 0.2 broadcast_in_dim.24
  3.5 0.0 copy-start.4
  3.5 0.0 copy-start.5
  3.5 33.5 %all_to_all.51 = bf16[8,2,256,256]{3,2,1,0:T(8,128)(2,1)S(1)} all-to-all(bf16[8,2,256,256]{3,2,1,0:T(8,128)(2,1)S(1)} %broadcast_in_dim.24), channel_id=1, replica_groups=mesh['chip'=8,'core'=2,'z'=16,'xl'=2] {'chip'}, dimensions={0} | all-to-all | bytes 4194304 | tf_op jit(solution)/shard_map/all_to_all | solution.py:24
  37.0 5.1 %collective-permute-start = (bf16[8,2,256,256]{3,2,1,0:T(8,128)(2,1)S(1)}, bf16[8,2,256,256]{3,2,1,0:T(8,128)(2,1)}, u32[]{:S(2)}, u32[]{:S(2)}) collective-permute-start(bf16[8,2,256,256]{3,2,1,0:T(8,128)(2,1)S(1)} %all_to_all.51), channel_id=1, source_target_pairs={{0,32},{32,0},{1,33},{33,1},{2,34},{34,2},{3,35},{35,3},{4,36},{36... | collective-permute-start | bytes 6291464 | tf_op jit(solution)/shard_map/ppermute | solution.py:25
  42.7 0.0 copy-done.4
  42.7 0.0 copy-done.5
  42.7 0.5 fusion.16
  43.3 2.7 collective-permute-done
  46.0 3.9 %pad_maximum_fusion = bf16[16,2,256,256]{3,2,1,0:T(8,128)(2,1)} fusion(bf16[8,2,256,256]{3,2,1,0:T(8,128)(2,1)} %collective-permute-done, bf16[8,2,256,256]{3,2,1,0:T(8,128)(2,1)S(1)} %all_to_all.51), kind=kLoop, calls=%fused_computation | loop fusion | flops 2097152 | bytes 8388608 | tf_op jit(solution)/shard_map/concatenate | solution.py:26
  49.8 8.3 %shard_map.121 = f32[2,256,256]{2,1,0:T(8,128)} custom-call(s32[16]{0:T(128)} %get-tuple-element.44.src_ref, s32[16]{0:T(128)} %get-tuple-element.45.tgt_ref, s32[1]{0:T(128)S(6)} %copy.48.cnt_ref, bf16[32,256,256]{2,1,0:T(8,128)(2,1)} %bitcast.58, bf16[16,256,256]{2,1,0:T(8,128)(2,1)} %l_ref.3, bf16[16,256,256]{2,1,0:T(8,128)(2,1)} %r_ref.3), custom_call_target="tpu_custom_call" | custom-call | tf_op jit(solution)/shard_map/pallas_call | solution.py:112
  58.2 1.1 copy.47
  59.3 0.1 reshape.167
  59.4 1.9 collective-permute-start.1
  61.4 0.0 copy-start
  61.4 0.0 copy-start.1
  61.4 5.9 %collective-permute-done.1 = f32[16,4224]{1,0:T(8,128)S(1)} collective-permute-done((f32[16,4224]{1,0:T(8,128)S(1)}, f32[16,4224]{1,0:T(8,128)S(1)}, u32[]{:S(2)}, u32[]{:S(2)}) %collective-permute-start.1) | collective-permute-done | bytes 270368 | tf_op jit(solution)/shard_map/ppermute | solution.py:48
  67.3 0.0 copy-start.3
  67.3 0.2 all_to_all.34
  67.5 33.1 %all_to_all.52 = f32[16,1,4224]{2,1,0:T(1,128)S(1)} all-to-all(f32[16,1,4224]{2,1,0:T(1,128)S(1)} %all_to_all.34), channel_id=1, replica_groups=mesh['chip'=8,'core'=2,'z'=16,'xl'=2] {'z'}, dimensions={0} | all-to-all | bytes 540672 | tf_op jit(solution)/shard_map/all_to_all | solution.py:49
  100.6 0.2 reduce_sum.117
  100.8 24.0 %all_to_all.53 = f32[16,2,8,256]{3,2,1,0:T(8,128)S(1)} all-to-all(f32[16,2,8,256]{3,2,1,0:T(8,128)S(1)} %broadcast_in_dim.26), channel_id=1, replica_groups=mesh['chip'=8,'core'=2,'z'=16,'xl'=2] {'z'}, dimensions={0} | all-to-all | bytes 524288 | tf_op jit(solution)/shard_map/all_to_all | solution.py:57
  124.8 3.7 %collective-permute-start.2 = (f32[16,2,8,256]{3,2,1,0:T(8,128)S(1)}, f32[16,2,8,256]{3,2,1,0:T(8,128)S(1)}, u32[]{:S(2)}, u32[]{:S(2)}) collective-permute-start(f32[16,2,8,256]{3,2,1,0:T(8,128)S(1)} %all_to_all.53), channel_id=1, source_target_pairs={{0,1},{1,0},{2,3},{3,2},{4,5},{5,4},{6,7},{7,6},{8,9},{9,8},{10,11... | collective-permute-start | bytes 786440 | tf_op jit(solution)/shard_map/ppermute | solution.py:58
  128.6 3.7 %collective-permute-done.2 = f32[16,2,8,256]{3,2,1,0:T(8,128)S(1)} collective-permute-done((f32[16,2,8,256]{3,2,1,0:T(8,128)S(1)}, f32[16,2,8,256]{3,2,1,0:T(8,128)S(1)}, u32[]{:S(2)}, u32[]{:S(2)}) %collective-permute-start.2) | collective-permute-done | bytes 262176 | tf_op jit(solution)/shard_map/ppermute | solution.py:58
  132.4 0.0 copy-done
  132.4 1.0 fusion.3
  133.4 1.4 pad_maximum_fusion.3
  134.8 16.5 %all_to_all.54 = f32[16,1,2]{2,1,0:T(1,128)S(1)} all-to-all(f32[16,1,2]{2,1,0:T(1,128)S(1)} %broadcast_in_dim.28), channel_id=1, replica_groups=mesh['chip'=8,'core'=2,'z'=16,'xl'=2] {'chip','core'}, dimensions={0} | all-to-all | bytes 256 | tf_op jit(solution)/shard_map/all_to_all | solution.py:31
  151.3 0.6 fusion.22
  153.3 1.1 fusion.7
  154.3 1.4 pad_maximum_fusion.4
  155.8 10.1 %all_to_all.55 = f32[16,1,2]{2,1,0:T(1,128)S(1)} all-to-all(f32[16,1,2]{2,1,0:T(1,128)S(1)} %broadcast_in_dim.30), channel_id=1, replica_groups=mesh['chip'=8,'core'=2,'z'=16,'xl'=2] {'chip','core'}, dimensions={0} | all-to-all | bytes 256 | tf_op jit(solution)/shard_map/all_to_all | solution.py:31
  165.9 0.7 fusion.21
  170.6 0.2 fusion.10
  170.8 0.0 copy-start.2
  170.8 0.2 broadcast_in_dim.31
  171.0 30.0 %all_to_all.56 = bf16[8,2,256,256]{3,2,1,0:T(8,128)(2,1)S(1)} all-to-all(bf16[8,2,256,256]{3,2,1,0:T(8,128)(2,1)S(1)} %broadcast_in_dim.31), channel_id=1, replica_groups=mesh['chip'=8,'core'=2,'z'=16,'xl'=2] {'chip'}, dimensions={0} | all-to-all | bytes 4194304 | tf_op jit(solution)/shard_map/all_to_all | solution.py:24
  201.0 3.7 %collective-permute-start.3 = (bf16[8,2,256,256]{3,2,1,0:T(8,128)(2,1)S(1)}, bf16[8,2,256,256]{3,2,1,0:T(8,128)(2,1)S(1)}, u32[]{:S(2)}, u32[]{:S(2)}) collective-permute-start(bf16[8,2,256,256]{3,2,1,0:T(8,128)(2,1)S(1)} %all_to_all.56), channel_id=1, source_target_pairs={{0,32},{32,0},{1,33},{33,1},{2,34},{34,2},{3,35},{35,3},{4,36},{36... | collective-permute-start | bytes 6291464 | tf_op jit(solution)/shard_map/ppermute | solution.py:25
  204.8 3.8 %collective-permute-done.3 = bf16[8,2,256,256]{3,2,1,0:T(8,128)(2,1)S(1)} collective-permute-done((bf16[8,2,256,256]{3,2,1,0:T(8,128)(2,1)S(1)}, bf16[8,2,256,256]{3,2,1,0:T(8,128)(2,1)S(1)}, u32[]{:S(2)}, u32[]{:S(2)}) %collective-permute-start.3) | collective-permute-done | bytes 2097184 | tf_op jit(solution)/shard_map/ppermute | solution.py:25
  208.5 2.3 pad_maximum_fusion.1
  210.8 8.3 %shard_map.122 = f32[2,256,256]{2,1,0:T(8,128)} custom-call(s32[16]{0:T(128)} %get-tuple-element.44.src_ref, s32[16]{0:T(128)} %get-tuple-element.45.tgt_ref, s32[1]{0:T(128)S(6)} %copy.48.cnt_ref, bf16[32,256,256]{2,1,0:T(8,128)(2,1)} %bitcast.57, bf16[16,256,256]{2,1,0:T(8,128)(2,1)} %l_ref.3, bf16[16,256,256]{2,1,0:T(8,128)(2,1)} %r_ref.3), custom_call_target="tpu_custom_call" | custom-call | tf_op jit(solution)/shard_map/pallas_call | solution.py:112
  219.2 2.0 fusion.11
  221.2 1.1 copy.46
  222.3 0.1 reshape.171
  222.4 1.4 fusion.17
  223.9 1.9 collective-permute-start.4
  225.8 5.9 %collective-permute-done.4 = f32[16,4224]{1,0:T(8,128)S(1)} collective-permute-done((f32[16,4224]{1,0:T(8,128)S(1)}, f32[16,4224]{1,0:T(8,128)S(1)}, u32[]{:S(2)}, u32[]{:S(2)}) %collective-permute-start.4) | collective-permute-done | bytes 270368 | tf_op jit(solution)/shard_map/ppermute | solution.py:48
  231.7 0.9 all_to_all.40
  232.6 11.6 %all-to-all-start.6 = ((f32[16,1,4224]{2,1,0:T(1,128)}), f32[16,1,4224]{2,1,0:T(1,128)S(1)}, u32[]{:S(2)}, u32[]{:S(2)}) async-start(f32[16,1,4224]{2,1,0:T(1,128)} %all_to_all.40), calls=%async_computation.6 | async-start | bytes 540672 | tf_op jit(solution)/shard_map/all_to_all | solution.py:49
  244.3 0.1 broadcast_and_fusion
  245.1 13.3 %all-to-all-done.6 = f32[16,1,4224]{2,1,0:T(1,128)S(1)} async-done(((f32[16,1,4224]{2,1,0:T(1,128)}), f32[16,1,4224]{2,1,0:T(1,128)S(1)}, u32[]{:S(2)}, u32[]{:S(2)}) %all-to-all-start.6) | async-done | bytes 270368 | tf_op jit(solution)/shard_map/all_to_all | solution.py:49
  258.5 0.2 reduce_sum.126
  258.6 1.3 slice_add_fusion
  259.9 0.6 broadcast_in_dim.33
  260.5 9.1 %all-to-all-start.7 = ((f32[16,1,2]{2,1,0:T(1,128)}), f32[16,1,2]{2,1,0:T(1,128)S(1)}, u32[]{:S(2)}, u32[]{:S(2)}) async-start(f32[16,1,2]{2,1,0:T(1,128)} %broadcast_in_dim.33), calls=%async_computation.7 | async-start | bytes 16384 | tf_op jit(solution)/shard_map/all_to_all | solution.py:31
  269.6 0.0 copy-done.2
  269.6 0.6 add_select_fusion
  270.2 6.4 %all-to-all-done.7 = f32[16,1,2]{2,1,0:T(1,128)S(1)} async-done(((f32[16,1,2]{2,1,0:T(1,128)}), f32[16,1,2]{2,1,0:T(1,128)S(1)}, u32[]{:S(2)}, u32[]{:S(2)}) %all-to-all-start.7) | async-done | bytes 160 | tf_op jit(solution)/shard_map/all_to_all | solution.py:31
  276.6 0.6 fusion.20
  278.4 0.6 pad_maximum_fusion.5
  (20 shorter events, 0.4 us)
Async XLA Ops:
  3.5 39.2 %copy-start.4 = (s32[16]{0:T(128)S(1)}, s32[16]{0:T(128)}, u32[]{:S(2)}) copy-start(s32[16]{0:T(128)} %param.19) | copy-start | bytes 196
  3.5 39.2 %copy-start.5 = (s32[16]{0:T(128)S(1)}, s32[16]{0:T(128)}, u32[]{:S(2)}) copy-start(s32[16]{0:T(128)} %param.20) | copy-start | bytes 196
  37.0 9.0 %collective-permute-start = (bf16[8,2,256,256]{3,2,1,0:T(8,128)(2,1)S(1)}, bf16[8,2,256,256]{3,2,1,0:T(8,128)(2,1)}, u32[]{:S(2)}, u32[]{:S(2)}) collective-permute-start(bf16[8,2,256,256]{3,2,1,0:T(8,128)(2,1)S(1)} %all_to_all.51), channel_id=1, source_target_pairs={{0,32},{32,0},{1,33},{33,1},{2,34},{34,2},{3,35},{35,3},{4,36},{36... | collective-permute-start | bytes 6291464 | tf_op jit(solution)/shard_map/ppermute | solution.py:25
  59.4 7.8 %collective-permute-start.1 = (f32[16,4224]{1,0:T(8,128)S(1)}, f32[16,4224]{1,0:T(8,128)S(1)}, u32[]{:S(2)}, u32[]{:S(2)}) collective-permute-start(f32[16,4224]{1,0:T(8,128)S(1)} %fusion.15), channel_id=1, source_target_pairs={{0,1},{1,0},{2,3},{3,2},{4,5},{5,4},{6,7},{7,6},{8,9},{9,8},{10,11... | collective-permute-start | bytes 811016 | tf_op jit(solution)/shard_map/ppermute | solution.py:48
  61.4 71.0 %copy-start = (bf16[2,256,256]{2,1,0:T(8,128)(2,1)S(1)}, bf16[2,256,256]{2,1,0:T(8,128)(2,1)}, u32[]{:S(2)}) copy-start(bf16[2,256,256]{2,1,0:T(8,128)(2,1)} %param.14) | copy-start | bytes 786436
  61.4 71.0 %copy-start.1 = (bf16[2,256,256]{2,1,0:T(8,128)(2,1)S(1)}, bf16[2,256,256]{2,1,0:T(8,128)(2,1)}, u32[]{:S(2)}) copy-start(bf16[2,256,256]{2,1,0:T(8,128)(2,1)} %param.15) | copy-start | bytes 786436
  67.3 86.0 %copy-start.3 = (bf16[2,256,256]{2,1,0:T(8,128)(2,1)S(1)}, bf16[2,256,256]{2,1,0:T(8,128)(2,1)}, u32[]{:S(2)}) copy-start(bf16[2,256,256]{2,1,0:T(8,128)(2,1)} %param.16) | copy-start | bytes 786436
  124.8 7.5 %collective-permute-start.2 = (f32[16,2,8,256]{3,2,1,0:T(8,128)S(1)}, f32[16,2,8,256]{3,2,1,0:T(8,128)S(1)}, u32[]{:S(2)}, u32[]{:S(2)}) collective-permute-start(f32[16,2,8,256]{3,2,1,0:T(8,128)S(1)} %all_to_all.53), channel_id=1, source_target_pairs={{0,1},{1,0},{2,3},{3,2},{4,5},{5,4},{6,7},{7,6},{8,9},{9,8},{10,11... | collective-permute-start | bytes 786440 | tf_op jit(solution)/shard_map/ppermute | solution.py:58
  170.8 98.8 %copy-start.2 = (bf16[2,256,256]{2,1,0:T(8,128)(2,1)}, bf16[2,256,256]{2,1,0:T(8,128)(2,1)S(1)}, u32[]{:S(2)}) copy-start(bf16[2,256,256]{2,1,0:T(8,128)(2,1)S(1)} %fusion.10) | copy-start | bytes 786436
  201.0 7.5 %collective-permute-start.3 = (bf16[8,2,256,256]{3,2,1,0:T(8,128)(2,1)S(1)}, bf16[8,2,256,256]{3,2,1,0:T(8,128)(2,1)S(1)}, u32[]{:S(2)}, u32[]{:S(2)}) collective-permute-start(bf16[8,2,256,256]{3,2,1,0:T(8,128)(2,1)S(1)} %all_to_all.56), channel_id=1, source_target_pairs={{0,32},{32,0},{1,33},{33,1},{2,34},{34,2},{3,35},{35,3},{4,36},{36... | collective-permute-start | bytes 6291464 | tf_op jit(solution)/shard_map/ppermute | solution.py:25
  223.9 7.8 %collective-permute-start.4 = (f32[16,4224]{1,0:T(8,128)S(1)}, f32[16,4224]{1,0:T(8,128)S(1)}, u32[]{:S(2)}, u32[]{:S(2)}) collective-permute-start(f32[16,4224]{1,0:T(8,128)S(1)} %dynamic-slice_bitcast_fusion), channel_id=1, source_target_pairs={{0,1},{1,0},{2,3},{3,2},{4,5},{5,4},{6,7},{7,6},{8,9},{9,8},{10,11... | collective-permute-start | bytes 811016 | tf_op jit(solution)/shard_map/ppermute | solution.py:48
  232.6 25.9 %all-to-all-start.6 = ((f32[16,1,4224]{2,1,0:T(1,128)}), f32[16,1,4224]{2,1,0:T(1,128)S(1)}, u32[]{:S(2)}, u32[]{:S(2)}) async-start(f32[16,1,4224]{2,1,0:T(1,128)} %all_to_all.40), calls=%async_computation.6 | async-start | bytes 540672 | tf_op jit(solution)/shard_map/all_to_all | solution.py:49
  260.5 16.1 %all-to-all-start.7 = ((f32[16,1,2]{2,1,0:T(1,128)}), f32[16,1,2]{2,1,0:T(1,128)S(1)}, u32[]{:S(2)}, u32[]{:S(2)}) async-start(f32[16,1,2]{2,1,0:T(1,128)} %broadcast_in_dim.33), calls=%async_computation.7 | async-start | bytes 16384 | tf_op jit(solution)/shard_map/all_to_all | solution.py:31

commit v5 on v4

--- a/solution.py
+++ b/solution.py
@@ -23,7 +23,7 @@
     spread = jnp.broadcast_to(value[None], (chips,) + value.shape)
     same_core = lax.all_to_all(spread, "chip", 0, 0, tiled=True)
     other_core = lax.ppermute(same_core, "core", [(0, 1), (1, 0)])
-    return jnp.concatenate([same_core, other_core], 0)
+    return same_core, other_core
 
 
 def ordered_gather(value, axis_name, count):
@@ -63,15 +63,14 @@
     )
 
 
-def pair_kernel(src_ref, tgt_ref, cnt_ref, s_ref, l_ref, r_ref, o_ref):
+def pair_kernel(same_idx, other_idx, side_ref, tgt_ref, cnt_ref, a_ref, b_ref, l_ref, r_ref, o_ref):
     k = pl.program_id(0)
 
     @pl.when(k == 0)
     def _():
         o_ref[...] = jnp.zeros_like(o_ref)
 
-    @pl.when(k < cnt_ref[0])
-    def _():
+    def add_pair(s_ref):
         middle = jnp.dot(l_ref[0], s_ref[0], preferred_element_type=jnp.float32)
         high = middle.astype(jnp.bfloat16)
         low = (middle - high.astype(jnp.float32)).astype(jnp.bfloat16)
@@ -82,31 +81,61 @@
         t = tgt_ref[k]
         o_ref[t] = o_ref[t] + contribution
 
+    live = k < cnt_ref[0]
+
+    @pl.when(live & (side_ref[k] == 0))
+    def _():
+        add_pair(a_ref)
+
+    @pl.when(live & (side_ref[k] != 0))
+    def _():
+        add_pair(b_ref)
+
+
+def carried(index, used):
+    slots = index.shape[0]
+    order = jnp.arange(slots, dtype=jnp.int32)
+    last = lax.cummax(jnp.where(used, order, -1), axis=0)
+    first = jnp.argmax(used).astype(jnp.int32)
+    return index[jnp.where(last < 0, first, last)]
+
 
 def pair_partial(sources, left_blocks, right_blocks, source_index, target_index, live_count, sector_count):
+    same_core, other_core = sources
     slots, block_size, _ = left_blocks.shape
-    n_sources = sources.shape[0]
-
-    def live_slot(k, cnt):
-        return jnp.minimum(k, jnp.clip(cnt[0] - 1, 0, slots - 1))
-
-    def source_map(k, src, tgt, cnt):
-        return (jnp.clip(src[live_slot(k, cnt)], 0, n_sources - 1), 0, 0)
-
-    def operator_map(k, src, tgt, cnt):
-        return (live_slot(k, cnt), 0, 0)
+    chips = same_core.shape[0]
+    same_core = same_core.reshape((chips * sector_count, block_size, block_size))
+    other_core = other_core.reshape((chips * sector_count, block_size, block_size))
+    last_live = jnp.clip(live_count[0] - 1, 0, slots - 1)
+    slot_ids = jnp.minimum(jnp.arange(slots, dtype=jnp.int32), last_live)
+    wanted = jnp.clip(source_index[slot_ids], 0, 2 * chips * sector_count - 1)
+    side = (wanted >= chips * sector_count).astype(jnp.int32)
+    within = wanted - side * chips * sector_count
+    same_idx = carried(within, side == 0)
+    other_idx = carried(within, side != 0)
+    target = target_index[slot_ids]
+
+    def same_map(k, a, b, sd, tg, cnt):
+        return (a[k], 0, 0)
+
+    def other_map(k, a, b, sd, tg, cnt):
+        return (b[k], 0, 0)
+
+    def operator_map(k, a, b, sd, tg, cnt):
+        return (jnp.minimum(k, jnp.clip(cnt[0] - 1, 0, slots - 1)), 0, 0)
 
     block = (1, block_size, block_size)
     grid_spec = pltpu.PrefetchScalarGridSpec(
-        num_scalar_prefetch=3,
+        num_scalar_prefetch=5,
         grid=(slots,),
         in_specs=[
-            pl.BlockSpec(block, source_map),
+            pl.BlockSpec(block, same_map),
+            pl.BlockSpec(block, other_map),
             pl.BlockSpec(block, operator_map),
             pl.BlockSpec(block, operator_map),
         ],
         out_specs=pl.BlockSpec(
-            (sector_count, block_size, block_size), lambda k, src, tgt, cnt: (0, 0, 0)
+            (sector_count, block_size, block_size), lambda k, a, b, sd, tg, cnt: (0, 0, 0)
         ),
     )
     return pl.pallas_call(
@@ -114,7 +143,7 @@
         grid_spec=grid_spec,
         out_shape=jax.ShapeDtypeStruct((sector_count, block_size, block_size), jnp.float32),
         compiler_params=pltpu.CompilerParams(dimension_semantics=("arbitrary",)),
-    )(source_index, target_index, live_count, sources, left_blocks, right_blocks)
+    )(same_idx, other_idx, side, target, live_count, same_core, other_core, left_blocks, right_blocks)
 
 
 def on_device(
@@ -160,9 +189,7 @@
     live_count = pair_count
 
     def apply_partial(field, weights):
-        sources = gather_sec(field, n_chip).reshape(
-            (n_sec * sector_count, block_size, block_size)
-        )
+        sources = gather_sec(field, n_chip)
         partial_value = pair_partial(
             sources,
             left_operator_blocks,

time: 280 us -> 282 us (level)
  local copies, waits for them, and re-layouts: 7.89 us -> 13.7 us
  Pallas kernels: 16.7 us -> 22.5 us
  waiting for transfers between devices: 41.7 us -> 37.1 us
  other arithmetic: 19.6 us -> 16.6 us
    concatenate x2 -> x0, other arithmetic: 6.16 us -> none  [gather_sec(): return jnp.concatenate([same_core, other_core], 0)]
    pallas_call x2, Pallas kernels: 16.7 us -> 22.5 us  [pair_partial(): pl.pallas_call(pair_kernel, grid_spec=grid_spec, out_shape=jax.ShapeDtype...]
    gather x0 -> x4, local copies, waits for them, and re-layouts: none -> 4.3 us  [the longest x2 2.41 us: carried(): return index[jnp.where(last < 0, first, last)]]
  transfers between devices with their start and end apart: 7 -> 7, of which waited for: 7 -> 6; matrix products, arithmetic and copies ran while one was open for 0% -> 3% of each run, Pallas kernels for 0% -> 0%
where the time goes in v5:
time: 282 us; the launch traced here: 281 us
  blocking collectives  146 us (52%)
  waiting for transfers between devices  37.1 us (13%)
  starting transfers between devices  36.2 us (13%)
  Pallas kernels  22.5 us (8%)
  other arithmetic  16.6 us (6%)
  local copies, waits for them, and re-layouts  13.7 us (5%)
  between operations  8.61 us (3%)
    all_to_all x2, blocking collectives, gather_sec(): same_core = lax.all_to_all(spread, 'chip', 0, 0, tiled=True)  63.5 us
    all_to_all x1, blocking collectives, reduce_scatter_rows(): total = jnp.sum(lax.all_to_all(pair_sum, 'z', 0, 0, tiled=True), axis=0)  32.2 us
    all_to_all x2, blocking collectives, ordered_gather(): return lax.all_to_all(spread, axis_name, 0, 0, tiled=True)  26.5 us
    all_to_all x1, blocking collectives, gather_rows(): same = lax.all_to_all(spread, 'z', 0, 0, tiled=True)  24 us
    pallas_call x2, Pallas kernels, pair_partial(): pl.pallas_call(pair_kernel, grid_spec=grid_spec, out_shape=jax.ShapeDtype...  22.5 us
    all_to_all x1, waiting for transfers between devices, reduce_scatter_rows(): total = jnp.sum(lax.all_to_all(pair_sum, 'z', 0, 0, tiled=True), axis=0)  12.4 us
    all_to_all x1, starting transfers between devices, reduce_scatter_rows(): total = jnp.sum(lax.all_to_all(pair_sum, 'z', 0, 0, tiled=True), axis=0)  10.6 us
    ppermute x2, waiting for transfers between devices, reduce_scatter_rows(): pair_sum = mine + lax.ppermute(other, 'xl', [(0, 1), (1, 0)])  10.5 us
  transfers between devices with their start and end apart: 7, of which 6 were waited for; matrix products, arithmetic and copies ran while one was open for 3% of the time, Pallas kernels for 0%

profile of v5, /device:TPU:1, one launch (start us, length us, event | category | flops | bytes accessed | tf_op | source)
XLA Modules:
  0.0 280.9 jit_solution(1659677950424885111)
XLA Ops:
  0.6 0.7 dynamic_slice.28
  1.4 0.7 dynamic_slice.29
  2.1 0.1 iota_compare_fusion
  2.2 1.1 and_select_fusion
  3.3 0.2 broadcast_in_dim.44
  3.5 0.0 copy-start.8
  3.5 33.5 %all_to_all.51 = bf16[8,2,256,256]{3,2,1,0:T(8,128)(2,1)S(1)} all-to-all(bf16[8,2,256,256]{3,2,1,0:T(8,128)(2,1)S(1)} %broadcast_in_dim.44), channel_id=1, replica_groups=mesh['chip'=8,'core'=2,'z'=16,'xl'=2] {'chip'}, dimensions={0} | all-to-all | bytes 4194304 | tf_op jit(solution)/shard_map/all_to_all | solution.py:24
  37.0 5.1 %collective-permute-start = (bf16[8,2,256,256]{3,2,1,0:T(8,128)(2,1)S(1)}, bf16[8,2,256,256]{3,2,1,0:T(8,128)(2,1)}, u32[]{:S(2)}, u32[]{:S(2)}) collective-permute-start(bf16[8,2,256,256]{3,2,1,0:T(8,128)(2,1)S(1)} %all_to_all.51), channel_id=1, source_target_pairs={{0,32},{32,0},{1,33},{33,1},{2,34},{34,2},{3,35},{35,3},{4,36},{36... | collective-permute-start | bytes 6291464 | tf_op jit(solution)/shard_map/ppermute | solution.py:25
  42.8 0.7 gather_fusion
  43.5 0.1 copy.34
  43.5 0.1 copy.33
  43.7 0.7 compare_reduce_fusion
  44.4 0.8 fusion.17
  45.1 1.2 gather_fusion.2
  46.4 0.7 compare_reduce_fusion.1
  47.0 0.8 fusion.16
  47.8 1.2 gather_fusion.1
  49.0 1.2 gather_fusion.3
  50.2 0.5 compare_convert_fusion.side_ref
  50.7 11.2 %shard_map.121 = f32[2,256,256]{2,1,0:T(8,128)} custom-call(s32[16]{0:T(128)} %gather_fusion.1, s32[16]{0:T(128)} %gather_fusion.2, s32[16]{0:T(128)} %compare_convert_fusion.side_ref, s32[16]{0:T(128)} %gather_fusion.3, s32[1]{0:T(128)S(6)} %copy.60.cnt_ref, bf16[16,256,256]{2,1,0:T(8,128)(2,1)} %bitcast.66, bf16[16,256,256]{2,1,0:T(8,128)(2,1)} %bitcast.5.b_ref, ...), custom_call_target="tpu_custom_call" | custom-call | tf_op jit(solution)/shard_map/pallas_call | solution.py:141
  62.0 1.1 copy.59
  63.1 0.1 reshape.280
  63.2 1.9 collective-permute-start.1
  65.2 0.0 copy-start.3
  65.2 5.3 %collective-permute-done.1 = f32[16,4224]{1,0:T(8,128)S(1)} collective-permute-done((f32[16,4224]{1,0:T(8,128)S(1)}, f32[16,4224]{1,0:T(8,128)S(1)}, u32[]{:S(2)}, u32[]{:S(2)}) %collective-permute-start.1) | collective-permute-done | bytes 270368 | tf_op jit(solution)/shard_map/ppermute | solution.py:48
  70.5 0.2 all_to_all.34
  70.7 32.2 %all_to_all.52 = f32[16,1,4224]{2,1,0:T(1,128)S(1)} all-to-all(f32[16,1,4224]{2,1,0:T(1,128)S(1)} %all_to_all.34), channel_id=1, replica_groups=mesh['chip'=8,'core'=2,'z'=16,'xl'=2] {'z'}, dimensions={0} | all-to-all | bytes 540672 | tf_op jit(solution)/shard_map/all_to_all | solution.py:49
  102.9 0.2 reduce_sum.117
  103.1 24.0 %all_to_all.53 = f32[16,2,8,256]{3,2,1,0:T(8,128)S(1)} all-to-all(f32[16,2,8,256]{3,2,1,0:T(8,128)S(1)} %broadcast_in_dim.84), channel_id=1, replica_groups=mesh['chip'=8,'core'=2,'z'=16,'xl'=2] {'z'}, dimensions={0} | all-to-all | bytes 524288 | tf_op jit(solution)/shard_map/all_to_all | solution.py:57
  127.1 3.1 %collective-permute-start.2 = (f32[16,2,8,256]{3,2,1,0:T(8,128)S(1)}, f32[16,2,8,256]{3,2,1,0:T(8,128)S(1)}, u32[]{:S(2)}, u32[]{:S(2)}) collective-permute-start(f32[16,2,8,256]{3,2,1,0:T(8,128)S(1)} %all_to_all.53), channel_id=1, source_target_pairs={{0,1},{1,0},{2,3},{3,2},{4,5},{5,4},{6,7},{7,6},{8,9},{9,8},{10,11... | collective-permute-start | bytes 786440 | tf_op jit(solution)/shard_map/ppermute | solution.py:58
  130.3 4.0 %collective-permute-done.2 = f32[16,2,8,256]{3,2,1,0:T(8,128)S(1)} collective-permute-done((f32[16,2,8,256]{3,2,1,0:T(8,128)S(1)}, f32[16,2,8,256]{3,2,1,0:T(8,128)S(1)}, u32[]{:S(2)}, u32[]{:S(2)}) %collective-permute-start.2) | collective-permute-done | bytes 262176 | tf_op jit(solution)/shard_map/ppermute | solution.py:58
  134.3 1.0 fusion.3
  135.3 1.4 pad_maximum_fusion.1
  136.7 16.4 %all_to_all.54 = f32[16,1,2]{2,1,0:T(1,128)S(1)} all-to-all(f32[16,1,2]{2,1,0:T(1,128)S(1)} %broadcast_in_dim.86), channel_id=1, replica_groups=mesh['chip'=8,'core'=2,'z'=16,'xl'=2] {'chip','core'}, dimensions={0} | all-to-all | bytes 256 | tf_op jit(solution)/shard_map/all_to_all | solution.py:31
  153.2 0.6 fusion.26
  155.0 1.1 fusion.7
  156.1 1.4 pad_maximum_fusion.2
  157.5 10.1 %all_to_all.55 = f32[16,1,2]{2,1,0:T(1,128)S(1)} all-to-all(f32[16,1,2]{2,1,0:T(1,128)S(1)} %broadcast_in_dim.87), channel_id=1, replica_groups=mesh['chip'=8,'core'=2,'z'=16,'xl'=2] {'chip','core'}, dimensions={0} | all-to-all | bytes 256 | tf_op jit(solution)/shard_map/all_to_all | solution.py:31
  167.7 0.7 fusion.25
  172.2 0.2 fusion.10
  172.4 0.2 broadcast_in_dim.88
  172.6 30.0 %all_to_all.56 = bf16[8,2,256,256]{3,2,1,0:T(8,128)(2,1)S(1)} all-to-all(bf16[8,2,256,256]{3,2,1,0:T(8,128)(2,1)S(1)} %broadcast_in_dim.88), channel_id=1, replica_groups=mesh['chip'=8,'core'=2,'z'=16,'xl'=2] {'chip'}, dimensions={0} | all-to-all | bytes 4194304 | tf_op jit(solution)/shard_map/all_to_all | solution.py:24
  202.6 3.7 %collective-permute-start.3 = (bf16[8,2,256,256]{3,2,1,0:T(8,128)(2,1)S(1)}, bf16[8,2,256,256]{3,2,1,0:T(8,128)(2,1)S(1)}, u32[]{:S(2)}, u32[]{:S(2)}) collective-permute-start(bf16[8,2,256,256]{3,2,1,0:T(8,128)(2,1)S(1)} %all_to_all.56), channel_id=1, source_target_pairs={{0,32},{32,0},{1,33},{33,1},{2,34},{34,2},{3,35},{35,3},{4,36},{36... | collective-permute-start | bytes 6291464 | tf_op jit(solution)/shard_map/ppermute | solution.py:25
  206.4 3.8 %collective-permute-done.3 = bf16[8,2,256,256]{3,2,1,0:T(8,128)(2,1)S(1)} collective-permute-done((bf16[8,2,256,256]{3,2,1,0:T(8,128)(2,1)S(1)}, bf16[8,2,256,256]{3,2,1,0:T(8,128)(2,1)S(1)}, u32[]{:S(2)}, u32[]{:S(2)}) %collective-permute-start.3) | collective-permute-done | bytes 2097184 | tf_op jit(solution)/shard_map/ppermute | solution.py:25
  210.1 1.3 copy-done.5
  211.4 11.2 %shard_map.122 = f32[2,256,256]{2,1,0:T(8,128)} custom-call(s32[16]{0:T(128)} %gather_fusion.1, s32[16]{0:T(128)} %gather_fusion.2, s32[16]{0:T(128)} %compare_convert_fusion.side_ref, s32[16]{0:T(128)} %gather_fusion.3, s32[1]{0:T(128)S(6)} %copy.60.cnt_ref, bf16[16,256,256]{2,1,0:T(8,128)(2,1)} %bitcast.67, bf16[16,256,256]{2,1,0:T(8,128)(2,1)} %bitcast.69, ...), custom_call_target="tpu_custom_call" | custom-call | tf_op jit(solution)/shard_map/pallas_call | solution.py:141
  222.7 2.1 fusion.11
  224.8 1.1 copy.58
  225.9 0.1 reshape.285
  226.0 1.4 fusion.21
  227.4 1.9 collective-permute-start.4
  229.3 5.3 %collective-permute-done.4 = f32[16,4224]{1,0:T(8,128)S(1)} collective-permute-done((f32[16,4224]{1,0:T(8,128)S(1)}, f32[16,4224]{1,0:T(8,128)S(1)}, u32[]{:S(2)}, u32[]{:S(2)}) %collective-permute-start.4) | collective-permute-done | bytes 270368 | tf_op jit(solution)/shard_map/ppermute | solution.py:48
  234.7 0.9 all_to_all.40
  235.5 10.6 %all-to-all-start.6 = ((f32[16,1,4224]{2,1,0:T(1,128)}), f32[16,1,4224]{2,1,0:T(1,128)S(1)}, u32[]{:S(2)}, u32[]{:S(2)}) async-start(f32[16,1,4224]{2,1,0:T(1,128)} %all_to_all.40), calls=%async_computation.6 | async-start | bytes 540672 | tf_op jit(solution)/shard_map/all_to_all | solution.py:49
  246.2 0.1 broadcast_and_fusion
  246.9 12.4 %all-to-all-done.6 = f32[16,1,4224]{2,1,0:T(1,128)S(1)} async-done(((f32[16,1,4224]{2,1,0:T(1,128)}), f32[16,1,4224]{2,1,0:T(1,128)S(1)}, u32[]{:S(2)}, u32[]{:S(2)}) %all-to-all-start.6) | async-done | bytes 270368 | tf_op jit(solution)/shard_map/all_to_all | solution.py:49
  259.3 0.2 reduce_sum.126
  259.5 1.4 slice_add_fusion
  260.9 0.6 broadcast_in_dim.90
  261.5 9.9 %all-to-all-start.7 = ((f32[16,1,2]{2,1,0:T(1,128)}), f32[16,1,2]{2,1,0:T(1,128)S(1)}, u32[]{:S(2)}, u32[]{:S(2)}) async-start(f32[16,1,2]{2,1,0:T(1,128)} %broadcast_in_dim.90), calls=%async_computation.7 | async-start | bytes 16384 | tf_op jit(solution)/shard_map/all_to_all | solution.py:31
  271.4 0.6 add_select_fusion
  272.1 6.4 %all-to-all-done.7 = f32[16,1,2]{2,1,0:T(1,128)S(1)} async-done(((f32[16,1,2]{2,1,0:T(1,128)}), f32[16,1,2]{2,1,0:T(1,128)S(1)}, u32[]{:S(2)}, u32[]{:S(2)}) %all-to-all-start.7) | async-done | bytes 160 | tf_op jit(solution)/shard_map/all_to_all | solution.py:31
  278.5 0.6 fusion.24
  280.3 0.6 pad_maximum_fusion.3
  (43 shorter events, 0.6 us)
Async XLA Ops:
  3.5 39.3 %copy-start.8 = (s32[16]{0:T(128)S(1)}, s32[16]{0:T(128)}, u32[]{:S(2)}) copy-start(s32[16]{0:T(128)} %param.19) | copy-start | bytes 196
  3.5 41.6 %copy-start.7 = (s32[16]{0:T(128)S(1)}, s32[16]{0:T(128)}, u32[]{:S(2)}) copy-start(s32[16]{0:T(128)} %param.20) | copy-start | bytes 196
  37.0 13.7 %copy-start = (bf16[8,2,256,256]{3,2,1,0:T(8,128)(2,1)}, bf16[8,2,256,256]{3,2,1,0:T(8,128)(2,1)S(1)}, u32[]{:S(2)}) copy-start(bf16[8,2,256,256]{3,2,1,0:T(8,128)(2,1)S(1)} %all_to_all.51) | copy-start | bytes 6291460
  37.0 13.7 %collective-permute-start = (bf16[8,2,256,256]{3,2,1,0:T(8,128)(2,1)S(1)}, bf16[8,2,256,256]{3,2,1,0:T(8,128)(2,1)}, u32[]{:S(2)}, u32[]{:S(2)}) collective-permute-start(bf16[8,2,256,256]{3,2,1,0:T(8,128)(2,1)S(1)} %all_to_all.51), channel_id=1, source_target_pairs={{0,32},{32,0},{1,33},{33,1},{2,34},{34,2},{3,35},{35,3},{4,36},{36... | collective-permute-start | bytes 6291464 | tf_op jit(solution)/shard_map/ppermute | solution.py:25
  63.2 7.2 %collective-permute-start.1 = (f32[16,4224]{1,0:T(8,128)S(1)}, f32[16,4224]{1,0:T(8,128)S(1)}, u32[]{:S(2)}, u32[]{:S(2)}) collective-permute-start(f32[16,4224]{1,0:T(8,128)S(1)} %fusion.15), channel_id=1, source_target_pairs={{0,1},{1,0},{2,3},{3,2},{4,5},{5,4},{6,7},{7,6},{8,9},{9,8},{10,11... | collective-permute-start | bytes 811016 | tf_op jit(solution)/shard_map/ppermute | solution.py:48
  65.1 69.1 %copy-start.2 = (bf16[2,256,256]{2,1,0:T(8,128)(2,1)S(1)}, bf16[2,256,256]{2,1,0:T(8,128)(2,1)}, u32[]{:S(2)}) copy-start(bf16[2,256,256]{2,1,0:T(8,128)(2,1)} %param.14) | copy-start | bytes 786436
  65.2 69.1 %copy-start.3 = (bf16[2,256,256]{2,1,0:T(8,128)(2,1)S(1)}, bf16[2,256,256]{2,1,0:T(8,128)(2,1)}, u32[]{:S(2)}) copy-start(bf16[2,256,256]{2,1,0:T(8,128)(2,1)} %param.15) | copy-start | bytes 786436
  70.5 84.5 %copy-start.6 = (bf16[2,256,256]{2,1,0:T(8,128)(2,1)S(1)}, bf16[2,256,256]{2,1,0:T(8,128)(2,1)}, u32[]{:S(2)}) copy-start(bf16[2,256,256]{2,1,0:T(8,128)(2,1)} %param.16) | copy-start | bytes 786436
  127.1 7.1 %collective-permute-start.2 = (f32[16,2,8,256]{3,2,1,0:T(8,128)S(1)}, f32[16,2,8,256]{3,2,1,0:T(8,128)S(1)}, u32[]{:S(2)}, u32[]{:S(2)}) collective-permute-start(f32[16,2,8,256]{3,2,1,0:T(8,128)S(1)} %all_to_all.53), channel_id=1, source_target_pairs={{0,1},{1,0},{2,3},{3,2},{4,5},{5,4},{6,7},{7,6},{8,9},{9,8},{10,11... | collective-permute-start | bytes 786440 | tf_op jit(solution)/shard_map/ppermute | solution.py:58
  172.4 99.0 %copy-start.4 = (bf16[2,256,256]{2,1,0:T(8,128)(2,1)}, bf16[2,256,256]{2,1,0:T(8,128)(2,1)S(1)}, u32[]{:S(2)}) copy-start(bf16[2,256,256]{2,1,0:T(8,128)(2,1)S(1)} %fusion.10) | copy-start | bytes 786436
  202.6 8.8 %copy-start.1 = (bf16[8,2,256,256]{3,2,1,0:T(8,128)(2,1)}, bf16[8,2,256,256]{3,2,1,0:T(8,128)(2,1)S(1)}, u32[]{:S(2)}) copy-start(bf16[8,2,256,256]{3,2,1,0:T(8,128)(2,1)S(1)} %all_to_all.56) | copy-start | bytes 6291460
  202.6 7.5 %collective-permute-start.3 = (bf16[8,2,256,256]{3,2,1,0:T(8,128)(2,1)S(1)}, bf16[8,2,256,256]{3,2,1,0:T(8,128)(2,1)S(1)}, u32[]{:S(2)}, u32[]{:S(2)}) collective-permute-start(bf16[8,2,256,256]{3,2,1,0:T(8,128)(2,1)S(1)} %all_to_all.56), channel_id=1, source_target_pairs={{0,32},{32,0},{1,33},{33,1},{2,34},{34,2},{3,35},{35,3},{4,36},{36... | collective-permute-start | bytes 6291464 | tf_op jit(solution)/shard_map/ppermute | solution.py:25
  210.1 1.3 copy-start.5
  227.4 7.2 %collective-permute-start.4 = (f32[16,4224]{1,0:T(8,128)S(1)}, f32[16,4224]{1,0:T(8,128)S(1)}, u32[]{:S(2)}, u32[]{:S(2)}) collective-permute-start(f32[16,4224]{1,0:T(8,128)S(1)} %dynamic-slice_bitcast_fusion), channel_id=1, source_target_pairs={{0,1},{1,0},{2,3},{3,2},{4,5},{5,4},{6,7},{7,6},{8,9},{9,8},{10,11... | collective-permute-start | bytes 811016 | tf_op jit(solution)/shard_map/ppermute | solution.py:48
  235.5 23.8 %all-to-all-start.6 = ((f32[16,1,4224]{2,1,0:T(1,128)}), f32[16,1,4224]{2,1,0:T(1,128)S(1)}, u32[]{:S(2)}, u32[]{:S(2)}) async-start(f32[16,1,4224]{2,1,0:T(1,128)} %all_to_all.40), calls=%async_computation.6 | async-start | bytes 540672 | tf_op jit(solution)/shard_map/all_to_all | solution.py:49
  261.5 17.0 %all-to-all-start.7 = ((f32[16,1,2]{2,1,0:T(1,128)}), f32[16,1,2]{2,1,0:T(1,128)S(1)}, u32[]{:S(2)}, u32[]{:S(2)}) async-start(f32[16,1,2]{2,1,0:T(1,128)} %broadcast_in_dim.90), calls=%async_computation.7 | async-start | bytes 16384 | tf_op jit(solution)/shard_map/all_to_all | solution.py:31

commit v6 on v5

--- a/solution.py
+++ b/solution.py
@@ -70,8 +70,10 @@
     def _():
         o_ref[...] = jnp.zeros_like(o_ref)
 
-    def add_pair(s_ref):
-        middle = jnp.dot(l_ref[0], s_ref[0], preferred_element_type=jnp.float32)
+    @pl.when(k < cnt_ref[0])
+    def _():
+        source = jnp.where(side_ref[k] == 0, a_ref[0], b_ref[0])
+        middle = jnp.dot(l_ref[0], source, preferred_element_type=jnp.float32)
         high = middle.astype(jnp.bfloat16)
         low = (middle - high.astype(jnp.float32)).astype(jnp.bfloat16)
         right = r_ref[0]
@@ -80,16 +82,6 @@
         )
         t = tgt_ref[k]
         o_ref[t] = o_ref[t] + contribution
-
-    live = k < cnt_ref[0]
-
-    @pl.when(live & (side_ref[k] == 0))
-    def _():
-        add_pair(a_ref)
-
-    @pl.when(live & (side_ref[k] != 0))
-    def _():
-        add_pair(b_ref)
 
 
 def carried(index, used):
@@ -202,14 +194,19 @@
         extra = jnp.stack([jnp.sum(w * partial_value) for w in weights] or [jnp.float32(0)])
         return reduce_scatter_rows(partial_value, extra, n_z)
 
-    pair_rows, _ = apply_partial(own_vector, ())
+    pair_rows, first_terms = apply_partial(own_vector, (vector_view,))
+    norm_vector, correlation = reduce_vector(
+        jnp.stack(
+            [
+                jnp.sum(vector_view * vector_view),
+                jnp.sum(vector_view * diag_view * vector_view) + first_terms[0],
+            ]
+        ),
+        SEC,
+        n_sec,
+    )
     pairs_first = gather_rows(pair_rows, n_z)
     sigma_first = jnp.where(own_mask, diag_view * vector_view + pairs_first, 0.0)
-    norm_vector, correlation = reduce_vector(
-        jnp.stack([jnp.sum(vector_view * vector_view), jnp.sum(vector_view * sigma_first)]),
-        SEC,
-        n_sec,
-    )
     rayleigh = correlation / norm_vector
     residual = sigma_first - rayleigh * vector_view
     scaled = scale_view * residual

time: 282 us -> 274 us (0.972)
  blocking collectives: 146 us -> 127 us
  starting transfers between devices: 36.2 us -> 49.8 us
  Pallas kernels: 22.5 us -> 9.03 us
  waiting for transfers between devices: 37.1 us -> 44.9 us
    all_to_all x2 -> x1, blocking collectives: 26.5 us -> 10.1 us  [ordered_gather(): return lax.all_to_all(spread, axis_name, 0, 0, tiled=True)]
    all_to_all x1 -> x2, starting transfers between devices: 9.91 us -> 25 us  [ordered_gather(): return lax.all_to_all(spread, axis_name, 0, 0, tiled=True)]
    pallas_call x2, Pallas kernels: 22.5 us -> 9.03 us  [pair_partial(): pl.pallas_call(pair_kernel, grid_spec=grid_spec, out_shape=jax.ShapeDtype...]
    all_to_all x1 -> x2, waiting for transfers between devices: 6.43 us -> 13.3 us  [ordered_gather(): return lax.all_to_all(spread, axis_name, 0, 0, tiled=True)]
    ppermute x2, waiting for transfers between devices: 10.5 us -> 15.9 us  [reduce_scatter_rows(): pair_sum = mine + lax.ppermute(other, 'xl', [(0, 1), (1, 0)])]
    ppermute x1, waiting for transfers between devices: 3.95 us -> 0.01 us  [gather_rows(): other = lax.ppermute(same, 'xl', [(0, 1), (1, 0)])]
  transfers between devices with their start and end apart: 7 -> 8, of which waited for: 6 -> 6; matrix products, arithmetic and copies ran while one was open for 3% -> 4% of each run, Pallas kernels for 0% -> 0%
where the time goes in v6:
time: 274 us; the launch traced here: 273 us
  blocking collectives  127 us (46%)
  starting transfers between devices  49.8 us (18%)
  waiting for transfers between devices  44.9 us (16%)
  other arithmetic  16.6 us (6%)
  local copies, waits for them, and re-layouts  14.8 us (5%)
  between operations  10.3 us (4%)
  Pallas kernels  9.03 us (3%)
    all_to_all x2, blocking collectives, gather_sec(): same_core = lax.all_to_all(spread, 'chip', 0, 0, tiled=True)  63.5 us
    all_to_all x1, blocking collectives, reduce_scatter_rows(): total = jnp.sum(lax.all_to_all(pair_sum, 'z', 0, 0, tiled=True), axis=0)  30.1 us
    all_to_all x2, starting transfers between devices, ordered_gather(): return lax.all_to_all(spread, axis_name, 0, 0, tiled=True)  25 us
    all_to_all x1, blocking collectives, gather_rows(): same = lax.all_to_all(spread, 'z', 0, 0, tiled=True)  23.7 us
    ppermute x2, waiting for transfers between devices, reduce_scatter_rows(): pair_sum = mine + lax.ppermute(other, 'xl', [(0, 1), (1, 0)])  15.9 us
    all_to_all x2, waiting for transfers between devices, ordered_gather(): return lax.all_to_all(spread, axis_name, 0, 0, tiled=True)  13.3 us
    all_to_all x1, waiting for transfers between devices, reduce_scatter_rows(): total = jnp.sum(lax.all_to_all(pair_sum, 'z', 0, 0, tiled=True), axis=0)  11.9 us
    all_to_all x1, blocking collectives, ordered_gather(): return lax.all_to_all(spread, axis_name, 0, 0, tiled=True)  10.1 us
  transfers between devices with their start and end apart: 8, of which 6 were waited for; matrix products, arithmetic and copies ran while one was open for 4% of the time, Pallas kernels for 0%

profile of v6, /device:TPU:1, one launch (start us, length us, event | category | flops | bytes accessed | tf_op | source)
XLA Modules:
  0.0 272.8 jit_solution(13460997105137560601)
XLA Ops:
  0.6 0.7 dynamic_slice.28
  1.4 0.7 dynamic_slice.29
  2.2 1.1 and_select_fusion
  3.3 0.2 broadcast_in_dim.44
  3.5 33.5 %all_to_all.51 = bf16[8,2,256,256]{3,2,1,0:T(8,128)(2,1)S(1)} all-to-all(bf16[8,2,256,256]{3,2,1,0:T(8,128)(2,1)S(1)} %broadcast_in_dim.44), channel_id=1, replica_groups=mesh['chip'=8,'core'=2,'z'=16,'xl'=2] {'chip'}, dimensions={0} | all-to-all | bytes 4194304 | tf_op jit(solution)/shard_map/all_to_all | solution.py:24
  37.0 5.1 %collective-permute-start = (bf16[8,2,256,256]{3,2,1,0:T(8,128)(2,1)S(1)}, bf16[8,2,256,256]{3,2,1,0:T(8,128)(2,1)}, u32[]{:S(2)}, u32[]{:S(2)}) collective-permute-start(bf16[8,2,256,256]{3,2,1,0:T(8,128)(2,1)S(1)} %all_to_all.51), channel_id=1, source_target_pairs={{0,32},{32,0},{1,33},{33,1},{2,34},{34,2},{3,35},{35,3},{4,36},{36... | collective-permute-start | bytes 6291464 | tf_op jit(solution)/shard_map/ppermute | solution.py:25
  42.8 0.7 gather_fusion
  43.5 0.1 copy.34
  43.5 0.1 copy.33
  43.7 0.7 compare_reduce_fusion
  44.4 0.8 fusion.15
  45.1 1.2 gather_fusion.2
  46.4 0.7 compare_reduce_fusion.1
  47.0 0.8 fusion.14
  47.8 1.2 gather_fusion.1
  49.0 1.2 gather_fusion.3
  50.1 0.6 compare_convert_fusion.side_ref
  50.7 4.5 %shard_map.121 = f32[2,256,256]{2,1,0:T(8,128)} custom-call(s32[16]{0:T(128)} %gather_fusion.1, s32[16]{0:T(128)} %gather_fusion.2, s32[16]{0:T(128)} %compare_convert_fusion.side_ref, s32[16]{0:T(128)} %gather_fusion.3, s32[1]{0:T(128)S(6)} %copy.56.cnt_ref, bf16[16,256,256]{2,1,0:T(8,128)(2,1)} %bitcast.62, bf16[16,256,256]{2,1,0:T(8,128)(2,1)} %bitcast.5.b_ref, ...), custom_call_target="tpu_custom_call" | custom-call | tf_op jit(solution)/shard_map/pallas_call | solution.py:133
  55.2 1.2 copy.55
  56.4 0.1 reshape.283
  56.6 1.0 fusion.4
  57.6 0.6 pad_select_fusion
  58.4 2.6 collective-permute-start.1
  61.0 7.8 %collective-permute-done.1 = f32[16,4224]{1,0:T(8,128)S(1)} collective-permute-done((f32[16,4224]{1,0:T(8,128)S(1)}, f32[16,4224]{1,0:T(8,128)S(1)}, u32[]{:S(2)}, u32[]{:S(2)}) %collective-permute-start.1) | collective-permute-done | bytes 270368 | tf_op jit(solution)/shard_map/ppermute | solution.py:48
  68.9 0.2 all_to_all.34
  69.1 30.1 %all_to_all.52 = f32[16,1,4224]{2,1,0:T(1,128)S(1)} all-to-all(f32[16,1,4224]{2,1,0:T(1,128)S(1)} %all_to_all.34), channel_id=1, replica_groups=mesh['chip'=8,'core'=2,'z'=16,'xl'=2] {'z'}, dimensions={0} | all-to-all | bytes 540672 | tf_op jit(solution)/shard_map/all_to_all | solution.py:49
  99.2 0.2 reduce_sum.127
  99.4 23.7 %all_to_all.53 = f32[16,2,8,256]{3,2,1,0:T(8,128)S(1)} all-to-all(f32[16,2,8,256]{3,2,1,0:T(8,128)S(1)} %broadcast_in_dim.84), channel_id=1, replica_groups=mesh['chip'=8,'core'=2,'z'=16,'xl'=2] {'z'}, dimensions={0} | all-to-all | bytes 524288 | tf_op jit(solution)/shard_map/all_to_all | solution.py:57
  123.1 1.9 collective-permute-start.2
  125.0 0.5 slice.67
  126.9 0.7 pad_maximum_fusion.2
  127.6 0.6 broadcast_in_dim.86
  128.2 13.8 %all-to-all-start.3 = ((f32[16,1,2]{2,1,0:T(1,128)}), f32[16,1,2]{2,1,0:T(1,128)S(1)}, u32[]{:S(2)}, u32[]{:S(2)}) async-start(f32[16,1,2]{2,1,0:T(1,128)} %broadcast_in_dim.86), calls=%async_computation.3 | async-start | bytes 16384 | tf_op jit(solution)/shard_map/all_to_all | solution.py:31
  142.0 6.9 %all-to-all-done.3 = f32[16,1,2]{2,1,0:T(1,128)S(1)} async-done(((f32[16,1,2]{2,1,0:T(1,128)}), f32[16,1,2]{2,1,0:T(1,128)S(1)}, u32[]{:S(2)}, u32[]{:S(2)}) %all-to-all-start.3) | async-done | bytes 160 | tf_op jit(solution)/shard_map/all_to_all | solution.py:31
  148.9 0.6 fusion.24
  150.9 1.1 fusion.8
  152.0 1.4 pad_maximum_fusion.3
  153.4 10.1 %all_to_all.54 = f32[16,1,2]{2,1,0:T(1,128)S(1)} all-to-all(f32[16,1,2]{2,1,0:T(1,128)S(1)} %broadcast_in_dim.87), channel_id=1, replica_groups=mesh['chip'=8,'core'=2,'z'=16,'xl'=2] {'chip','core'}, dimensions={0} | all-to-all | bytes 256 | tf_op jit(solution)/shard_map/all_to_all | solution.py:31
  163.6 0.7 fusion.23
  168.3 0.2 fusion.11
  168.5 0.2 broadcast_in_dim.88
  168.7 30.0 %all_to_all.55 = bf16[8,2,256,256]{3,2,1,0:T(8,128)(2,1)S(1)} all-to-all(bf16[8,2,256,256]{3,2,1,0:T(8,128)(2,1)S(1)} %broadcast_in_dim.88), channel_id=1, replica_groups=mesh['chip'=8,'core'=2,'z'=16,'xl'=2] {'chip'}, dimensions={0} | all-to-all | bytes 4194304 | tf_op jit(solution)/shard_map/all_to_all | solution.py:24
  198.7 3.7 %collective-permute-start.3 = (bf16[8,2,256,256]{3,2,1,0:T(8,128)(2,1)S(1)}, bf16[8,2,256,256]{3,2,1,0:T(8,128)(2,1)S(1)}, u32[]{:S(2)}, u32[]{:S(2)}) collective-permute-start(bf16[8,2,256,256]{3,2,1,0:T(8,128)(2,1)S(1)} %all_to_all.55), channel_id=1, source_target_pairs={{0,32},{32,0},{1,33},{33,1},{2,34},{34,2},{3,35},{35,3},{4,36},{36... | collective-permute-start | bytes 6291464 | tf_op jit(solution)/shard_map/ppermute | solution.py:25
  202.5 3.8 %collective-permute-done.3 = bf16[8,2,256,256]{3,2,1,0:T(8,128)(2,1)S(1)} collective-permute-done((bf16[8,2,256,256]{3,2,1,0:T(8,128)(2,1)S(1)}, bf16[8,2,256,256]{3,2,1,0:T(8,128)(2,1)S(1)}, u32[]{:S(2)}, u32[]{:S(2)}) %collective-permute-start.3) | collective-permute-done | bytes 2097184 | tf_op jit(solution)/shard_map/ppermute | solution.py:25
  206.2 1.3 copy-done.6
  207.5 4.5 %shard_map.122 = f32[2,256,256]{2,1,0:T(8,128)} custom-call(s32[16]{0:T(128)} %gather_fusion.1, s32[16]{0:T(128)} %gather_fusion.2, s32[16]{0:T(128)} %compare_convert_fusion.side_ref, s32[16]{0:T(128)} %gather_fusion.3, s32[1]{0:T(128)S(6)} %copy.56.cnt_ref, bf16[16,256,256]{2,1,0:T(8,128)(2,1)} %bitcast.63, bf16[16,256,256]{2,1,0:T(8,128)(2,1)} %bitcast.66, ...), custom_call_target="tpu_custom_call" | custom-call | tf_op jit(solution)/shard_map/pallas_call | solution.py:133
  212.0 2.1 fusion.12
  214.1 1.1 copy.54
  215.2 0.1 reshape.289
  215.3 1.4 fusion.19
  216.8 1.9 collective-permute-start.4
  218.8 8.0 %collective-permute-done.4 = f32[16,4224]{1,0:T(8,128)S(1)} collective-permute-done((f32[16,4224]{1,0:T(8,128)S(1)}, f32[16,4224]{1,0:T(8,128)S(1)}, u32[]{:S(2)}, u32[]{:S(2)}) %collective-permute-start.4) | collective-permute-done | bytes 270368 | tf_op jit(solution)/shard_map/ppermute | solution.py:48
  226.8 0.9 all_to_all.40
  227.7 9.7 %all-to-all-start.6 = ((f32[16,1,4224]{2,1,0:T(1,128)}), f32[16,1,4224]{2,1,0:T(1,128)S(1)}, u32[]{:S(2)}, u32[]{:S(2)}) async-start(f32[16,1,4224]{2,1,0:T(1,128)} %all_to_all.40), calls=%async_computation.6 | async-start | bytes 540672 | tf_op jit(solution)/shard_map/all_to_all | solution.py:49
  237.4 0.1 broadcast_and_fusion
  238.3 11.9 %all-to-all-done.6 = f32[16,1,4224]{2,1,0:T(1,128)S(1)} async-done(((f32[16,1,4224]{2,1,0:T(1,128)}), f32[16,1,4224]{2,1,0:T(1,128)S(1)}, u32[]{:S(2)}, u32[]{:S(2)}) %all-to-all-start.6) | async-done | bytes 270368 | tf_op jit(solution)/shard_map/all_to_all | solution.py:49
  250.2 0.2 reduce_sum.136
  250.4 1.3 slice_add_fusion
  251.6 0.6 broadcast_in_dim.90
  252.2 11.2 %all-to-all-start.7 = ((f32[16,1,2]{2,1,0:T(1,128)}), f32[16,1,2]{2,1,0:T(1,128)S(1)}, u32[]{:S(2)}, u32[]{:S(2)}) async-start(f32[16,1,2]{2,1,0:T(1,128)} %broadcast_in_dim.90), calls=%async_computation.7 | async-start | bytes 16384 | tf_op jit(solution)/shard_map/all_to_all | solution.py:31
  263.4 0.6 add_select_fusion
  264.0 6.4 %all-to-all-done.7 = f32[16,1,2]{2,1,0:T(1,128)S(1)} async-done(((f32[16,1,2]{2,1,0:T(1,128)}), f32[16,1,2]{2,1,0:T(1,128)S(1)}, u32[]{:S(2)}, u32[]{:S(2)}) %all-to-all-start.7) | async-done | bytes 160 | tf_op jit(solution)/shard_map/all_to_all | solution.py:31
  270.5 0.6 fusion.22
  272.2 0.6 pad_maximum_fusion.4
  (49 shorter events, 0.7 us)
Async XLA Ops:
  3.5 39.3 %copy-start.9 = (s32[16]{0:T(128)S(1)}, s32[16]{0:T(128)}, u32[]{:S(2)}) copy-start(s32[16]{0:T(128)} %param.19) | copy-start | bytes 196
  3.5 41.6 %copy-start.8 = (s32[16]{0:T(128)S(1)}, s32[16]{0:T(128)}, u32[]{:S(2)}) copy-start(s32[16]{0:T(128)} %param.20) | copy-start | bytes 196
  37.0 13.7 %copy-start = (bf16[8,2,256,256]{3,2,1,0:T(8,128)(2,1)}, bf16[8,2,256,256]{3,2,1,0:T(8,128)(2,1)S(1)}, u32[]{:S(2)}) copy-start(bf16[8,2,256,256]{3,2,1,0:T(8,128)(2,1)S(1)} %all_to_all.51) | copy-start | bytes 6291460
  37.0 13.7 %collective-permute-start = (bf16[8,2,256,256]{3,2,1,0:T(8,128)(2,1)S(1)}, bf16[8,2,256,256]{3,2,1,0:T(8,128)(2,1)}, u32[]{:S(2)}, u32[]{:S(2)}) collective-permute-start(bf16[8,2,256,256]{3,2,1,0:T(8,128)(2,1)S(1)} %all_to_all.51), channel_id=1, source_target_pairs={{0,32},{32,0},{1,33},{33,1},{2,34},{34,2},{3,35},{35,3},{4,36},{36... | collective-permute-start | bytes 6291464 | tf_op jit(solution)/shard_map/ppermute | solution.py:25
  55.2 1.3 copy-start.2
  55.2 1.3 copy-start.3
  55.2 1.3 copy-start.4
  58.3 92.6 %copy-start.7 = (bf16[2,256,256]{2,1,0:T(8,128)(2,1)S(1)}, bf16[2,256,256]{2,1,0:T(8,128)(2,1)}, u32[]{:S(2)}) copy-start(bf16[2,256,256]{2,1,0:T(8,128)(2,1)} %param.16) | copy-start | bytes 786436
  58.4 10.5 %collective-permute-start.1 = (f32[16,4224]{1,0:T(8,128)S(1)}, f32[16,4224]{1,0:T(8,128)S(1)}, u32[]{:S(2)}, u32[]{:S(2)}) collective-permute-start(f32[16,4224]{1,0:T(8,128)S(1)} %dynamic-slice_bitcast_fusion.1), channel_id=1, source_target_pairs={{0,1},{1,0},{2,3},{3,2},{4,5},{5,4},{6,7},{7,6},{8,9},{9,8},{10,11... | collective-permute-start | bytes 811016 | tf_op jit(solution)/shard_map/ppermute | solution.py:48
  123.1 27.8 %collective-permute-start.2 = (f32[16,2,8,256]{3,2,1,0:T(8,128)S(1)}, f32[16,2,8,256]{3,2,1,0:T(8,128)S(1)}, u32[]{:S(2)}, u32[]{:S(2)}) collective-permute-start(f32[16,2,8,256]{3,2,1,0:T(8,128)S(1)} %all_to_all.53), channel_id=1, source_target_pairs={{0,1},{1,0},{2,3},{3,2},{4,5},{5,4},{6,7},{7,6},{8,9},{9,8},{10,11... | collective-permute-start | bytes 786440 | tf_op jit(solution)/shard_map/ppermute | solution.py:58
  128.2 20.7 %all-to-all-start.3 = ((f32[16,1,2]{2,1,0:T(1,128)}), f32[16,1,2]{2,1,0:T(1,128)S(1)}, u32[]{:S(2)}, u32[]{:S(2)}) async-start(f32[16,1,2]{2,1,0:T(1,128)} %broadcast_in_dim.86), calls=%async_computation.3 | async-start | bytes 16384 | tf_op jit(solution)/shard_map/all_to_all | solution.py:31
  168.5 94.9 %copy-start.5 = (bf16[2,256,256]{2,1,0:T(8,128)(2,1)}, bf16[2,256,256]{2,1,0:T(8,128)(2,1)S(1)}, u32[]{:S(2)}) copy-start(bf16[2,256,256]{2,1,0:T(8,128)(2,1)S(1)} %fusion.11) | copy-start | bytes 786436
  198.7 8.8 %copy-start.1 = (bf16[8,2,256,256]{3,2,1,0:T(8,128)(2,1)}, bf16[8,2,256,256]{3,2,1,0:T(8,128)(2,1)S(1)}, u32[]{:S(2)}) copy-start(bf16[8,2,256,256]{3,2,1,0:T(8,128)(2,1)S(1)} %all_to_all.55) | copy-start | bytes 6291460
  198.7 7.5 %collective-permute-start.3 = (bf16[8,2,256,256]{3,2,1,0:T(8,128)(2,1)S(1)}, bf16[8,2,256,256]{3,2,1,0:T(8,128)(2,1)S(1)}, u32[]{:S(2)}, u32[]{:S(2)}) collective-permute-start(bf16[8,2,256,256]{3,2,1,0:T(8,128)(2,1)S(1)} %all_to_all.55), channel_id=1, source_target_pairs={{0,32},{32,0},{1,33},{33,1},{2,34},{34,2},{3,35},{35,3},{4,36},{36... | collective-permute-start | bytes 6291464 | tf_op jit(solution)/shard_map/ppermute | solution.py:25
  206.2 1.3 copy-start.6
  216.8 10.0 %collective-permute-start.4 = (f32[16,4224]{1,0:T(8,128)S(1)}, f32[16,4224]{1,0:T(8,128)S(1)}, u32[]{:S(2)}, u32[]{:S(2)}) collective-permute-start(f32[16,4224]{1,0:T(8,128)S(1)} %dynamic-slice_bitcast_fusion), channel_id=1, source_target_pairs={{0,1},{1,0},{2,3},{3,2},{4,5},{5,4},{6,7},{7,6},{8,9},{9,8},{10,11... | collective-permute-start | bytes 811016 | tf_op jit(solution)/shard_map/ppermute | solution.py:48
  227.7 22.5 %all-to-all-start.6 = ((f32[16,1,4224]{2,1,0:T(1,128)}), f32[16,1,4224]{2,1,0:T(1,128)S(1)}, u32[]{:S(2)}, u32[]{:S(2)}) async-start(f32[16,1,4224]{2,1,0:T(1,128)} %all_to_all.40), calls=%async_computation.6 | async-start | bytes 540672 | tf_op jit(solution)/shard_map/all_to_all | solution.py:49
  252.2 18.2 %all-to-all-start.7 = ((f32[16,1,2]{2,1,0:T(1,128)}), f32[16,1,2]{2,1,0:T(1,128)S(1)}, u32[]{:S(2)}, u32[]{:S(2)}) async-start(f32[16,1,2]{2,1,0:T(1,128)} %broadcast_in_dim.90), calls=%async_computation.7 | async-start | bytes 16384 | tf_op jit(solution)/shard_map/all_to_all | solution.py:31

commit v7 on v6

--- a/solution.py
+++ b/solution.py
@@ -63,33 +63,85 @@
     )
 
 
-def pair_kernel(same_idx, other_idx, side_ref, tgt_ref, cnt_ref, a_ref, b_ref, l_ref, r_ref, o_ref):
-    k = pl.program_id(0)
-
-    @pl.when(k == 0)
-    def _():
-        o_ref[...] = jnp.zeros_like(o_ref)
-
-    @pl.when(k < cnt_ref[0])
-    def _():
-        source = jnp.where(side_ref[k] == 0, a_ref[0], b_ref[0])
-        middle = jnp.dot(l_ref[0], source, preferred_element_type=jnp.float32)
+DEPTH = 3
+
+
+def pair_kernel_dma(src_ref, side_ref, tgt_ref, cnt_ref, a_hbm, b_hbm, l_hbm, r_hbm, o_ref,
+                    s_buf, l_buf, r_buf, sems):
+    slots = l_hbm.shape[0]
+    nbuf = s_buf.shape[0]
+    count = jnp.clip(cnt_ref[0], 0, slots)
+
+    def copies(k, slot):
+        index = src_ref[k]
+        from_a = pltpu.make_async_copy(a_hbm.at[index], s_buf.at[slot], sems.at[0, slot])
+        from_b = pltpu.make_async_copy(b_hbm.at[index], s_buf.at[slot], sems.at[0, slot])
+        left = pltpu.make_async_copy(l_hbm.at[k], l_buf.at[slot], sems.at[1, slot])
+        right = pltpu.make_async_copy(r_hbm.at[k], r_buf.at[slot], sems.at[2, slot])
+        return from_a, from_b, left, right
+
+    def start(k):
+        slot = k % nbuf
+        from_a, from_b, left, right = copies(k, slot)
+
+        @pl.when(side_ref[k] == 0)
+        def _():
+            from_a.start()
+
+        @pl.when(side_ref[k] != 0)
+        def _():
+            from_b.start()
+
+        left.start()
+        right.start()
+
+    o_ref[...] = jnp.zeros_like(o_ref)
+    for k in range(DEPTH):
+        @pl.when(k < count)
+        def _():
+            start(k)
+
+    def body(k, carry):
+        slot = k % nbuf
+        pltpu.make_async_copy(a_hbm.at[0], s_buf.at[slot], sems.at[0, slot]).wait()
+        pltpu.make_async_copy(l_hbm.at[0], l_buf.at[slot], sems.at[1, slot]).wait()
+        pltpu.make_async_copy(r_hbm.at[0], r_buf.at[slot], sems.at[2, slot]).wait()
+
+        @pl.when(k + DEPTH < count)
+        def _():
+            start(k + DEPTH)
+
+        middle = jnp.dot(l_buf[slot], s_buf[slot], preferred_element_type=jnp.float32)
         high = middle.astype(jnp.bfloat16)
         low = (middle - high.astype(jnp.float32)).astype(jnp.bfloat16)
-        right = r_ref[0]
-        contribution = jnp.dot(high, right, preferred_element_type=jnp.float32) + jnp.dot(
-            low, right, preferred_element_type=jnp.float32
+        rb = r_buf[slot]
+        contribution = jnp.dot(high, rb, preferred_element_type=jnp.float32) + jnp.dot(
+            low, rb, preferred_element_type=jnp.float32
         )
         t = tgt_ref[k]
         o_ref[t] = o_ref[t] + contribution
-
-
-def carried(index, used):
-    slots = index.shape[0]
-    order = jnp.arange(slots, dtype=jnp.int32)
-    last = lax.cummax(jnp.where(used, order, -1), axis=0)
-    first = jnp.argmax(used).astype(jnp.int32)
-    return index[jnp.where(last < 0, first, last)]
+        return carry
+
+    lax.fori_loop(0, count, body, 0)
+
+
+def pair_call(src, side, tgt, cnt, a, b, l, r, sector_count):
+    slots, bs, _ = l.shape
+    nbuf = DEPTH + 1
+    any_spec = pl.BlockSpec(memory_space=pl.ANY)
+    smem = pl.BlockSpec(memory_space=pltpu.SMEM)
+    return pl.pallas_call(
+        pair_kernel_dma,
+        in_specs=[smem, smem, smem, smem, any_spec, any_spec, any_spec, any_spec],
+        out_specs=pl.BlockSpec(memory_space=pltpu.VMEM),
+        out_shape=jax.ShapeDtypeStruct((sector_count, bs, bs), jnp.float32),
+        scratch_shapes=[
+            pltpu.VMEM((nbuf, bs, bs), jnp.bfloat16),
+            pltpu.VMEM((nbuf, bs, bs), jnp.bfloat16),
+            pltpu.VMEM((nbuf, bs, bs), jnp.bfloat16),
+            pltpu.SemaphoreType.DMA((3, nbuf)),
+        ],
+    )(src, side, tgt, cnt, a, b, l, r)
 
 
 def pair_partial(sources, left_blocks, right_blocks, source_index, target_index, live_count, sector_count):
@@ -98,44 +150,12 @@
     chips = same_core.shape[0]
     same_core = same_core.reshape((chips * sector_count, block_size, block_size))
     other_core = other_core.reshape((chips * sector_count, block_size, block_size))
-    last_live = jnp.clip(live_count[0] - 1, 0, slots - 1)
-    slot_ids = jnp.minimum(jnp.arange(slots, dtype=jnp.int32), last_live)
-    wanted = jnp.clip(source_index[slot_ids], 0, 2 * chips * sector_count - 1)
+    wanted = jnp.clip(source_index, 0, 2 * chips * sector_count - 1)
     side = (wanted >= chips * sector_count).astype(jnp.int32)
     within = wanted - side * chips * sector_count
-    same_idx = carried(within, side == 0)
-    other_idx = carried(within, side != 0)
-    target = target_index[slot_ids]
-
-    def same_map(k, a, b, sd, tg, cnt):
-        return (a[k], 0, 0)
-
-    def other_map(k, a, b, sd, tg, cnt):
-        return (b[k], 0, 0)
-
-    def operator_map(k, a, b, sd, tg, cnt):
-        return (jnp.minimum(k, jnp.clip(cnt[0] - 1, 0, slots - 1)), 0, 0)
-
-    block = (1, block_size, block_size)
-    grid_spec = pltpu.PrefetchScalarGridSpec(
-        num_scalar_prefetch=5,
-        grid=(slots,),
-        in_specs=[
-            pl.BlockSpec(block, same_map),
-            pl.BlockSpec(block, other_map),
-            pl.BlockSpec(block, operator_map),
-            pl.BlockSpec(block, operator_map),
-        ],
-        out_specs=pl.BlockSpec(
-            (sector_count, block_size, block_size), lambda k, a, b, sd, tg, cnt: (0, 0, 0)
-        ),
-    )
-    return pl.pallas_call(
-        pair_kernel,
-        grid_spec=grid_spec,
-        out_shape=jax.ShapeDtypeStruct((sector_count, block_size, block_size), jnp.float32),
-        compiler_params=pltpu.CompilerParams(dimension_semantics=("arbitrary",)),
-    )(same_idx, other_idx, side, target, live_count, same_core, other_core, left_blocks, right_blocks)
+    return pair_call(
+        within, side, target_index, live_count, same_core, other_core, left_blocks, right_blocks, sector_count
+    )
 
 
 def on_device(

time: 274 us -> 264 us (0.964)
  local copies, waits for them, and re-layouts: 14.8 us -> 10.4 us
  starting transfers between devices: 49.8 us -> 45.8 us
    all_to_all x2, starting transfers between devices: 25 us -> 18 us  [ordered_gather(): return lax.all_to_all(spread, axis_name, 0, 0, tiled=True)]
    gather x4 -> x0, local copies, waits for them, and re-layouts: 4.23 us -> none  [the longest x2 2.41 us: carried(): return index[jnp.where(last < 0, first, last)]]
    ppermute x2, starting transfers between devices: 4.54 us -> 8.5 us  [reduce_scatter_rows(): pair_sum = mine + lax.ppermute(other, 'xl', [(0, 1), (1, 0)])]
    all_to_all x1, blocking collectives: 30.1 us -> 33.8 us  [reduce_scatter_rows(): total = jnp.sum(lax.all_to_all(pair_sum, 'z', 0, 0, tiled=True), axis=0)]
    ppermute x2, waiting for transfers between devices: 15.9 us -> 13 us  [reduce_scatter_rows(): pair_sum = mine + lax.ppermute(other, 'xl', [(0, 1), (1, 0)])]
  transfers between devices with their start and end apart: 8 -> 8, of which waited for: 6 -> 7; matrix products, arithmetic and copies ran while one was open for 4% -> 2% of each run, Pallas kernels for 0% -> 0%
where the time goes in v7:
time: 264 us; the launch traced here: 262 us
  blocking collectives  129 us (49%)
  starting transfers between devices  45.8 us (17%)
  waiting for transfers between devices  45.3 us (17%)
  other arithmetic  14.2 us (5%)
  local copies, waits for them, and re-layouts  10.4 us (4%)
  between operations  10.3 us (4%)
  Pallas kernels  7.75 us (3%)
    all_to_all x2, blocking collectives, gather_sec(): same_core = lax.all_to_all(spread, 'chip', 0, 0, tiled=True)  63.5 us
    all_to_all x1, blocking collectives, reduce_scatter_rows(): total = jnp.sum(lax.all_to_all(pair_sum, 'z', 0, 0, tiled=True), axis=0)  33.8 us
    all_to_all x1, blocking collectives, gather_rows(): same = lax.all_to_all(spread, 'z', 0, 0, tiled=True)  21.3 us
    all_to_all x2, starting transfers between devices, ordered_gather(): return lax.all_to_all(spread, axis_name, 0, 0, tiled=True)  18 us
    all_to_all x2, waiting for transfers between devices, ordered_gather(): return lax.all_to_all(spread, axis_name, 0, 0, tiled=True)  13.4 us
    ppermute x2, waiting for transfers between devices, reduce_scatter_rows(): pair_sum = mine + lax.ppermute(other, 'xl', [(0, 1), (1, 0)])  13 us
    all_to_all x1, waiting for transfers between devices, reduce_scatter_rows(): total = jnp.sum(lax.all_to_all(pair_sum, 'z', 0, 0, tiled=True), axis=0)  13 us
    all_to_all x1, blocking collectives, ordered_gather(): return lax.all_to_all(spread, axis_name, 0, 0, tiled=True)  10.1 us
  transfers between devices with their start and end apart: 8, of which 7 were waited for; matrix products, arithmetic and copies ran while one was open for 2% of the time, Pallas kernels for 0%

profile of v7, /device:TPU:1, one launch (start us, length us, event | category | flops | bytes accessed | tf_op | source)
XLA Modules:
  0.0 262.5 jit_solution(3981820388338707685)
XLA Ops:
  0.6 0.7 dynamic_slice.28
  1.4 0.7 dynamic_slice.29
  2.1 0.1 iota_compare_fusion.1
  2.2 1.1 and_select_fusion
  3.3 0.2 broadcast_in_dim.24
  3.5 0.0 copy-start.8
  3.5 0.0 copy-start.9
  3.5 33.5 %all_to_all.51 = bf16[8,2,256,256]{3,2,1,0:T(8,128)(2,1)S(1)} all-to-all(bf16[8,2,256,256]{3,2,1,0:T(8,128)(2,1)S(1)} %broadcast_in_dim.24), channel_id=1, replica_groups=mesh['chip'=8,'core'=2,'z'=16,'xl'=2] {'chip'}, dimensions={0} | all-to-all | bytes 4194304 | tf_op jit(solution)/shard_map/all_to_all | solution.py:24
  37.0 5.1 %collective-permute-start = (bf16[8,2,256,256]{3,2,1,0:T(8,128)(2,1)S(1)}, bf16[8,2,256,256]{3,2,1,0:T(8,128)(2,1)}, u32[]{:S(2)}, u32[]{:S(2)}) collective-permute-start(bf16[8,2,256,256]{3,2,1,0:T(8,128)(2,1)S(1)} %all_to_all.51), channel_id=1, source_target_pairs={{0,32},{32,0},{1,33},{33,1},{2,34},{34,2},{3,35},{35,3},{4,36},{36... | collective-permute-start | bytes 6291464 | tf_op jit(solution)/shard_map/ppermute | solution.py:25
  42.7 0.5 compare_convert_fusion
  43.3 0.6 fusion.16
  43.9 2.1 collective-permute-done
  46.0 3.9 %shard_map.121 = f32[2,256,256]{2,1,0:T(8,128)} custom-call(s32[16]{0:T(128)} %get-tuple-element.47.src_ref, s32[16]{0:T(128)} %get-tuple-element.39.side_ref, s32[16]{0:T(128)} %get-tuple-element.48.tgt_ref, s32[1]{0:T(128)S(6)} %copy.44.cnt_ref, bf16[16,256,256]{2,1,0:T(8,128)(2,1)} %bitcast.55, bf16[16,256,256]{2,1,0:T(8,128)(2,1)} %bitcast.1.b_hbm, ...), custom_call_target="tpu_custom_call" | custom-call | tf_op jit(solution)/shard_map/pallas_call | solution.py:133
  49.8 0.0 copy-start.2
  49.9 0.0 copy-start.4
  49.9 1.2 copy.43
  51.1 0.1 reshape.177
  51.2 1.0 fusion.4
  52.2 0.6 pad_select_fusion
  53.0 0.0 copy-start.7
  53.0 3.9 %collective-permute-start.1 = (f32[16,4224]{1,0:T(8,128)S(1)}, f32[16,4224]{1,0:T(8,128)S(1)}, u32[]{:S(2)}, u32[]{:S(2)}) collective-permute-start(f32[16,4224]{1,0:T(8,128)S(1)} %dynamic-slice_bitcast_fusion.1), channel_id=1, source_target_pairs={{0,1},{1,0},{2,3},{3,2},{4,5},{5,4},{6,7},{7,6},{8,9},{9,8},{10,11... | collective-permute-start | bytes 811016 | tf_op jit(solution)/shard_map/ppermute | solution.py:48
  56.9 7.0 %collective-permute-done.1 = f32[16,4224]{1,0:T(8,128)S(1)} collective-permute-done((f32[16,4224]{1,0:T(8,128)S(1)}, f32[16,4224]{1,0:T(8,128)S(1)}, u32[]{:S(2)}, u32[]{:S(2)}) %collective-permute-start.1) | collective-permute-done | bytes 270368 | tf_op jit(solution)/shard_map/ppermute | solution.py:48
  63.9 0.2 all_to_all.34
  64.1 33.8 %all_to_all.52 = f32[16,1,4224]{2,1,0:T(1,128)S(1)} all-to-all(f32[16,1,4224]{2,1,0:T(1,128)S(1)} %all_to_all.34), channel_id=1, replica_groups=mesh['chip'=8,'core'=2,'z'=16,'xl'=2] {'z'}, dimensions={0} | all-to-all | bytes 540672 | tf_op jit(solution)/shard_map/all_to_all | solution.py:49
  97.9 0.2 reduce_sum.127
  98.2 21.3 %all_to_all.53 = f32[16,2,8,256]{3,2,1,0:T(8,128)S(1)} all-to-all(f32[16,2,8,256]{3,2,1,0:T(8,128)S(1)} %broadcast_in_dim.26), channel_id=1, replica_groups=mesh['chip'=8,'core'=2,'z'=16,'xl'=2] {'z'}, dimensions={0} | all-to-all | bytes 524288 | tf_op jit(solution)/shard_map/all_to_all | solution.py:57
  119.5 1.9 collective-permute-start.2
  121.4 0.5 slice.59
  123.3 0.7 pad_maximum_fusion.2
  124.0 0.6 broadcast_in_dim.28
  124.6 8.7 %all-to-all-start.3 = ((f32[16,1,2]{2,1,0:T(1,128)}), f32[16,1,2]{2,1,0:T(1,128)S(1)}, u32[]{:S(2)}, u32[]{:S(2)}) async-start(f32[16,1,2]{2,1,0:T(1,128)} %broadcast_in_dim.28), calls=%async_computation.3 | async-start | bytes 16384 | tf_op jit(solution)/shard_map/all_to_all | solution.py:31
  133.3 7.0 %all-to-all-done.3 = f32[16,1,2]{2,1,0:T(1,128)S(1)} async-done(((f32[16,1,2]{2,1,0:T(1,128)}), f32[16,1,2]{2,1,0:T(1,128)S(1)}, u32[]{:S(2)}, u32[]{:S(2)}) %all-to-all-start.3) | async-done | bytes 160 | tf_op jit(solution)/shard_map/all_to_all | solution.py:31
  140.4 0.6 fusion.24
  142.3 0.0 collective-permute-done.2
  142.4 1.1 fusion.8
  143.5 1.4 pad_maximum_fusion.3
  144.9 10.1 %all_to_all.54 = f32[16,1,2]{2,1,0:T(1,128)S(1)} all-to-all(f32[16,1,2]{2,1,0:T(1,128)S(1)} %broadcast_in_dim.30), channel_id=1, replica_groups=mesh['chip'=8,'core'=2,'z'=16,'xl'=2] {'chip','core'}, dimensions={0} | all-to-all | bytes 256 | tf_op jit(solution)/shard_map/all_to_all | solution.py:31
  155.0 0.7 fusion.23
  159.7 0.2 fusion.11
  159.9 0.0 copy-start.5
  160.0 0.2 broadcast_in_dim.31
  160.2 30.0 %all_to_all.55 = bf16[8,2,256,256]{3,2,1,0:T(8,128)(2,1)S(1)} all-to-all(bf16[8,2,256,256]{3,2,1,0:T(8,128)(2,1)S(1)} %broadcast_in_dim.31), channel_id=1, replica_groups=mesh['chip'=8,'core'=2,'z'=16,'xl'=2] {'chip'}, dimensions={0} | all-to-all | bytes 4194304 | tf_op jit(solution)/shard_map/all_to_all | solution.py:24
  190.2 3.7 %collective-permute-start.3 = (bf16[8,2,256,256]{3,2,1,0:T(8,128)(2,1)S(1)}, bf16[8,2,256,256]{3,2,1,0:T(8,128)(2,1)S(1)}, u32[]{:S(2)}, u32[]{:S(2)}) collective-permute-start(bf16[8,2,256,256]{3,2,1,0:T(8,128)(2,1)S(1)} %all_to_all.55), channel_id=1, source_target_pairs={{0,32},{32,0},{1,33},{33,1},{2,34},{34,2},{3,35},{35,3},{4,36},{36... | collective-permute-start | bytes 6291464 | tf_op jit(solution)/shard_map/ppermute | solution.py:25
  193.9 3.8 %collective-permute-done.3 = bf16[8,2,256,256]{3,2,1,0:T(8,128)(2,1)S(1)} collective-permute-done((bf16[8,2,256,256]{3,2,1,0:T(8,128)(2,1)S(1)}, bf16[8,2,256,256]{3,2,1,0:T(8,128)(2,1)S(1)}, u32[]{:S(2)}, u32[]{:S(2)}) %collective-permute-start.3) | collective-permute-done | bytes 2097184 | tf_op jit(solution)/shard_map/ppermute | solution.py:25
  197.7 1.3 copy-done.6
  199.0 3.9 %shard_map.122 = f32[2,256,256]{2,1,0:T(8,128)} custom-call(s32[16]{0:T(128)} %get-tuple-element.47.src_ref, s32[16]{0:T(128)} %get-tuple-element.39.side_ref, s32[16]{0:T(128)} %get-tuple-element.48.tgt_ref, s32[1]{0:T(128)S(6)} %copy.44.cnt_ref, bf16[16,256,256]{2,1,0:T(8,128)(2,1)} %bitcast.56, bf16[16,256,256]{2,1,0:T(8,128)(2,1)} %bitcast.59, ...), custom_call_target="tpu_custom_call" | custom-call | tf_op jit(solution)/shard_map/pallas_call | solution.py:133
  202.8 2.1 fusion.12
  204.9 1.1 copy.42
  206.0 0.1 reshape.183
  206.1 1.4 fusion.17
  207.6 4.6 %collective-permute-start.4 = (f32[16,4224]{1,0:T(8,128)S(1)}, f32[16,4224]{1,0:T(8,128)S(1)}, u32[]{:S(2)}, u32[]{:S(2)}) collective-permute-start(f32[16,4224]{1,0:T(8,128)S(1)} %dynamic-slice_bitcast_fusion), channel_id=1, source_target_pairs={{0,1},{1,0},{2,3},{3,2},{4,5},{5,4},{6,7},{7,6},{8,9},{9,8},{10,11... | collective-permute-start | bytes 811016 | tf_op jit(solution)/shard_map/ppermute | solution.py:48
  212.3 6.0 %collective-permute-done.4 = f32[16,4224]{1,0:T(8,128)S(1)} collective-permute-done((f32[16,4224]{1,0:T(8,128)S(1)}, f32[16,4224]{1,0:T(8,128)S(1)}, u32[]{:S(2)}, u32[]{:S(2)}) %collective-permute-start.4) | collective-permute-done | bytes 270368 | tf_op jit(solution)/shard_map/ppermute | solution.py:48
  218.3 0.9 all_to_all.40
  219.2 8.6 %all-to-all-start.6 = ((f32[16,1,4224]{2,1,0:T(1,128)}), f32[16,1,4224]{2,1,0:T(1,128)S(1)}, u32[]{:S(2)}, u32[]{:S(2)}) async-start(f32[16,1,4224]{2,1,0:T(1,128)} %all_to_all.40), calls=%async_computation.6 | async-start | bytes 540672 | tf_op jit(solution)/shard_map/all_to_all | solution.py:49
  227.9 0.1 broadcast_and_fusion
  228.7 13.0 %all-to-all-done.6 = f32[16,1,4224]{2,1,0:T(1,128)S(1)} async-done(((f32[16,1,4224]{2,1,0:T(1,128)}), f32[16,1,4224]{2,1,0:T(1,128)S(1)}, u32[]{:S(2)}, u32[]{:S(2)}) %all-to-all-start.6) | async-done | bytes 270368 | tf_op jit(solution)/shard_map/all_to_all | solution.py:49
  241.7 0.2 reduce_sum.136
  241.9 1.3 slice_add_fusion
  243.1 0.6 broadcast_in_dim.33
  243.7 9.2 %all-to-all-start.7 = ((f32[16,1,2]{2,1,0:T(1,128)}), f32[16,1,2]{2,1,0:T(1,128)S(1)}, u32[]{:S(2)}, u32[]{:S(2)}) async-start(f32[16,1,2]{2,1,0:T(1,128)} %broadcast_in_dim.33), calls=%async_computation.7 | async-start | bytes 16384 | tf_op jit(solution)/shard_map/all_to_all | solution.py:31
  253.0 0.6 add_select_fusion
  253.6 6.4 %all-to-all-done.7 = f32[16,1,2]{2,1,0:T(1,128)S(1)} async-done(((f32[16,1,2]{2,1,0:T(1,128)}), f32[16,1,2]{2,1,0:T(1,128)S(1)}, u32[]{:S(2)}, u32[]{:S(2)}) %all-to-all-start.7) | async-done | bytes 160 | tf_op jit(solution)/shard_map/all_to_all | solution.py:31
  260.1 0.6 fusion.22
  261.9 0.6 pad_maximum_fusion.4
  (31 shorter events, 0.5 us)
Async XLA Ops:
  3.5 39.2 %copy-start.8 = (s32[16]{0:T(128)S(1)}, s32[16]{0:T(128)}, u32[]{:S(2)}) copy-start(s32[16]{0:T(128)} %param.19) | copy-start | bytes 196
  3.5 39.8 %copy-start.9 = (s32[16]{0:T(128)S(1)}, s32[16]{0:T(128)}, u32[]{:S(2)}) copy-start(s32[16]{0:T(128)} %param.20) | copy-start | bytes 196
  37.0 9.0 %copy-start = (bf16[8,2,256,256]{3,2,1,0:T(8,128)(2,1)}, bf16[8,2,256,256]{3,2,1,0:T(8,128)(2,1)S(1)}, u32[]{:S(2)}) copy-start(bf16[8,2,256,256]{3,2,1,0:T(8,128)(2,1)S(1)} %all_to_all.51) | copy-start | bytes 6291460
  37.0 9.0 %collective-permute-start = (bf16[8,2,256,256]{3,2,1,0:T(8,128)(2,1)S(1)}, bf16[8,2,256,256]{3,2,1,0:T(8,128)(2,1)}, u32[]{:S(2)}, u32[]{:S(2)}) collective-permute-start(bf16[8,2,256,256]{3,2,1,0:T(8,128)(2,1)S(1)} %all_to_all.51), channel_id=1, source_target_pairs={{0,32},{32,0},{1,33},{33,1},{2,34},{34,2},{3,35},{35,3},{4,36},{36... | collective-permute-start | bytes 6291464 | tf_op jit(solution)/shard_map/ppermute | solution.py:25
  49.8 1.3 copy-start.2
  49.9 1.3 copy-start.3
  49.9 1.3 copy-start.4
  53.0 89.4 %copy-start.7 = (bf16[2,256,256]{2,1,0:T(8,128)(2,1)S(1)}, bf16[2,256,256]{2,1,0:T(8,128)(2,1)}, u32[]{:S(2)}) copy-start(bf16[2,256,256]{2,1,0:T(8,128)(2,1)} %param.16) | copy-start | bytes 786436
  53.0 10.9 %collective-permute-start.1 = (f32[16,4224]{1,0:T(8,128)S(1)}, f32[16,4224]{1,0:T(8,128)S(1)}, u32[]{:S(2)}, u32[]{:S(2)}) collective-permute-start(f32[16,4224]{1,0:T(8,128)S(1)} %dynamic-slice_bitcast_fusion.1), channel_id=1, source_target_pairs={{0,1},{1,0},{2,3},{3,2},{4,5},{5,4},{6,7},{7,6},{8,9},{9,8},{10,11... | collective-permute-start | bytes 811016 | tf_op jit(solution)/shard_map/ppermute | solution.py:48
  119.5 22.8 %collective-permute-start.2 = (f32[16,2,8,256]{3,2,1,0:T(8,128)S(1)}, f32[16,2,8,256]{3,2,1,0:T(8,128)S(1)}, u32[]{:S(2)}, u32[]{:S(2)}) collective-permute-start(f32[16,2,8,256]{3,2,1,0:T(8,128)S(1)} %all_to_all.53), channel_id=1, source_target_pairs={{0,1},{1,0},{2,3},{3,2},{4,5},{5,4},{6,7},{7,6},{8,9},{9,8},{10,11... | collective-permute-start | bytes 786440 | tf_op jit(solution)/shard_map/ppermute | solution.py:58
  124.6 15.7 %all-to-all-start.3 = ((f32[16,1,2]{2,1,0:T(1,128)}), f32[16,1,2]{2,1,0:T(1,128)S(1)}, u32[]{:S(2)}, u32[]{:S(2)}) async-start(f32[16,1,2]{2,1,0:T(1,128)} %broadcast_in_dim.28), calls=%async_computation.3 | async-start | bytes 16384 | tf_op jit(solution)/shard_map/all_to_all | solution.py:31
  159.9 93.1 %copy-start.5 = (bf16[2,256,256]{2,1,0:T(8,128)(2,1)}, bf16[2,256,256]{2,1,0:T(8,128)(2,1)S(1)}, u32[]{:S(2)}) copy-start(bf16[2,256,256]{2,1,0:T(8,128)(2,1)S(1)} %fusion.11) | copy-start | bytes 786436
  190.2 8.8 %copy-start.1 = (bf16[8,2,256,256]{3,2,1,0:T(8,128)(2,1)}, bf16[8,2,256,256]{3,2,1,0:T(8,128)(2,1)S(1)}, u32[]{:S(2)}) copy-start(bf16[8,2,256,256]{3,2,1,0:T(8,128)(2,1)S(1)} %all_to_all.55) | copy-start | bytes 6291460
  190.2 7.5 %collective-permute-start.3 = (bf16[8,2,256,256]{3,2,1,0:T(8,128)(2,1)S(1)}, bf16[8,2,256,256]{3,2,1,0:T(8,128)(2,1)S(1)}, u32[]{:S(2)}, u32[]{:S(2)}) collective-permute-start(bf16[8,2,256,256]{3,2,1,0:T(8,128)(2,1)S(1)} %all_to_all.55), channel_id=1, source_target_pairs={{0,32},{32,0},{1,33},{33,1},{2,34},{34,2},{3,35},{35,3},{4,36},{36... | collective-permute-start | bytes 6291464 | tf_op jit(solution)/shard_map/ppermute | solution.py:25
  197.7 1.3 copy-start.6
  207.6 10.6 %collective-permute-start.4 = (f32[16,4224]{1,0:T(8,128)S(1)}, f32[16,4224]{1,0:T(8,128)S(1)}, u32[]{:S(2)}, u32[]{:S(2)}) collective-permute-start(f32[16,4224]{1,0:T(8,128)S(1)} %dynamic-slice_bitcast_fusion), channel_id=1, source_target_pairs={{0,1},{1,0},{2,3},{3,2},{4,5},{5,4},{6,7},{7,6},{8,9},{9,8},{10,11... | collective-permute-start | bytes 811016 | tf_op jit(solution)/shard_map/ppermute | solution.py:48
  219.2 22.5 %all-to-all-start.6 = ((f32[16,1,4224]{2,1,0:T(1,128)}), f32[16,1,4224]{2,1,0:T(1,128)S(1)}, u32[]{:S(2)}, u32[]{:S(2)}) async-start(f32[16,1,4224]{2,1,0:T(1,128)} %all_to_all.40), calls=%async_computation.6 | async-start | bytes 540672 | tf_op jit(solution)/shard_map/all_to_all | solution.py:49
  243.7 16.3 %all-to-all-start.7 = ((f32[16,1,2]{2,1,0:T(1,128)}), f32[16,1,2]{2,1,0:T(1,128)S(1)}, u32[]{:S(2)}, u32[]{:S(2)}) async-start(f32[16,1,2]{2,1,0:T(1,128)} %broadcast_in_dim.33), calls=%async_computation.7 | async-start | bytes 16384 | tf_op jit(solution)/shard_map/all_to_all | solution.py:31

commit v8 on v7

--- a/solution.py
+++ b/solution.py
@@ -36,10 +36,8 @@
 
 
 def reduce_scatter_rows(partial_value, extra, zs):
-    sectors, rows, cols = partial_value.shape
-    share = rows // (2 * zs)
-    chunks = partial_value.reshape((sectors, zs, 2, share, cols)).transpose(2, 1, 0, 3, 4)
-    chunks = chunks.reshape((2, zs, sectors * share * cols))
+    _, _, sectors, share, cols = partial_value.shape
+    chunks = partial_value.reshape((2, zs, sectors * share * cols))
     tail = jnp.zeros((2, zs, 128), jnp.float32).at[:, :, : extra.shape[0]].set(extra)
     chunks = jnp.concatenate([chunks, tail], axis=2)
     xl = lax.axis_index("xl")
@@ -119,13 +117,16 @@
             low, rb, preferred_element_type=jnp.float32
         )
         t = tgt_ref[k]
-        o_ref[t] = o_ref[t] + contribution
+        lanes = o_ref.shape[0]
+        pieces = contribution.reshape((o_ref.shape[1], lanes) + o_ref.shape[3:])
+        for x in range(lanes):
+            o_ref[x, :, t] = o_ref[x, :, t] + pieces[:, x]
         return carry
 
     lax.fori_loop(0, count, body, 0)
 
 
-def pair_call(src, side, tgt, cnt, a, b, l, r, sector_count):
+def pair_call(src, side, tgt, cnt, a, b, l, r, sector_count, zs):
     slots, bs, _ = l.shape
     nbuf = DEPTH + 1
     any_spec = pl.BlockSpec(memory_space=pl.ANY)
@@ -134,7 +135,7 @@
         pair_kernel_dma,
         in_specs=[smem, smem, smem, smem, any_spec, any_spec, any_spec, any_spec],
         out_specs=pl.BlockSpec(memory_space=pltpu.VMEM),
-        out_shape=jax.ShapeDtypeStruct((sector_count, bs, bs), jnp.float32),
+        out_shape=jax.ShapeDtypeStruct((2, zs, sector_count, bs // (2 * zs), bs), jnp.float32),
         scratch_shapes=[
             pltpu.VMEM((nbuf, bs, bs), jnp.bfloat16),
             pltpu.VMEM((nbuf, bs, bs), jnp.bfloat16),
@@ -144,7 +145,7 @@
     )(src, side, tgt, cnt, a, b, l, r)
 
 
-def pair_partial(sources, left_blocks, right_blocks, source_index, target_index, live_count, sector_count):
+def pair_partial(sources, left_blocks, right_blocks, source_index, target_index, live_count, sector_count, zs):
     same_core, other_core = sources
     slots, block_size, _ = left_blocks.shape
     chips = same_core.shape[0]
@@ -154,7 +155,8 @@
     side = (wanted >= chips * sector_count).astype(jnp.int32)
     within = wanted - side * chips * sector_count
     return pair_call(
-        within, side, target_index, live_count, same_core, other_core, left_blocks, right_blocks, sector_count
+        within, side, target_index, live_count, same_core, other_core, left_blocks, right_blocks,
+        sector_count, zs,
     )
 
 
@@ -210,8 +212,15 @@
             target_index,
             live_count,
             sector_count,
+            n_z,
         )
-        extra = jnp.stack([jnp.sum(w * partial_value) for w in weights] or [jnp.float32(0)])
+
+        def laid_out(w):
+            return w.reshape((sector_count, n_z, 2, share_rows, block_size)).transpose(2, 1, 0, 3, 4)
+
+        extra = jnp.stack(
+            [jnp.sum(laid_out(w) * partial_value) for w in weights] or [jnp.float32(0)]
+        )
         return reduce_scatter_rows(partial_value, extra, n_z)
 
     pair_rows, first_terms = apply_partial(own_vector, (vector_view,))

time: 264 us -> 266 us (level)
  Pallas kernels: 7.75 us -> 11.2 us
  other arithmetic: 14.2 us -> 17.2 us
    all_to_all x1, blocking collectives: 33.8 us -> 29.5 us  [reduce_scatter_rows(): total = jnp.sum(lax.all_to_all(pair_sum, 'z', 0, 0, tiled=True), axis=0)]
    ppermute x2, starting transfers between devices: 8.5 us -> 4.96 us  [reduce_scatter_rows(): pair_sum = mine + lax.ppermute(other, 'xl', [(0, 1), (1, 0)])]
    pallas_call x2, Pallas kernels: 7.75 us -> 11.2 us  [pair_call(): pl.pallas_call(pair_kernel_dma, in_specs=[smem, smem, smem, smem, any_spe...]
    all_to_all x2, starting transfers between devices: 18 us -> 21.4 us  [ordered_gather(): return lax.all_to_all(spread, axis_name, 0, 0, tiled=True)]
    all_to_all x1, blocking collectives: 21.3 us -> 24.2 us  [gather_rows(): same = lax.all_to_all(spread, 'z', 0, 0, tiled=True)]
    reduce_sum x1 -> x3, other arithmetic: 2.09 us -> 4.76 us  [the longest x2 3.8 us: apply_partial(): jnp.sum(laid_out(w) * partial_value)]
where the time goes in v8:
time: 266 us; the launch traced here: 265 us
  blocking collectives  127 us (48%)
  waiting for transfers between devices  45.9 us (17%)
  starting transfers between devices  43.4 us (16%)
  other arithmetic  17.2 us (6%)
  Pallas kernels  11.2 us (4%)
  local copies, waits for them, and re-layouts  10.1 us (4%)
  between operations  10.1 us (4%)
    all_to_all x2, blocking collectives, gather_sec(): same_core = lax.all_to_all(spread, 'chip', 0, 0, tiled=True)  63.5 us
    all_to_all x1, blocking collectives, reduce_scatter_rows(): total = jnp.sum(lax.all_to_all(pair_sum, 'z', 0, 0, tiled=True), axis=0)  29.5 us
    all_to_all x1, blocking collectives, gather_rows(): same = lax.all_to_all(spread, 'z', 0, 0, tiled=True)  24.2 us
    all_to_all x2, starting transfers between devices, ordered_gather(): return lax.all_to_all(spread, axis_name, 0, 0, tiled=True)  21.4 us
    ppermute x2, waiting for transfers between devices, reduce_scatter_rows(): pair_sum = mine + lax.ppermute(other, 'xl', [(0, 1), (1, 0)])  14.7 us
    all_to_all x2, waiting for transfers between devices, ordered_gather(): return lax.all_to_all(spread, axis_name, 0, 0, tiled=True)  13.3 us
    all_to_all x1, waiting for transfers between devices, reduce_scatter_rows(): total = jnp.sum(lax.all_to_all(pair_sum, 'z', 0, 0, tiled=True), axis=0)  13 us
    pallas_call x2, Pallas kernels, pair_call(): pl.pallas_call(pair_kernel_dma, in_specs=[smem, smem, smem, smem, any_spe...  11.2 us
  transfers between devices with their start and end apart: 8, of which 7 were waited for; matrix products, arithmetic and copies ran while one was open for 2% of the time, Pallas kernels for 0%

profile of v8, /device:TPU:1, one launch (start us, length us, event | category | flops | bytes accessed | tf_op | source)
XLA Modules:
  0.0 265.3 jit_solution(18278842603909517713)
XLA Ops:
  0.6 0.7 dynamic_slice.28
  1.4 0.7 dynamic_slice.29
  2.1 0.1 iota_compare_fusion.1
  2.2 1.9 fusion
  4.1 0.2 broadcast_in_dim.24
  4.3 0.0 copy-start.6
  4.3 0.0 copy-start.7
  4.3 33.5 %all_to_all.51 = bf16[8,2,256,256]{3,2,1,0:T(8,128)(2,1)S(1)} all-to-all(bf16[8,2,256,256]{3,2,1,0:T(8,128)(2,1)S(1)} %broadcast_in_dim.24), channel_id=1, replica_groups=mesh['chip'=8,'core'=2,'z'=16,'xl'=2] {'chip'}, dimensions={0} | all-to-all | bytes 4194304 | tf_op jit(solution)/shard_map/all_to_all | solution.py:24
  37.8 5.1 %collective-permute-start = (bf16[8,2,256,256]{3,2,1,0:T(8,128)(2,1)S(1)}, bf16[8,2,256,256]{3,2,1,0:T(8,128)(2,1)}, u32[]{:S(2)}, u32[]{:S(2)}) collective-permute-start(bf16[8,2,256,256]{3,2,1,0:T(8,128)(2,1)S(1)} %all_to_all.51), channel_id=1, source_target_pairs={{0,32},{32,0},{1,33},{33,1},{2,34},{34,2},{3,35},{35,3},{4,36},{36... | collective-permute-start | bytes 6291464 | tf_op jit(solution)/shard_map/ppermute | solution.py:25
  43.6 0.0 copy-done.6
  43.6 0.6 compare_convert_fusion
  44.2 0.5 fusion.15
  44.8 2.0 collective-permute-done
  46.8 0.0 copy-done
  46.8 5.6 %shard_map.121 = f32[2,16,2,8,256]{4,3,2,1,0:T(8,128)} custom-call(s32[16]{0:T(128)} %get-tuple-element.46.src_ref, s32[16]{0:T(128)} %get-tuple-element.38.side_ref, s32[16]{0:T(128)} %get-tuple-element.47.tgt_ref, s32[1]{0:T(128)S(6)} %copy.43.cnt_ref, bf16[16,256,256]{2,1,0:T(8,128)(2,1)} %bitcast.64, bf16[16,256,256]{2,1,0:T(8,128)(2,1)} %bitcast.1.b_hbm, ...), custom_call_target="tpu_custom_call" | custom-call | tf_op jit(solution)/shard_map/pallas_call | solution.py:134
  52.4 1.1 reshape.177
  53.5 1.8 fusion.11
  55.3 0.6 pad_select_fusion
  56.1 0.0 copy-start.2
  56.1 0.0 copy-start.5
  56.1 3.0 %collective-permute-start.1 = (f32[16,4224]{1,0:T(8,128)S(1)}, f32[16,4224]{1,0:T(8,128)S(1)}, u32[]{:S(2)}, u32[]{:S(2)}) collective-permute-start(f32[16,4224]{1,0:T(8,128)S(1)} %dynamic-slice_bitcast_fusion.1), channel_id=1, source_target_pairs={{0,1},{1,0},{2,3},{3,2},{4,5},{5,4},{6,7},{7,6},{8,9},{9,8},{10,11... | collective-permute-start | bytes 811016 | tf_op jit(solution)/shard_map/ppermute | solution.py:46
  59.1 6.5 %collective-permute-done.1 = f32[16,4224]{1,0:T(8,128)S(1)} collective-permute-done((f32[16,4224]{1,0:T(8,128)S(1)}, f32[16,4224]{1,0:T(8,128)S(1)}, u32[]{:S(2)}, u32[]{:S(2)}) %collective-permute-start.1) | collective-permute-done | bytes 270368 | tf_op jit(solution)/shard_map/ppermute | solution.py:46
  65.7 0.2 all_to_all.34
  65.9 29.5 %all_to_all.52 = f32[16,1,4224]{2,1,0:T(1,128)S(1)} all-to-all(f32[16,1,4224]{2,1,0:T(1,128)S(1)} %all_to_all.34), channel_id=1, replica_groups=mesh['chip'=8,'core'=2,'z'=16,'xl'=2] {'z'}, dimensions={0} | all-to-all | bytes 540672 | tf_op jit(solution)/shard_map/all_to_all | solution.py:47
  95.4 0.2 reduce_sum.127
  95.6 24.2 %all_to_all.53 = f32[16,2,8,256]{3,2,1,0:T(8,128)S(1)} all-to-all(f32[16,2,8,256]{3,2,1,0:T(8,128)S(1)} %broadcast_in_dim.26), channel_id=1, replica_groups=mesh['chip'=8,'core'=2,'z'=16,'xl'=2] {'z'}, dimensions={0} | all-to-all | bytes 524288 | tf_op jit(solution)/shard_map/all_to_all | solution.py:55
  119.8 2.1 collective-permute-start.2
  121.9 0.5 slice.59
  123.7 0.7 pad_maximum_fusion.2
  124.4 0.6 broadcast_in_dim.28
  125.0 12.0 %all-to-all-start.3 = ((f32[16,1,2]{2,1,0:T(1,128)}), f32[16,1,2]{2,1,0:T(1,128)S(1)}, u32[]{:S(2)}, u32[]{:S(2)}) async-start(f32[16,1,2]{2,1,0:T(1,128)} %broadcast_in_dim.28), calls=%async_computation.3 | async-start | bytes 16384 | tf_op jit(solution)/shard_map/all_to_all | solution.py:31
  137.0 6.9 %all-to-all-done.3 = f32[16,1,2]{2,1,0:T(1,128)S(1)} async-done(((f32[16,1,2]{2,1,0:T(1,128)}), f32[16,1,2]{2,1,0:T(1,128)S(1)}, u32[]{:S(2)}, u32[]{:S(2)}) %all-to-all-start.3) | async-done | bytes 160 | tf_op jit(solution)/shard_map/all_to_all | solution.py:31
  144.0 0.6 fusion.24
  145.9 0.0 collective-permute-done.2
  146.0 0.9 fusion.4
  146.9 1.4 pad_maximum_fusion.3
  148.3 10.1 %all_to_all.54 = f32[16,1,2]{2,1,0:T(1,128)S(1)} all-to-all(f32[16,1,2]{2,1,0:T(1,128)S(1)} %broadcast_in_dim.30), channel_id=1, replica_groups=mesh['chip'=8,'core'=2,'z'=16,'xl'=2] {'chip','core'}, dimensions={0} | all-to-all | bytes 256 | tf_op jit(solution)/shard_map/all_to_all | solution.py:31
  158.5 0.6 fusion.23
  163.1 1.0 multiply_reduce_fusion
  164.0 0.2 broadcast_in_dim.31
  164.2 30.0 %all_to_all.55 = bf16[8,2,256,256]{3,2,1,0:T(8,128)(2,1)S(1)} all-to-all(bf16[8,2,256,256]{3,2,1,0:T(8,128)(2,1)S(1)} %broadcast_in_dim.31), channel_id=1, replica_groups=mesh['chip'=8,'core'=2,'z'=16,'xl'=2] {'chip'}, dimensions={0} | all-to-all | bytes 4194304 | tf_op jit(solution)/shard_map/all_to_all | solution.py:24
  194.2 3.7 %collective-permute-start.3 = (bf16[8,2,256,256]{3,2,1,0:T(8,128)(2,1)S(1)}, bf16[8,2,256,256]{3,2,1,0:T(8,128)(2,1)S(1)}, u32[]{:S(2)}, u32[]{:S(2)}) collective-permute-start(bf16[8,2,256,256]{3,2,1,0:T(8,128)(2,1)S(1)} %all_to_all.55), channel_id=1, source_target_pairs={{0,32},{32,0},{1,33},{33,1},{2,34},{34,2},{3,35},{35,3},{4,36},{36... | collective-permute-start | bytes 6291464 | tf_op jit(solution)/shard_map/ppermute | solution.py:25
  198.0 0.9 bitcast_convert_fusion
  198.8 2.9 %collective-permute-done.3 = bf16[8,2,256,256]{3,2,1,0:T(8,128)(2,1)S(1)} collective-permute-done((bf16[8,2,256,256]{3,2,1,0:T(8,128)(2,1)S(1)}, bf16[8,2,256,256]{3,2,1,0:T(8,128)(2,1)S(1)}, u32[]{:S(2)}, u32[]{:S(2)}) %collective-permute-start.3) | collective-permute-done | bytes 2097184 | tf_op jit(solution)/shard_map/ppermute | solution.py:25
  201.7 1.3 copy-done.4
  203.0 5.6 %shard_map.122 = f32[2,16,2,8,256]{4,3,2,1,0:T(8,128)} custom-call(s32[16]{0:T(128)} %get-tuple-element.46.src_ref, s32[16]{0:T(128)} %get-tuple-element.38.side_ref, s32[16]{0:T(128)} %get-tuple-element.47.tgt_ref, s32[1]{0:T(128)S(6)} %copy.43.cnt_ref, bf16[16,256,256]{2,1,0:T(8,128)(2,1)} %bitcast.65, bf16[16,256,256]{2,1,0:T(8,128)(2,1)} %bitcast.66, ...), custom_call_target="tpu_custom_call" | custom-call | tf_op jit(solution)/shard_map/pallas_call | solution.py:134
  208.6 1.1 reshape.183
  209.8 2.0 fusion.12
  211.8 1.3 fusion.16
  213.2 1.9 collective-permute-start.4
  215.1 8.2 %collective-permute-done.4 = f32[16,4224]{1,0:T(8,128)S(1)} collective-permute-done((f32[16,4224]{1,0:T(8,128)S(1)}, f32[16,4224]{1,0:T(8,128)S(1)}, u32[]{:S(2)}, u32[]{:S(2)}) %collective-permute-start.4) | collective-permute-done | bytes 270368 | tf_op jit(solution)/shard_map/ppermute | solution.py:46
  223.3 0.9 all_to_all.40
  224.2 6.2 %all-to-all-start.6 = ((f32[16,1,4224]{2,1,0:T(1,128)}), f32[16,1,4224]{2,1,0:T(1,128)S(1)}, u32[]{:S(2)}, u32[]{:S(2)}) async-start(f32[16,1,4224]{2,1,0:T(1,128)} %all_to_all.40), calls=%async_computation.6 | async-start | bytes 540672 | tf_op jit(solution)/shard_map/all_to_all | solution.py:47
  230.5 0.1 broadcast_and_fusion
  231.4 13.0 %all-to-all-done.6 = f32[16,1,4224]{2,1,0:T(1,128)S(1)} async-done(((f32[16,1,4224]{2,1,0:T(1,128)}), f32[16,1,4224]{2,1,0:T(1,128)S(1)}, u32[]{:S(2)}, u32[]{:S(2)}) %all-to-all-start.6) | async-done | bytes 270368 | tf_op jit(solution)/shard_map/all_to_all | solution.py:47
  244.3 0.2 reduce_sum.136
  244.5 1.4 slice_add_fusion
  245.9 0.6 broadcast_in_dim.33
  246.5 9.4 %all-to-all-start.7 = ((f32[16,1,2]{2,1,0:T(1,128)}), f32[16,1,2]{2,1,0:T(1,128)S(1)}, u32[]{:S(2)}, u32[]{:S(2)}) async-start(f32[16,1,2]{2,1,0:T(1,128)} %broadcast_in_dim.33), calls=%async_computation.7 | async-start | bytes 16384 | tf_op jit(solution)/shard_map/all_to_all | solution.py:31
  255.9 0.0 copy-done.3
  255.9 0.6 add_select_fusion
  256.5 6.4 %all-to-all-done.7 = f32[16,1,2]{2,1,0:T(1,128)S(1)} async-done(((f32[16,1,2]{2,1,0:T(1,128)}), f32[16,1,2]{2,1,0:T(1,128)S(1)}, u32[]{:S(2)}, u32[]{:S(2)}) %all-to-all-start.7) | async-done | bytes 160 | tf_op jit(solution)/shard_map/all_to_all | solution.py:31
  262.9 0.6 fusion.22
  264.7 0.6 pad_maximum_fusion.4
  (27 shorter events, 0.5 us)
Async XLA Ops:
  4.3 39.2 %copy-start.6 = (s32[16]{0:T(128)S(1)}, s32[16]{0:T(128)}, u32[]{:S(2)}) copy-start(s32[16]{0:T(128)} %param.19) | copy-start | bytes 196
  4.3 39.9 %copy-start.7 = (s32[16]{0:T(128)S(1)}, s32[16]{0:T(128)}, u32[]{:S(2)}) copy-start(s32[16]{0:T(128)} %param.20) | copy-start | bytes 196
  37.8 9.0 %copy-start = (bf16[8,2,256,256]{3,2,1,0:T(8,128)(2,1)}, bf16[8,2,256,256]{3,2,1,0:T(8,128)(2,1)S(1)}, u32[]{:S(2)}) copy-start(bf16[8,2,256,256]{3,2,1,0:T(8,128)(2,1)S(1)} %all_to_all.51) | copy-start | bytes 6291460
  37.8 9.0 %collective-permute-start = (bf16[8,2,256,256]{3,2,1,0:T(8,128)(2,1)S(1)}, bf16[8,2,256,256]{3,2,1,0:T(8,128)(2,1)}, u32[]{:S(2)}, u32[]{:S(2)}) collective-permute-start(bf16[8,2,256,256]{3,2,1,0:T(8,128)(2,1)S(1)} %all_to_all.51), channel_id=1, source_target_pairs={{0,32},{32,0},{1,33},{33,1},{2,34},{34,2},{3,35},{35,3},{4,36},{36... | collective-permute-start | bytes 6291464 | tf_op jit(solution)/shard_map/ppermute | solution.py:25
  56.1 89.9 %copy-start.2 = (bf16[2,256,256]{2,1,0:T(8,128)(2,1)S(1)}, bf16[2,256,256]{2,1,0:T(8,128)(2,1)}, u32[]{:S(2)}) copy-start(bf16[2,256,256]{2,1,0:T(8,128)(2,1)} %param.15) | copy-start | bytes 786436
  56.1 89.9 %copy-start.5 = (bf16[2,256,256]{2,1,0:T(8,128)(2,1)S(1)}, bf16[2,256,256]{2,1,0:T(8,128)(2,1)}, u32[]{:S(2)}) copy-start(bf16[2,256,256]{2,1,0:T(8,128)(2,1)} %param.16) | copy-start | bytes 786436
  56.1 9.6 %collective-permute-start.1 = (f32[16,4224]{1,0:T(8,128)S(1)}, f32[16,4224]{1,0:T(8,128)S(1)}, u32[]{:S(2)}, u32[]{:S(2)}) collective-permute-start(f32[16,4224]{1,0:T(8,128)S(1)} %dynamic-slice_bitcast_fusion.1), channel_id=1, source_target_pairs={{0,1},{1,0},{2,3},{3,2},{4,5},{5,4},{6,7},{7,6},{8,9},{9,8},{10,11... | collective-permute-start | bytes 811016 | tf_op jit(solution)/shard_map/ppermute | solution.py:46
  119.8 26.1 %collective-permute-start.2 = (f32[16,2,8,256]{3,2,1,0:T(8,128)S(1)}, f32[16,2,8,256]{3,2,1,0:T(8,128)S(1)}, u32[]{:S(2)}, u32[]{:S(2)}) collective-permute-start(f32[16,2,8,256]{3,2,1,0:T(8,128)S(1)} %all_to_all.53), channel_id=1, source_target_pairs={{0,1},{1,0},{2,3},{3,2},{4,5},{5,4},{6,7},{7,6},{8,9},{9,8},{10,11... | collective-permute-start | bytes 786440 | tf_op jit(solution)/shard_map/ppermute | solution.py:56
  125.0 18.9 %all-to-all-start.3 = ((f32[16,1,2]{2,1,0:T(1,128)}), f32[16,1,2]{2,1,0:T(1,128)S(1)}, u32[]{:S(2)}, u32[]{:S(2)}) async-start(f32[16,1,2]{2,1,0:T(1,128)} %broadcast_in_dim.28), calls=%async_computation.3 | async-start | bytes 16384 | tf_op jit(solution)/shard_map/all_to_all | solution.py:31
  164.0 91.9 %copy-start.3 = (bf16[2,256,256]{2,1,0:T(8,128)(2,1)}, bf16[2,256,256]{2,1,0:T(8,128)(2,1)S(1)}, u32[]{:S(2)}) copy-start(bf16[2,256,256]{2,1,0:T(8,128)(2,1)S(1)} %get-tuple-element.35) | copy-start | bytes 786436
  194.2 8.8 %copy-start.1 = (bf16[8,2,256,256]{3,2,1,0:T(8,128)(2,1)}, bf16[8,2,256,256]{3,2,1,0:T(8,128)(2,1)S(1)}, u32[]{:S(2)}) copy-start(bf16[8,2,256,256]{3,2,1,0:T(8,128)(2,1)S(1)} %all_to_all.55) | copy-start | bytes 6291460
  194.2 7.5 %collective-permute-start.3 = (bf16[8,2,256,256]{3,2,1,0:T(8,128)(2,1)S(1)}, bf16[8,2,256,256]{3,2,1,0:T(8,128)(2,1)S(1)}, u32[]{:S(2)}, u32[]{:S(2)}) collective-permute-start(bf16[8,2,256,256]{3,2,1,0:T(8,128)(2,1)S(1)} %all_to_all.55), channel_id=1, source_target_pairs={{0,32},{32,0},{1,33},{33,1},{2,34},{34,2},{3,35},{35,3},{4,36},{36... | collective-permute-start | bytes 6291464 | tf_op jit(solution)/shard_map/ppermute | solution.py:25
  201.7 1.3 copy-start.4
  213.2 10.1 %collective-permute-start.4 = (f32[16,4224]{1,0:T(8,128)S(1)}, f32[16,4224]{1,0:T(8,128)S(1)}, u32[]{:S(2)}, u32[]{:S(2)}) collective-permute-start(f32[16,4224]{1,0:T(8,128)S(1)} %dynamic-slice_bitcast_fusion), channel_id=1, source_target_pairs={{0,1},{1,0},{2,3},{3,2},{4,5},{5,4},{6,7},{7,6},{8,9},{9,8},{10,11... | collective-permute-start | bytes 811016 | tf_op jit(solution)/shard_map/ppermute | solution.py:46
  224.2 20.1 %all-to-all-start.6 = ((f32[16,1,4224]{2,1,0:T(1,128)}), f32[16,1,4224]{2,1,0:T(1,128)S(1)}, u32[]{:S(2)}, u32[]{:S(2)}) async-start(f32[16,1,4224]{2,1,0:T(1,128)} %all_to_all.40), calls=%async_computation.6 | async-start | bytes 540672 | tf_op jit(solution)/shard_map/all_to_all | solution.py:47
  246.5 16.4 %all-to-all-start.7 = ((f32[16,1,2]{2,1,0:T(1,128)}), f32[16,1,2]{2,1,0:T(1,128)S(1)}, u32[]{:S(2)}, u32[]{:S(2)}) async-start(f32[16,1,2]{2,1,0:T(1,128)} %broadcast_in_dim.33), calls=%async_computation.7 | async-start | bytes 16384 | tf_op jit(solution)/shard_map/all_to_all | solution.py:31

commit v9 on v7

--- a/solution.py
+++ b/solution.py
@@ -53,12 +53,12 @@
 
 def gather_rows(rows_value, zs):
     sectors, share, cols = rows_value.shape
-    spread = jnp.broadcast_to(rows_value[None], (zs,) + rows_value.shape)
-    same = lax.all_to_all(spread, "z", 0, 0, tiled=True)
-    other = lax.ppermute(same, "xl", [(0, 1), (1, 0)])
     xl = lax.axis_index("xl")
-    pair = jnp.where(xl == 0, jnp.stack([same, other], 1), jnp.stack([other, same], 1))
-    return pair.reshape((2 * zs, sectors, share, cols)).transpose(1, 0, 2, 3).reshape(
+    other = lax.ppermute(rows_value, "xl", [(0, 1), (1, 0)])
+    pair = jnp.where(xl == 0, jnp.stack([rows_value, other]), jnp.stack([other, rows_value]))
+    spread = jnp.broadcast_to(pair[None], (zs,) + pair.shape)
+    every = lax.all_to_all(spread, "z", 0, 0, tiled=True)
+    return every.reshape((2 * zs, sectors, share, cols)).transpose(1, 0, 2, 3).reshape(
         (sectors, 2 * zs * share, cols)
     )
 

time: 264 us -> 274 us (1.038)
  blocking collectives: 129 us -> 80 us
  waiting for transfers between devices: 45.3 us -> 76.2 us
  starting transfers between devices: 45.8 us -> 73.9 us
    all_to_all x2 -> x0, blocking collectives: 55.1 us -> none  [the longest x1 33.8 us: reduce_scatter_rows(): total = jnp.sum(lax.all_to_all(pair_sum, 'z', 0, 0, tiled=True), axis=0)]
    all_to_all x0 -> x1, waiting for transfers between devices: none -> 21 us  [gather_rows(): every = lax.all_to_all(spread, 'z', 0, 0, tiled=True)]
    all_to_all x1 -> x2, starting transfers between devices: 8.62 us -> 29.3 us  [reduce_scatter_rows(): total = jnp.sum(lax.all_to_all(pair_sum, 'z', 0, 0, tiled=True), axis=0)]
    all_to_all x1 -> x2, waiting for transfers between devices: 13 us -> 24.9 us  [reduce_scatter_rows(): total = jnp.sum(lax.all_to_all(pair_sum, 'z', 0, 0, tiled=True), axis=0)]
    all_to_all x1, blocking collectives: 10.1 us -> 16.5 us  [ordered_gather(): return lax.all_to_all(spread, axis_name, 0, 0, tiled=True)]
    all_to_all x0 -> x1, starting transfers between devices: none -> 5.87 us  [gather_rows(): every = lax.all_to_all(spread, 'z', 0, 0, tiled=True)]
    ppermute x2, starting transfers between devices: 8.5 us -> 4.67 us  [reduce_scatter_rows(): pair_sum = mine + lax.ppermute(other, 'xl', [(0, 1), (1, 0)])]
    all_to_all x2, starting transfers between devices: 18 us -> 21.1 us  [ordered_gather(): return lax.all_to_all(spread, axis_name, 0, 0, tiled=True)]
  transfers between devices with their start and end apart: 8 -> 10, of which waited for: 7 -> 9; matrix products, arithmetic and copies ran while one was open for 2% -> 1% of each run, Pallas kernels for 0% -> 0%
where the time goes in v9:
time: 274 us; the launch traced here: 273 us
  blocking collectives  80 us (29%)
  waiting for transfers between devices  76.2 us (28%)
  starting transfers between devices  73.9 us (27%)
  other arithmetic  14.1 us (5%)
  local copies, waits for them, and re-layouts  12 us (4%)
  between operations  10.2 us (4%)
  Pallas kernels  6.9 us (3%)
    all_to_all x2, blocking collectives, gather_sec(): same_core = lax.all_to_all(spread, 'chip', 0, 0, tiled=True)  63.5 us
    all_to_all x2, starting transfers between devices, reduce_scatter_rows(): total = jnp.sum(lax.all_to_all(pair_sum, 'z', 0, 0, tiled=True), axis=0)  29.3 us
    all_to_all x2, waiting for transfers between devices, reduce_scatter_rows(): total = jnp.sum(lax.all_to_all(pair_sum, 'z', 0, 0, tiled=True), axis=0)  24.9 us
    all_to_all x2, starting transfers between devices, ordered_gather(): return lax.all_to_all(spread, axis_name, 0, 0, tiled=True)  21.1 us
    all_to_all x1, waiting for transfers between devices, gather_rows(): every = lax.all_to_all(spread, 'z', 0, 0, tiled=True)  21 us
    all_to_all x1, blocking collectives, ordered_gather(): return lax.all_to_all(spread, axis_name, 0, 0, tiled=True)  16.5 us
    all_to_all x2, waiting for transfers between devices, ordered_gather(): return lax.all_to_all(spread, axis_name, 0, 0, tiled=True)  13.3 us
    ppermute x2, waiting for transfers between devices, reduce_scatter_rows(): pair_sum = mine + lax.ppermute(other, 'xl', [(0, 1), (1, 0)])  11 us
  transfers between devices with their start and end apart: 10, of which 9 were waited for; matrix products, arithmetic and copies ran while one was open for 1% of the time, Pallas kernels for 0%

profile of v9, /device:TPU:1, one launch (start us, length us, event | category | flops | bytes accessed | tf_op | source)
XLA Modules:
  0.0 273.2 jit_solution(13168954639811799867)
XLA Ops:
  0.6 0.7 dynamic_slice.28
  1.4 0.7 dynamic_slice.29
  2.1 0.1 iota_compare_fusion.1
  2.2 1.1 and_select_fusion
  3.3 0.2 broadcast_in_dim.22
  3.5 0.0 copy-start.8
  3.5 33.5 %all_to_all.51 = bf16[8,2,256,256]{3,2,1,0:T(8,128)(2,1)S(1)} all-to-all(bf16[8,2,256,256]{3,2,1,0:T(8,128)(2,1)S(1)} %broadcast_in_dim.22), channel_id=1, replica_groups=mesh['chip'=8,'core'=2,'z'=16,'xl'=2] {'chip'}, dimensions={0} | all-to-all | bytes 4194304 | tf_op jit(solution)/shard_map/all_to_all | solution.py:24
  37.0 5.1 %collective-permute-start = (bf16[8,2,256,256]{3,2,1,0:T(8,128)(2,1)S(1)}, bf16[8,2,256,256]{3,2,1,0:T(8,128)(2,1)}, u32[]{:S(2)}, u32[]{:S(2)}) collective-permute-start(bf16[8,2,256,256]{3,2,1,0:T(8,128)(2,1)S(1)} %all_to_all.51), channel_id=1, source_target_pairs={{0,32},{32,0},{1,33},{33,1},{2,34},{34,2},{3,35},{35,3},{4,36},{36... | collective-permute-start | bytes 6291464 | tf_op jit(solution)/shard_map/ppermute | solution.py:25
  42.7 0.5 compare_convert_fusion
  43.3 0.6 fusion.16
  43.9 2.1 collective-permute-done
  46.0 3.4 %shard_map.121 = f32[2,256,256]{2,1,0:T(8,128)} custom-call(s32[16]{0:T(128)} %get-tuple-element.47.src_ref, s32[16]{0:T(128)} %get-tuple-element.39.side_ref, s32[16]{0:T(128)} %get-tuple-element.48.tgt_ref, s32[1]{0:T(128)S(6)} %copy.47.cnt_ref, bf16[16,256,256]{2,1,0:T(8,128)(2,1)} %bitcast.54, bf16[16,256,256]{2,1,0:T(8,128)(2,1)} %bitcast.1.b_hbm, ...), custom_call_target="tpu_custom_call" | custom-call | tf_op jit(solution)/shard_map/pallas_call | solution.py:133
  49.4 0.0 copy-start.2
  49.5 1.2 copy.46
  50.7 0.1 reshape.210
  50.8 1.0 fusion.4
  51.8 0.6 pad_select_fusion
  52.5 2.5 collective-permute-start.1
  55.0 5.4 %collective-permute-done.1 = f32[16,4224]{1,0:T(8,128)S(1)} collective-permute-done((f32[16,4224]{1,0:T(8,128)S(1)}, f32[16,4224]{1,0:T(8,128)S(1)}, u32[]{:S(2)}, u32[]{:S(2)}) %collective-permute-start.1) | collective-permute-done | bytes 270368 | tf_op jit(solution)/shard_map/ppermute | solution.py:48
  60.4 0.0 copy-start.7
  60.4 0.9 all_to_all.34
  61.3 18.2 %all-to-all-start.1 = ((f32[16,1,4224]{2,1,0:T(1,128)}), f32[16,1,4224]{2,1,0:T(1,128)S(1)}, u32[]{:S(2)}, u32[]{:S(2)}) async-start(f32[16,1,4224]{2,1,0:T(1,128)} %all_to_all.34), calls=%async_computation.1 | async-start | bytes 540672 | tf_op jit(solution)/shard_map/all_to_all | solution.py:49
  79.5 12.8 %all-to-all-done.1 = f32[16,1,4224]{2,1,0:T(1,128)S(1)} async-done(((f32[16,1,4224]{2,1,0:T(1,128)}), f32[16,1,4224]{2,1,0:T(1,128)S(1)}, u32[]{:S(2)}, u32[]{:S(2)}) %all-to-all-start.1) | async-done | bytes 270368 | tf_op jit(solution)/shard_map/all_to_all | solution.py:49
  92.3 0.2 reduce_sum.127
  92.5 0.5 slice.59
  93.0 4.2 %collective-permute-start.2 = (f32[2,8,256]{2,1,0:T(8,128)S(1)}, f32[2,8,256]{2,1,0:T(8,128)S(1)}, u32[]{:S(2)}, u32[]{:S(2)}) collective-permute-start(f32[2,8,256]{2,1,0:T(8,128)S(1)} %reshape.212), channel_id=1, source_target_pairs={{0,1},{1,0},{2,3},{3,2},{4,5},{5,4},{6,7},{7,6},{8,9},{9,8},{10,11... | collective-permute-start | bytes 49160 | tf_op jit(solution)/shard_map/ppermute | solution.py:57
  98.5 0.7 pad_maximum_fusion.2
  99.2 0.6 broadcast_in_dim.25
  99.8 10.2 %all-to-all-start.3 = ((f32[16,1,2]{2,1,0:T(1,128)}), f32[16,1,2]{2,1,0:T(1,128)S(1)}, u32[]{:S(2)}, u32[]{:S(2)}) async-start(f32[16,1,2]{2,1,0:T(1,128)} %broadcast_in_dim.25), calls=%async_computation.3 | async-start | bytes 16384 | tf_op jit(solution)/shard_map/all_to_all | solution.py:31
  110.0 6.9 %all-to-all-done.3 = f32[16,1,2]{2,1,0:T(1,128)S(1)} async-done(((f32[16,1,2]{2,1,0:T(1,128)}), f32[16,1,2]{2,1,0:T(1,128)S(1)}, u32[]{:S(2)}, u32[]{:S(2)}) %all-to-all-start.3) | async-done | bytes 160 | tf_op jit(solution)/shard_map/all_to_all | solution.py:31
  117.0 0.8 broadcast_in_dim.23
  117.8 5.9 %all-to-all-start.2 = ((f32[16,2,2,8,256]{4,3,1,2,0:T(8,128)}), f32[16,2,2,8,256]{4,3,1,2,0:T(8,128)S(1)}, u32[]{:S(2)}, u32[]{:S(2)}) async-start(f32[16,2,2,8,256]{4,3,1,2,0:T(8,128)} %broadcast_in_dim.23), calls=%async_computation.2 | async-start | bytes 1048576 | tf_op jit(solution)/shard_map/all_to_all | solution.py:60
  123.7 0.6 fusion.24
  125.6 21.0 %all-to-all-done.2 = f32[16,2,2,8,256]{4,3,1,2,0:T(8,128)S(1)} async-done(((f32[16,2,2,8,256]{4,3,1,2,0:T(8,128)}), f32[16,2,2,8,256]{4,3,1,2,0:T(8,128)S(1)}, u32[]{:S(2)}, u32[]{:S(2)}) %all-to-all-start.2) | async-done | bytes 524320 | tf_op jit(solution)/shard_map/all_to_all | solution.py:60
  146.7 0.1 copy.26
  146.8 1.1 fusion.8
  147.9 1.4 pad_maximum_fusion.3
  149.3 16.5 %all_to_all.52 = f32[16,1,2]{2,1,0:T(1,128)S(1)} all-to-all(f32[16,1,2]{2,1,0:T(1,128)S(1)} %broadcast_in_dim.26), channel_id=1, replica_groups=mesh['chip'=8,'core'=2,'z'=16,'xl'=2] {'chip','core'}, dimensions={0} | all-to-all | bytes 256 | tf_op jit(solution)/shard_map/all_to_all | solution.py:31
  165.8 0.7 fusion.23
  170.5 0.2 fusion.11
  170.7 0.2 broadcast_in_dim.27
  170.9 30.0 %all_to_all.53 = bf16[8,2,256,256]{3,2,1,0:T(8,128)(2,1)S(1)} all-to-all(bf16[8,2,256,256]{3,2,1,0:T(8,128)(2,1)S(1)} %broadcast_in_dim.27), channel_id=1, replica_groups=mesh['chip'=8,'core'=2,'z'=16,'xl'=2] {'chip'}, dimensions={0} | all-to-all | bytes 4194304 | tf_op jit(solution)/shard_map/all_to_all | solution.py:24
  200.9 3.7 %collective-permute-start.3 = (bf16[8,2,256,256]{3,2,1,0:T(8,128)(2,1)S(1)}, bf16[8,2,256,256]{3,2,1,0:T(8,128)(2,1)S(1)}, u32[]{:S(2)}, u32[]{:S(2)}) collective-permute-start(bf16[8,2,256,256]{3,2,1,0:T(8,128)(2,1)S(1)} %all_to_all.53), channel_id=1, source_target_pairs={{0,32},{32,0},{1,33},{33,1},{2,34},{34,2},{3,35},{35,3},{4,36},{36... | collective-permute-start | bytes 6291464 | tf_op jit(solution)/shard_map/ppermute | solution.py:25
  204.6 3.8 %collective-permute-done.3 = bf16[8,2,256,256]{3,2,1,0:T(8,128)(2,1)S(1)} collective-permute-done((bf16[8,2,256,256]{3,2,1,0:T(8,128)(2,1)S(1)}, bf16[8,2,256,256]{3,2,1,0:T(8,128)(2,1)S(1)}, u32[]{:S(2)}, u32[]{:S(2)}) %collective-permute-start.3) | collective-permute-done | bytes 2097184 | tf_op jit(solution)/shard_map/ppermute | solution.py:25
  208.4 1.3 copy-done.6
  209.7 3.4 %shard_map.122 = f32[2,256,256]{2,1,0:T(8,128)} custom-call(s32[16]{0:T(128)} %get-tuple-element.47.src_ref, s32[16]{0:T(128)} %get-tuple-element.39.side_ref, s32[16]{0:T(128)} %get-tuple-element.48.tgt_ref, s32[1]{0:T(128)S(6)} %copy.47.cnt_ref, bf16[16,256,256]{2,1,0:T(8,128)(2,1)} %bitcast.55, bf16[16,256,256]{2,1,0:T(8,128)(2,1)} %bitcast.58, ...), custom_call_target="tpu_custom_call" | custom-call | tf_op jit(solution)/shard_map/pallas_call | solution.py:133
  213.2 2.1 fusion.12
  215.2 1.1 copy.45
  216.3 0.1 reshape.218
  216.5 1.4 fusion.17
  218.0 2.2 collective-permute-start.4
  220.1 5.7 %collective-permute-done.4 = f32[16,4224]{1,0:T(8,128)S(1)} collective-permute-done((f32[16,4224]{1,0:T(8,128)S(1)}, f32[16,4224]{1,0:T(8,128)S(1)}, u32[]{:S(2)}, u32[]{:S(2)}) %collective-permute-start.4) | collective-permute-done | bytes 270368 | tf_op jit(solution)/shard_map/ppermute | solution.py:48
  225.8 0.9 all_to_all.40
  226.7 11.1 %all-to-all-start.6 = ((f32[16,1,4224]{2,1,0:T(1,128)}), f32[16,1,4224]{2,1,0:T(1,128)S(1)}, u32[]{:S(2)}, u32[]{:S(2)}) async-start(f32[16,1,4224]{2,1,0:T(1,128)} %all_to_all.40), calls=%async_computation.6 | async-start | bytes 540672 | tf_op jit(solution)/shard_map/all_to_all | solution.py:49
  237.9 0.1 broadcast_and_fusion
  238.7 12.2 %all-to-all-done.6 = f32[16,1,4224]{2,1,0:T(1,128)S(1)} async-done(((f32[16,1,4224]{2,1,0:T(1,128)}), f32[16,1,4224]{2,1,0:T(1,128)S(1)}, u32[]{:S(2)}, u32[]{:S(2)}) %all-to-all-start.6) | async-done | bytes 270368 | tf_op jit(solution)/shard_map/all_to_all | solution.py:49
  250.9 0.2 reduce_sum.136
  251.0 1.3 slice_add_fusion
  252.3 0.6 broadcast_in_dim.29
  252.9 10.9 %all-to-all-start.7 = ((f32[16,1,2]{2,1,0:T(1,128)}), f32[16,1,2]{2,1,0:T(1,128)S(1)}, u32[]{:S(2)}, u32[]{:S(2)}) async-start(f32[16,1,2]{2,1,0:T(1,128)} %broadcast_in_dim.29), calls=%async_computation.7 | async-start | bytes 16384 | tf_op jit(solution)/shard_map/all_to_all | solution.py:31
  263.8 0.6 add_select_fusion
  264.4 6.4 %all-to-all-done.7 = f32[16,1,2]{2,1,0:T(1,128)S(1)} async-done(((f32[16,1,2]{2,1,0:T(1,128)}), f32[16,1,2]{2,1,0:T(1,128)S(1)}, u32[]{:S(2)}, u32[]{:S(2)}) %all-to-all-start.7) | async-done | bytes 160 | tf_op jit(solution)/shard_map/all_to_all | solution.py:31
  270.9 0.6 fusion.22
  272.6 0.6 pad_maximum_fusion.4
  (35 shorter events, 0.4 us)
Async XLA Ops:
  3.5 39.2 %copy-start.8 = (s32[16]{0:T(128)S(1)}, s32[16]{0:T(128)}, u32[]{:S(2)}) copy-start(s32[16]{0:T(128)} %param.19) | copy-start | bytes 196
  3.5 39.8 %copy-start.9 = (s32[16]{0:T(128)S(1)}, s32[16]{0:T(128)}, u32[]{:S(2)}) copy-start(s32[16]{0:T(128)} %param.20) | copy-start | bytes 196
  37.0 9.0 %copy-start = (bf16[8,2,256,256]{3,2,1,0:T(8,128)(2,1)}, bf16[8,2,256,256]{3,2,1,0:T(8,128)(2,1)S(1)}, u32[]{:S(2)}) copy-start(bf16[8,2,256,256]{3,2,1,0:T(8,128)(2,1)S(1)} %all_to_all.51) | copy-start | bytes 6291460
  37.0 9.0 %collective-permute-start = (bf16[8,2,256,256]{3,2,1,0:T(8,128)(2,1)S(1)}, bf16[8,2,256,256]{3,2,1,0:T(8,128)(2,1)}, u32[]{:S(2)}, u32[]{:S(2)}) collective-permute-start(bf16[8,2,256,256]{3,2,1,0:T(8,128)(2,1)S(1)} %all_to_all.51), channel_id=1, source_target_pairs={{0,32},{32,0},{1,33},{33,1},{2,34},{34,2},{3,35},{35,3},{4,36},{36... | collective-permute-start | bytes 6291464 | tf_op jit(solution)/shard_map/ppermute | solution.py:25
  49.4 1.3 copy-start.2
  49.4 1.3 copy-start.3
  49.4 1.3 copy-start.4
  52.5 7.9 %collective-permute-start.1 = (f32[16,4224]{1,0:T(8,128)S(1)}, f32[16,4224]{1,0:T(8,128)S(1)}, u32[]{:S(2)}, u32[]{:S(2)}) collective-permute-start(f32[16,4224]{1,0:T(8,128)S(1)} %dynamic-slice_bitcast_fusion.1), channel_id=1, source_target_pairs={{0,1},{1,0},{2,3},{3,2},{4,5},{5,4},{6,7},{7,6},{8,9},{9,8},{10,11... | collective-permute-start | bytes 811016 | tf_op jit(solution)/shard_map/ppermute | solution.py:48
  60.4 86.4 %copy-start.7 = (bf16[2,256,256]{2,1,0:T(8,128)(2,1)S(1)}, bf16[2,256,256]{2,1,0:T(8,128)(2,1)}, u32[]{:S(2)}) copy-start(bf16[2,256,256]{2,1,0:T(8,128)(2,1)} %param.16) | copy-start | bytes 786436
  61.3 31.0 %all-to-all-start.1 = ((f32[16,1,4224]{2,1,0:T(1,128)}), f32[16,1,4224]{2,1,0:T(1,128)S(1)}, u32[]{:S(2)}, u32[]{:S(2)}) async-start(f32[16,1,4224]{2,1,0:T(1,128)} %all_to_all.34), calls=%async_computation.1 | async-start | bytes 540672 | tf_op jit(solution)/shard_map/all_to_all | solution.py:49
  93.0 17.0 %collective-permute-start.2 = (f32[2,8,256]{2,1,0:T(8,128)S(1)}, f32[2,8,256]{2,1,0:T(8,128)S(1)}, u32[]{:S(2)}, u32[]{:S(2)}) collective-permute-start(f32[2,8,256]{2,1,0:T(8,128)S(1)} %reshape.212), channel_id=1, source_target_pairs={{0,1},{1,0},{2,3},{3,2},{4,5},{5,4},{6,7},{7,6},{8,9},{9,8},{10,11... | collective-permute-start | bytes 49160 | tf_op jit(solution)/shard_map/ppermute | solution.py:57
  99.8 17.2 %all-to-all-start.3 = ((f32[16,1,2]{2,1,0:T(1,128)}), f32[16,1,2]{2,1,0:T(1,128)S(1)}, u32[]{:S(2)}, u32[]{:S(2)}) async-start(f32[16,1,2]{2,1,0:T(1,128)} %broadcast_in_dim.25), calls=%async_computation.3 | async-start | bytes 16384 | tf_op jit(solution)/shard_map/all_to_all | solution.py:31
  117.8 28.9 %all-to-all-start.2 = ((f32[16,2,2,8,256]{4,3,1,2,0:T(8,128)}), f32[16,2,2,8,256]{4,3,1,2,0:T(8,128)S(1)}, u32[]{:S(2)}, u32[]{:S(2)}) async-start(f32[16,2,2,8,256]{4,3,1,2,0:T(8,128)} %broadcast_in_dim.23), calls=%async_computation.2 | async-start | bytes 1048576 | tf_op jit(solution)/shard_map/all_to_all | solution.py:60
  170.7 93.1 %copy-start.5 = (bf16[2,256,256]{2,1,0:T(8,128)(2,1)}, bf16[2,256,256]{2,1,0:T(8,128)(2,1)S(1)}, u32[]{:S(2)}) copy-start(bf16[2,256,256]{2,1,0:T(8,128)(2,1)S(1)} %fusion.11) | copy-start | bytes 786436
  200.9 8.8 %copy-start.1 = (bf16[8,2,256,256]{3,2,1,0:T(8,128)(2,1)}, bf16[8,2,256,256]{3,2,1,0:T(8,128)(2,1)S(1)}, u32[]{:S(2)}) copy-start(bf16[8,2,256,256]{3,2,1,0:T(8,128)(2,1)S(1)} %all_to_all.53) | copy-start | bytes 6291460
  200.9 7.5 %collective-permute-start.3 = (bf16[8,2,256,256]{3,2,1,0:T(8,128)(2,1)S(1)}, bf16[8,2,256,256]{3,2,1,0:T(8,128)(2,1)S(1)}, u32[]{:S(2)}, u32[]{:S(2)}) collective-permute-start(bf16[8,2,256,256]{3,2,1,0:T(8,128)(2,1)S(1)} %all_to_all.53), channel_id=1, source_target_pairs={{0,32},{32,0},{1,33},{33,1},{2,34},{34,2},{3,35},{35,3},{4,36},{36... | collective-permute-start | bytes 6291464 | tf_op jit(solution)/shard_map/ppermute | solution.py:25
  208.4 1.3 copy-start.6
  218.0 7.9 %collective-permute-start.4 = (f32[16,4224]{1,0:T(8,128)S(1)}, f32[16,4224]{1,0:T(8,128)S(1)}, u32[]{:S(2)}, u32[]{:S(2)}) collective-permute-start(f32[16,4224]{1,0:T(8,128)S(1)} %dynamic-slice_bitcast_fusion), channel_id=1, source_target_pairs={{0,1},{1,0},{2,3},{3,2},{4,5},{5,4},{6,7},{7,6},{8,9},{9,8},{10,11... | collective-permute-start | bytes 811016 | tf_op jit(solution)/shard_map/ppermute | solution.py:48
  226.7 24.1 %all-to-all-start.6 = ((f32[16,1,4224]{2,1,0:T(1,128)}), f32[16,1,4224]{2,1,0:T(1,128)S(1)}, u32[]{:S(2)}, u32[]{:S(2)}) async-start(f32[16,1,4224]{2,1,0:T(1,128)} %all_to_all.40), calls=%async_computation.6 | async-start | bytes 540672 | tf_op jit(solution)/shard_map/all_to_all | solution.py:49
  252.9 17.9 %all-to-all-start.7 = ((f32[16,1,2]{2,1,0:T(1,128)}), f32[16,1,2]{2,1,0:T(1,128)S(1)}, u32[]{:S(2)}, u32[]{:S(2)}) async-start(f32[16,1,2]{2,1,0:T(1,128)} %broadcast_in_dim.29), calls=%async_computation.7 | async-start | bytes 16384 | tf_op jit(solution)/shard_map/all_to_all | solution.py:31

commit v10 on v7

--- a/solution.py
+++ b/solution.py
@@ -63,7 +63,7 @@
     )
 
 
-DEPTH = 3
+DEPTH = 4
 
 
 def pair_kernel_dma(src_ref, side_ref, tgt_ref, cnt_ref, a_hbm, b_hbm, l_hbm, r_hbm, o_ref,

time: 264 us -> 264 us (level)
  blocking collectives: 129 us -> 122 us
  starting transfers between devices: 45.8 us -> 50.6 us
  Pallas kernels: 7.75 us -> 10.4 us
    all_to_all x1, blocking collectives: 33.8 us -> 26.2 us  [reduce_scatter_rows(): total = jnp.sum(lax.all_to_all(pair_sum, 'z', 0, 0, tiled=True), axis=0)]
    ppermute x1, starting transfers between devices: 1.91 us -> 7.38 us  [gather_rows(): other = lax.ppermute(same, 'xl', [(0, 1), (1, 0)])]
    all_to_all x2, starting transfers between devices: 18 us -> 22.4 us  [ordered_gather(): return lax.all_to_all(spread, axis_name, 0, 0, tiled=True)]
    ppermute x2, starting transfers between devices: 8.5 us -> 5.07 us  [reduce_scatter_rows(): pair_sum = mine + lax.ppermute(other, 'xl', [(0, 1), (1, 0)])]
where the time goes in v10:
time: 264 us; the launch traced here: 263 us
  blocking collectives  122 us (46%)
  starting transfers between devices  50.6 us (19%)
  waiting for transfers between devices  45.5 us (17%)
  other arithmetic  14.2 us (5%)
  local copies, waits for them, and re-layouts  10.4 us (4%)
  Pallas kernels  10.4 us (4%)
  between operations  10.3 us (4%)
    all_to_all x2, blocking collectives, gather_sec(): same_core = lax.all_to_all(spread, 'chip', 0, 0, tiled=True)  63.5 us
    all_to_all x1, blocking collectives, reduce_scatter_rows(): total = jnp.sum(lax.all_to_all(pair_sum, 'z', 0, 0, tiled=True), axis=0)  26.2 us
    all_to_all x2, starting transfers between devices, ordered_gather(): return lax.all_to_all(spread, axis_name, 0, 0, tiled=True)  22.4 us
    all_to_all x1, blocking collectives, gather_rows(): same = lax.all_to_all(spread, 'z', 0, 0, tiled=True)  22 us
    ppermute x2, waiting for transfers between devices, reduce_scatter_rows(): pair_sum = mine + lax.ppermute(other, 'xl', [(0, 1), (1, 0)])  14.3 us
    all_to_all x2, waiting for transfers between devices, ordered_gather(): return lax.all_to_all(spread, axis_name, 0, 0, tiled=True)  13.4 us
    all_to_all x1, waiting for transfers between devices, reduce_scatter_rows(): total = jnp.sum(lax.all_to_all(pair_sum, 'z', 0, 0, tiled=True), axis=0)  11.9 us
    pallas_call x2, Pallas kernels, pair_call(): pl.pallas_call(pair_kernel_dma, in_specs=[smem, smem, smem, smem, any_spe...  10.4 us
  transfers between devices with their start and end apart: 8, of which 7 were waited for; matrix products, arithmetic and copies ran while one was open for 2% of the time, Pallas kernels for 0%

profile of v10, /device:TPU:1, one launch (start us, length us, event | category | flops | bytes accessed | tf_op | source)
XLA Modules:
  0.0 263.1 jit_solution(5821464228834355925)
XLA Ops:
  0.6 0.7 dynamic_slice.28
  1.4 0.7 dynamic_slice.29
  2.1 0.1 iota_compare_fusion.1
  2.2 1.1 and_select_fusion
  3.3 0.2 broadcast_in_dim.24
  3.5 0.0 copy-start.8
  3.5 0.0 copy-start.9
  3.5 33.5 %all_to_all.51 = bf16[8,2,256,256]{3,2,1,0:T(8,128)(2,1)S(1)} all-to-all(bf16[8,2,256,256]{3,2,1,0:T(8,128)(2,1)S(1)} %broadcast_in_dim.24), channel_id=1, replica_groups=mesh['chip'=8,'core'=2,'z'=16,'xl'=2] {'chip'}, dimensions={0} | all-to-all | bytes 4194304 | tf_op jit(solution)/shard_map/all_to_all | solution.py:24
  37.0 5.1 %collective-permute-start = (bf16[8,2,256,256]{3,2,1,0:T(8,128)(2,1)S(1)}, bf16[8,2,256,256]{3,2,1,0:T(8,128)(2,1)}, u32[]{:S(2)}, u32[]{:S(2)}) collective-permute-start(bf16[8,2,256,256]{3,2,1,0:T(8,128)(2,1)S(1)} %all_to_all.51), channel_id=1, source_target_pairs={{0,32},{32,0},{1,33},{33,1},{2,34},{34,2},{3,35},{35,3},{4,36},{36... | collective-permute-start | bytes 6291464 | tf_op jit(solution)/shard_map/ppermute | solution.py:25
  42.7 0.5 compare_convert_fusion
  43.3 0.6 fusion.16
  43.9 2.1 collective-permute-done
  46.0 5.2 %shard_map.121 = f32[2,256,256]{2,1,0:T(8,128)} custom-call(s32[16]{0:T(128)} %get-tuple-element.47.src_ref, s32[16]{0:T(128)} %get-tuple-element.39.side_ref, s32[16]{0:T(128)} %get-tuple-element.48.tgt_ref, s32[1]{0:T(128)S(6)} %copy.44.cnt_ref, bf16[16,256,256]{2,1,0:T(8,128)(2,1)} %bitcast.55, bf16[16,256,256]{2,1,0:T(8,128)(2,1)} %bitcast.1.b_hbm, ...), custom_call_target="tpu_custom_call" | custom-call | tf_op jit(solution)/shard_map/pallas_call | solution.py:133
  51.2 0.0 copy-start.2
  51.2 0.0 copy-start.4
  51.2 1.2 copy.43
  52.4 0.1 reshape.177
  52.5 1.0 fusion.4
  53.6 0.6 pad_select_fusion
  54.3 0.0 copy-start.7
  54.3 3.0 %collective-permute-start.1 = (f32[16,4224]{1,0:T(8,128)S(1)}, f32[16,4224]{1,0:T(8,128)S(1)}, u32[]{:S(2)}, u32[]{:S(2)}) collective-permute-start(f32[16,4224]{1,0:T(8,128)S(1)} %dynamic-slice_bitcast_fusion.1), channel_id=1, source_target_pairs={{0,1},{1,0},{2,3},{3,2},{4,5},{5,4},{6,7},{7,6},{8,9},{9,8},{10,11... | collective-permute-start | bytes 811016 | tf_op jit(solution)/shard_map/ppermute | solution.py:48
  57.4 6.7 %collective-permute-done.1 = f32[16,4224]{1,0:T(8,128)S(1)} collective-permute-done((f32[16,4224]{1,0:T(8,128)S(1)}, f32[16,4224]{1,0:T(8,128)S(1)}, u32[]{:S(2)}, u32[]{:S(2)}) %collective-permute-start.1) | collective-permute-done | bytes 270368 | tf_op jit(solution)/shard_map/ppermute | solution.py:48
  64.1 0.2 all_to_all.34
  64.3 26.2 %all_to_all.52 = f32[16,1,4224]{2,1,0:T(1,128)S(1)} all-to-all(f32[16,1,4224]{2,1,0:T(1,128)S(1)} %all_to_all.34), channel_id=1, replica_groups=mesh['chip'=8,'core'=2,'z'=16,'xl'=2] {'z'}, dimensions={0} | all-to-all | bytes 540672 | tf_op jit(solution)/shard_map/all_to_all | solution.py:49
  90.5 0.2 reduce_sum.127
  90.8 22.0 %all_to_all.53 = f32[16,2,8,256]{3,2,1,0:T(8,128)S(1)} all-to-all(f32[16,2,8,256]{3,2,1,0:T(8,128)S(1)} %broadcast_in_dim.26), channel_id=1, replica_groups=mesh['chip'=8,'core'=2,'z'=16,'xl'=2] {'z'}, dimensions={0} | all-to-all | bytes 524288 | tf_op jit(solution)/shard_map/all_to_all | solution.py:57
  112.7 7.4 %collective-permute-start.2 = (f32[16,2,8,256]{3,2,1,0:T(8,128)S(1)}, f32[16,2,8,256]{3,2,1,0:T(8,128)S(1)}, u32[]{:S(2)}, u32[]{:S(2)}) collective-permute-start(f32[16,2,8,256]{3,2,1,0:T(8,128)S(1)} %all_to_all.53), channel_id=1, source_target_pairs={{0,1},{1,0},{2,3},{3,2},{4,5},{5,4},{6,7},{7,6},{8,9},{9,8},{10,11... | collective-permute-start | bytes 786440 | tf_op jit(solution)/shard_map/ppermute | solution.py:58
  120.1 0.5 slice.59
  122.0 0.7 pad_maximum_fusion.2
  122.7 0.6 broadcast_in_dim.28
  123.3 11.8 %all-to-all-start.3 = ((f32[16,1,2]{2,1,0:T(1,128)}), f32[16,1,2]{2,1,0:T(1,128)S(1)}, u32[]{:S(2)}, u32[]{:S(2)}) async-start(f32[16,1,2]{2,1,0:T(1,128)} %broadcast_in_dim.28), calls=%async_computation.3 | async-start | bytes 16384 | tf_op jit(solution)/shard_map/all_to_all | solution.py:31
  135.1 6.9 %all-to-all-done.3 = f32[16,1,2]{2,1,0:T(1,128)S(1)} async-done(((f32[16,1,2]{2,1,0:T(1,128)}), f32[16,1,2]{2,1,0:T(1,128)S(1)}, u32[]{:S(2)}, u32[]{:S(2)}) %all-to-all-start.3) | async-done | bytes 160 | tf_op jit(solution)/shard_map/all_to_all | solution.py:31
  142.1 0.6 fusion.24
  144.0 0.0 collective-permute-done.2
  144.1 1.1 fusion.8
  145.2 1.4 pad_maximum_fusion.3
  146.6 10.1 %all_to_all.54 = f32[16,1,2]{2,1,0:T(1,128)S(1)} all-to-all(f32[16,1,2]{2,1,0:T(1,128)S(1)} %broadcast_in_dim.30), channel_id=1, replica_groups=mesh['chip'=8,'core'=2,'z'=16,'xl'=2] {'chip','core'}, dimensions={0} | all-to-all | bytes 256 | tf_op jit(solution)/shard_map/all_to_all | solution.py:31
  156.7 0.7 fusion.23
  161.5 0.2 fusion.11
  161.7 0.0 copy-start.5
  161.7 0.2 broadcast_in_dim.31
  161.9 30.0 %all_to_all.55 = bf16[8,2,256,256]{3,2,1,0:T(8,128)(2,1)S(1)} all-to-all(bf16[8,2,256,256]{3,2,1,0:T(8,128)(2,1)S(1)} %broadcast_in_dim.31), channel_id=1, replica_groups=mesh['chip'=8,'core'=2,'z'=16,'xl'=2] {'chip'}, dimensions={0} | all-to-all | bytes 4194304 | tf_op jit(solution)/shard_map/all_to_all | solution.py:24
  191.9 3.7 %collective-permute-start.3 = (bf16[8,2,256,256]{3,2,1,0:T(8,128)(2,1)S(1)}, bf16[8,2,256,256]{3,2,1,0:T(8,128)(2,1)S(1)}, u32[]{:S(2)}, u32[]{:S(2)}) collective-permute-start(bf16[8,2,256,256]{3,2,1,0:T(8,128)(2,1)S(1)} %all_to_all.55), channel_id=1, source_target_pairs={{0,32},{32,0},{1,33},{33,1},{2,34},{34,2},{3,35},{35,3},{4,36},{36... | collective-permute-start | bytes 6291464 | tf_op jit(solution)/shard_map/ppermute | solution.py:25
  195.6 3.8 %collective-permute-done.3 = bf16[8,2,256,256]{3,2,1,0:T(8,128)(2,1)S(1)} collective-permute-done((bf16[8,2,256,256]{3,2,1,0:T(8,128)(2,1)S(1)}, bf16[8,2,256,256]{3,2,1,0:T(8,128)(2,1)S(1)}, u32[]{:S(2)}, u32[]{:S(2)}) %collective-permute-start.3) | collective-permute-done | bytes 2097184 | tf_op jit(solution)/shard_map/ppermute | solution.py:25
  199.4 1.3 copy-done.6
  200.7 5.2 %shard_map.122 = f32[2,256,256]{2,1,0:T(8,128)} custom-call(s32[16]{0:T(128)} %get-tuple-element.47.src_ref, s32[16]{0:T(128)} %get-tuple-element.39.side_ref, s32[16]{0:T(128)} %get-tuple-element.48.tgt_ref, s32[1]{0:T(128)S(6)} %copy.44.cnt_ref, bf16[16,256,256]{2,1,0:T(8,128)(2,1)} %bitcast.56, bf16[16,256,256]{2,1,0:T(8,128)(2,1)} %bitcast.59, ...), custom_call_target="tpu_custom_call" | custom-call | tf_op jit(solution)/shard_map/pallas_call | solution.py:133
  205.9 2.1 fusion.12
  208.0 1.1 copy.42
  209.1 0.1 reshape.183
  209.2 1.4 fusion.17
  210.7 2.0 collective-permute-start.4
  212.7 7.6 %collective-permute-done.4 = f32[16,4224]{1,0:T(8,128)S(1)} collective-permute-done((f32[16,4224]{1,0:T(8,128)S(1)}, f32[16,4224]{1,0:T(8,128)S(1)}, u32[]{:S(2)}, u32[]{:S(2)}) %collective-permute-start.4) | collective-permute-done | bytes 270368 | tf_op jit(solution)/shard_map/ppermute | solution.py:48
  220.4 0.9 all_to_all.40
  221.3 7.0 %all-to-all-start.6 = ((f32[16,1,4224]{2,1,0:T(1,128)}), f32[16,1,4224]{2,1,0:T(1,128)S(1)}, u32[]{:S(2)}, u32[]{:S(2)}) async-start(f32[16,1,4224]{2,1,0:T(1,128)} %all_to_all.40), calls=%async_computation.6 | async-start | bytes 540672 | tf_op jit(solution)/shard_map/all_to_all | solution.py:49
  228.3 0.1 broadcast_and_fusion
  229.1 11.9 %all-to-all-done.6 = f32[16,1,4224]{2,1,0:T(1,128)S(1)} async-done(((f32[16,1,4224]{2,1,0:T(1,128)}), f32[16,1,4224]{2,1,0:T(1,128)S(1)}, u32[]{:S(2)}, u32[]{:S(2)}) %all-to-all-start.6) | async-done | bytes 270368 | tf_op jit(solution)/shard_map/all_to_all | solution.py:49
  241.0 0.2 reduce_sum.136
  241.2 1.3 slice_add_fusion
  242.5 0.6 broadcast_in_dim.33
  243.1 10.6 %all-to-all-start.7 = ((f32[16,1,2]{2,1,0:T(1,128)}), f32[16,1,2]{2,1,0:T(1,128)S(1)}, u32[]{:S(2)}, u32[]{:S(2)}) async-start(f32[16,1,2]{2,1,0:T(1,128)} %broadcast_in_dim.33), calls=%async_computation.7 | async-start | bytes 16384 | tf_op jit(solution)/shard_map/all_to_all | solution.py:31
  253.7 0.6 add_select_fusion
  254.3 6.4 %all-to-all-done.7 = f32[16,1,2]{2,1,0:T(1,128)S(1)} async-done(((f32[16,1,2]{2,1,0:T(1,128)}), f32[16,1,2]{2,1,0:T(1,128)S(1)}, u32[]{:S(2)}, u32[]{:S(2)}) %all-to-all-start.7) | async-done | bytes 160 | tf_op jit(solution)/shard_map/all_to_all | solution.py:31
  260.8 0.6 fusion.22
  262.5 0.6 pad_maximum_fusion.4
  (31 shorter events, 0.5 us)
Async XLA Ops:
  3.5 39.2 %copy-start.8 = (s32[16]{0:T(128)S(1)}, s32[16]{0:T(128)}, u32[]{:S(2)}) copy-start(s32[16]{0:T(128)} %param.19) | copy-start | bytes 196
  3.5 39.8 %copy-start.9 = (s32[16]{0:T(128)S(1)}, s32[16]{0:T(128)}, u32[]{:S(2)}) copy-start(s32[16]{0:T(128)} %param.20) | copy-start | bytes 196
  37.0 9.0 %copy-start = (bf16[8,2,256,256]{3,2,1,0:T(8,128)(2,1)}, bf16[8,2,256,256]{3,2,1,0:T(8,128)(2,1)S(1)}, u32[]{:S(2)}) copy-start(bf16[8,2,256,256]{3,2,1,0:T(8,128)(2,1)S(1)} %all_to_all.51) | copy-start | bytes 6291460
  37.0 9.0 %collective-permute-start = (bf16[8,2,256,256]{3,2,1,0:T(8,128)(2,1)S(1)}, bf16[8,2,256,256]{3,2,1,0:T(8,128)(2,1)}, u32[]{:S(2)}, u32[]{:S(2)}) collective-permute-start(bf16[8,2,256,256]{3,2,1,0:T(8,128)(2,1)S(1)} %all_to_all.51), channel_id=1, source_target_pairs={{0,32},{32,0},{1,33},{33,1},{2,34},{34,2},{3,35},{35,3},{4,36},{36... | collective-permute-start | bytes 6291464 | tf_op jit(solution)/shard_map/ppermute | solution.py:25
  51.2 1.3 copy-start.2
  51.2 1.3 copy-start.3
  51.2 1.3 copy-start.4
  54.3 89.8 %copy-start.7 = (bf16[2,256,256]{2,1,0:T(8,128)(2,1)S(1)}, bf16[2,256,256]{2,1,0:T(8,128)(2,1)}, u32[]{:S(2)}) copy-start(bf16[2,256,256]{2,1,0:T(8,128)(2,1)} %param.16) | copy-start | bytes 786436
  54.3 9.8 %collective-permute-start.1 = (f32[16,4224]{1,0:T(8,128)S(1)}, f32[16,4224]{1,0:T(8,128)S(1)}, u32[]{:S(2)}, u32[]{:S(2)}) collective-permute-start(f32[16,4224]{1,0:T(8,128)S(1)} %dynamic-slice_bitcast_fusion.1), channel_id=1, source_target_pairs={{0,1},{1,0},{2,3},{3,2},{4,5},{5,4},{6,7},{7,6},{8,9},{9,8},{10,11... | collective-permute-start | bytes 811016 | tf_op jit(solution)/shard_map/ppermute | solution.py:48
  112.7 31.3 %collective-permute-start.2 = (f32[16,2,8,256]{3,2,1,0:T(8,128)S(1)}, f32[16,2,8,256]{3,2,1,0:T(8,128)S(1)}, u32[]{:S(2)}, u32[]{:S(2)}) collective-permute-start(f32[16,2,8,256]{3,2,1,0:T(8,128)S(1)} %all_to_all.53), channel_id=1, source_target_pairs={{0,1},{1,0},{2,3},{3,2},{4,5},{5,4},{6,7},{7,6},{8,9},{9,8},{10,11... | collective-permute-start | bytes 786440 | tf_op jit(solution)/shard_map/ppermute | solution.py:58
  123.3 18.8 %all-to-all-start.3 = ((f32[16,1,2]{2,1,0:T(1,128)}), f32[16,1,2]{2,1,0:T(1,128)S(1)}, u32[]{:S(2)}, u32[]{:S(2)}) async-start(f32[16,1,2]{2,1,0:T(1,128)} %broadcast_in_dim.28), calls=%async_computation.3 | async-start | bytes 16384 | tf_op jit(solution)/shard_map/all_to_all | solution.py:31
  161.7 92.0 %copy-start.5 = (bf16[2,256,256]{2,1,0:T(8,128)(2,1)}, bf16[2,256,256]{2,1,0:T(8,128)(2,1)S(1)}, u32[]{:S(2)}) copy-start(bf16[2,256,256]{2,1,0:T(8,128)(2,1)S(1)} %fusion.11) | copy-start | bytes 786436
  191.9 8.8 %copy-start.1 = (bf16[8,2,256,256]{3,2,1,0:T(8,128)(2,1)}, bf16[8,2,256,256]{3,2,1,0:T(8,128)(2,1)S(1)}, u32[]{:S(2)}) copy-start(bf16[8,2,256,256]{3,2,1,0:T(8,128)(2,1)S(1)} %all_to_all.55) | copy-start | bytes 6291460
  191.9 7.5 %collective-permute-start.3 = (bf16[8,2,256,256]{3,2,1,0:T(8,128)(2,1)S(1)}, bf16[8,2,256,256]{3,2,1,0:T(8,128)(2,1)S(1)}, u32[]{:S(2)}, u32[]{:S(2)}) collective-permute-start(bf16[8,2,256,256]{3,2,1,0:T(8,128)(2,1)S(1)} %all_to_all.55), channel_id=1, source_target_pairs={{0,32},{32,0},{1,33},{33,1},{2,34},{34,2},{3,35},{35,3},{4,36},{36... | collective-permute-start | bytes 6291464 | tf_op jit(solution)/shard_map/ppermute | solution.py:25
  199.4 1.3 copy-start.6
  210.7 9.7 %collective-permute-start.4 = (f32[16,4224]{1,0:T(8,128)S(1)}, f32[16,4224]{1,0:T(8,128)S(1)}, u32[]{:S(2)}, u32[]{:S(2)}) collective-permute-start(f32[16,4224]{1,0:T(8,128)S(1)} %dynamic-slice_bitcast_fusion), channel_id=1, source_target_pairs={{0,1},{1,0},{2,3},{3,2},{4,5},{5,4},{6,7},{7,6},{8,9},{9,8},{10,11... | collective-permute-start | bytes 811016 | tf_op jit(solution)/shard_map/ppermute | solution.py:48
  221.3 19.8 %all-to-all-start.6 = ((f32[16,1,4224]{2,1,0:T(1,128)}), f32[16,1,4224]{2,1,0:T(1,128)S(1)}, u32[]{:S(2)}, u32[]{:S(2)}) async-start(f32[16,1,4224]{2,1,0:T(1,128)} %all_to_all.40), calls=%async_computation.6 | async-start | bytes 540672 | tf_op jit(solution)/shard_map/all_to_all | solution.py:49
  243.1 17.6 %all-to-all-start.7 = ((f32[16,1,2]{2,1,0:T(1,128)}), f32[16,1,2]{2,1,0:T(1,128)S(1)}, u32[]{:S(2)}, u32[]{:S(2)}) async-start(f32[16,1,2]{2,1,0:T(1,128)} %broadcast_in_dim.33), calls=%async_computation.7 | async-start | bytes 16384 | tf_op jit(solution)/shard_map/all_to_all | solution.py:31
